TPU v7x, 128 devices: a whole 4x4x4 slice. The times are simulated.
128 devices in a mesh: ep: 4 (over y), tp: 32 (over z, x, core).
Axes of the slice: x: 4, y: 4, z: 4, core: 2. Of those that a mesh axis runs over, the one named last changes fastest.
Arguments:
- tokens: bfloat16 [1024, 7168], P(('ep', 'tp')), may hold values from -6 to 6
- cotangent: bfloat16 [1024, 7168], P(('ep', 'tp')), may hold values from -6 to 6
- routing: int32 [1024, 2], P(('ep', 'tp')), may hold values from 0 to 7, all different within a row; in each aligned block of 8 rows (0 to 7, 8 to 15, ...) at most 3 rows name the same one
- route_gates: bfloat16 [1024, 2], P(('ep', 'tp')), may hold values from 0.5 to 2.5
- gate_weight: bfloat16 [8, 2048, 7168], P(None, 'tp', 'ep'), may hold values from -0.0625 to 0.0625
- up_weight: bfloat16 [8, 2048, 7168], P(None, 'tp', 'ep'), may hold values from -0.0625 to 0.0625
- down_weight: bfloat16 [8, 2048, 7168], P(None, 'tp', 'ep'), may hold values from -0.125 to 0.125
Outputs:
- token_grad: bfloat16 [1024, 7168], P(('ep', 'tp'))
- route_grad: float32 [1024, 2], P(('ep', 'tp'))
- gate_grad: bfloat16 [8, 2048, 7168], P(None, 'tp', 'ep')
- up_grad: bfloat16 [8, 2048, 7168], P(None, 'tp', 'ep')
- down_grad: bfloat16 [8, 2048, 7168], P(None, 'tp', 'ep')
Inputs may be any that keep to these rules, and one draw needn't show every extreme that they name: `routing`: in the rows of one device a row names 2 different experts, no expert is named more than 3 times, a bound that some block reaches.
All inputs are finite; a program needn't handle non-finite values.
Results may differ from a plain program's by a relative error of at most 0.017.
Values may be sent and summed in bfloat16 or wider, within the bound.
No kernel may reach another device: no remote copies, remote signals or barrier semaphores. Data moves between devices by JAX's collectives and lax.ppermute only.
A program may use at most 192 MiB of HBM per device.

v0:
```python
import jax
import jax.numpy as jnp
from jax import lax
from jax.experimental import pallas as pl
from jax.experimental.pallas import tpu as pltpu
from jax.sharding import Mesh
from jax.sharding import PartitionSpec as P

BF = jnp.bfloat16
F32 = jnp.float32
EXPERTS = 8
HID = 64
COLS = EXPERTS * HID
LANES = 128
SIDE = 4
PLANE = ("z", "x", "core")
TORUS = ("ep", "z", "x")


def params():
    return pltpu.CompilerParams(vmem_limit_bytes=58 << 20)


def first_half(rows):
    return lax.broadcasted_iota(jnp.int32, (rows, LANES), 1) < HID


def dot_t(rows, mat):
    return lax.dot_general(rows, mat, (((1,), (1,)), ((), ())), preferred_element_type=F32)


def flat(ref):
    lead, rows, width = ref.shape
    return ref[...].reshape(lead * rows, width)


def pre_acts(count, width):
    def body(*refs):
        xs, ys, mats = refs[:count], refs[count:2 * count], refs[2 * count:2 * count + 6]
        out_ref, acc_ref = refs[-2:]
        step = pl.program_id(0)
        chunk = mats[0].shape[0]
        x_all = jnp.concatenate([flat(r) for r in xs], axis=0)
        y = jnp.concatenate([flat(r) for r in ys], axis=0)
        rows = y.shape[0]
        x, meta = x_all[:, :width], x_all[:, width:].astype(F32)
        lane = lax.broadcasted_iota(jnp.int32, (rows, chunk), 1)
        owner = (lane // HID + step * (chunk // HID)).astype(F32)
        hit_a, hit_b = owner == meta[:, 0:1], owner == meta[:, 1:2]
        low = first_half(rows)
        lead, short_rows = xs[0].shape[0], xs[0].shape[1]
        for m in range(6):
            full = dot_t(y if m % 3 == 2 else x, mats[m][...])
            sums = []
            for k, hit in enumerate((hit_a, hit_b)):
                kept = jnp.where(hit, full, 0.0)
                short = sum(kept[:, g * LANES:(g + 1) * LANES] for g in range(chunk // LANES))
                spot = slice((2 * m + k) * LANES, (2 * m + k + 1) * LANES)
                short = short + jnp.where(step == 0, 0.0, acc_ref[:, spot])
                acc_ref[:, spot] = short
                sums.append(short + pltpu.roll(short, HID, 1))
            val = jnp.where(low, sums[0], sums[1]).astype(BF)
            for n in range(count):
                part = val[n * lead * short_rows:(n + 1) * lead * short_rows]
                part = part.reshape(lead, short_rows, LANES)
                out_ref[:, n * short_rows:(n + 1) * short_rows, m * LANES:(m + 1) * LANES] = part

    return body


def pre_call(xs, ys, mats, first, total, into):
    count = len(xs)
    lead, rows, _ = xs[0].shape
    width = ys[0].shape[2]
    steps = 2
    whole = lambda a: pl.BlockSpec(a.shape, lambda i: (0,) * a.ndim)
    extra = [] if into is None else [into]
    return pl.pallas_call(
        pre_acts(count, width),
        grid=(steps,),
        in_specs=[whole(a) for a in xs + ys]
        + [pl.BlockSpec((COLS // steps, width), lambda i: (i, 0))] * 6
        + [pl.BlockSpec(memory_space=pl.ANY)] * len(extra),
        out_specs=pl.BlockSpec((lead, rows * count, 6 * LANES), lambda i: (0, first // count, 0)),
        out_shape=jax.ShapeDtypeStruct((lead, rows * total, 6 * LANES), BF),
        scratch_shapes=[pltpu.VMEM((count * lead * rows, 12 * LANES), F32)],
        input_output_aliases={2 * count + 6: 0} if extra else {},
        compiler_params=params(),
    )(*xs, *ys, *mats, *extra)


def middle(plane_ref, parts_ref, meta_ref, out_ref, route_ref):
    rows = parts_ref.shape[1]
    meta = meta_ref[...].reshape(rows, LANES).astype(F32)
    low = first_half(rows)
    factor = jnp.where(low, meta[:, 2:3], meta[:, 3:4])
    prod = jnp.zeros((rows, LANES), F32)
    for side in range(2):
        vals = []
        for m in range(3):
            at = (3 * side + m) * LANES
            vals.append(sum(parts_ref[j, :, at:at + LANES].astype(F32) for j in range(SIDE)))
        gate, upper, reverse = vals
        sigma = jax.nn.sigmoid(gate)
        act = gate * sigma
        hidden = (act * upper).astype(BF).astype(F32)
        back = factor * reverse
        d_gate = back * upper * sigma * (1.0 + gate * (1.0 - sigma))
        at = 3 * side * LANES
        for n, val in enumerate((d_gate, back * act, factor * hidden)):
            low_bits = val.astype(BF)
            for j in range(SIDE):
                out_ref[j, :, at + n * LANES:at + (n + 1) * LANES] = low_bits
        prod = prod + hidden * reverse
    term_a = jnp.sum(jnp.where(low, prod, 0.0), axis=1, keepdims=True)
    term_b = jnp.sum(jnp.where(low, 0.0, prod), axis=1, keepdims=True)
    lane = lax.broadcasted_iota(jnp.int32, (rows, LANES), 1)
    route_ref[...] = jnp.where(lane == 0, term_a, jnp.where(lane == 1, term_b, 0.0)).astype(BF)


def middle_call(plane, parts, meta):
    _, rows, width = parts.shape
    return pl.pallas_call(
        middle,
        grid_spec=pltpu.PrefetchScalarGridSpec(
            num_scalar_prefetch=1,
            grid=(1,),
            in_specs=[
                pl.BlockSpec(parts.shape, lambda i, s: (0, 0, 0)),
                pl.BlockSpec((1, rows, LANES), lambda i, s: (s[0], 0, 0)),
            ],
            out_specs=[
                pl.BlockSpec((SIDE, rows, width), lambda i, s: (0, 0, 0)),
                pl.BlockSpec((rows, LANES), lambda i, s: (0, 0)),
            ],
        ),
        out_shape=[
            jax.ShapeDtypeStruct((SIDE, rows, width), BF),
            jax.ShapeDtypeStruct((rows, LANES), BF),
        ],
        compiler_params=params(),
    )(plane, parts, meta)


def spread(short, route_a, route_b, owner, low):
    turned = pltpu.roll(short, HID, 1)
    val_a = jnp.where(low, short, turned)
    val_b = jnp.where(low, turned, short)
    groups = COLS // LANES
    wide_a = jnp.concatenate([val_a] * groups, axis=1)
    wide_b = jnp.concatenate([val_b] * groups, axis=1)
    return jnp.where(owner == route_a, wide_a, jnp.where(owner == route_b, wide_b, 0.0))


def dense(acts_ref, meta_ref, picks):
    meta = flat(meta_ref).astype(F32)
    acts = flat(acts_ref).astype(F32)
    rows = meta.shape[0]
    lane = lax.broadcasted_iota(jnp.int32, (rows, COLS), 1)
    owner, low = (lane // HID).astype(F32), first_half(rows)
    return [
        spread(
            acts[:, m * LANES:(m + 1) * LANES], meta[:, 0:1], meta[:, 1:2], owner, low
        ).astype(BF)
        for m in picks
    ]


def widen(acts_ref, meta_ref, *outs):
    for out, val in zip(outs, dense(acts_ref, meta_ref, range(6))):
        out[...] = val


def widen_call(acts, meta):
    lead, rows, width = acts.shape
    view = lambda w: pl.BlockSpec((1, rows, w), lambda i: (i, 0, 0))
    return pl.pallas_call(
        widen,
        grid=(lead,),
        in_specs=[view(width), view(LANES)],
        out_specs=[pl.BlockSpec((rows, COLS), lambda i: (i, 0))] * 6,
        out_shape=[jax.ShapeDtypeStruct((lead * rows, COLS), BF)] * 6,
        compiler_params=params(),
    )(acts, meta)


def terms(spots_ref, acts_ref, meta_ref, route_ref, *refs):
    mats, out_ref, wide_ref = refs[:4], refs[4], refs[5]
    lead, rows, _ = acts_ref.shape
    step = pl.program_id(0)
    chunk = mats[0].shape[1]

    @pl.when(step == 0)
    def _():
        for n, val in enumerate(dense(acts_ref, meta_ref, (0, 1, 3, 4))):
            wide_ref[:, n * COLS:(n + 1) * COLS] = val
        route = route_ref[...].astype(F32)
        deep = out_ref.shape[2] - LANES
        for j in range(lead):
            mine = jnp.where(j == spots_ref[16], 1.0, 0.0)
            for b in range(16):
                spot = pl.multiple_of(spots_ref[b] * 8, 8)
                out_ref[j, pl.ds(spot, 8), deep:] = (route[b * 8:b * 8 + 8] * mine).astype(BF)

    wide = wide_ref[...]
    mat = jnp.concatenate([m[...] for m in mats], axis=0)
    total = jnp.dot(wide, mat, preferred_element_type=F32)
    where = pl.ds(pl.multiple_of(step * chunk, LANES), chunk)
    for j in range(lead):
        for b in range(16):
            at = j * rows + b * 8
            spot = pl.multiple_of(spots_ref[b] * 8, 8)
            out_ref[j, pl.ds(spot, 8), where] = total[at:at + 8].astype(BF)


def terms_call(spots, acts, meta, route, mats):
    lead, rows, _ = acts.shape
    deep = mats[0].shape[1]
    chunk = 256
    whole = lambda a: pl.BlockSpec(a.shape, lambda i, s: (0,) * a.ndim)
    out = jax.ShapeDtypeStruct((lead, rows, deep + LANES), BF)
    return pl.pallas_call(
        terms,
        grid_spec=pltpu.PrefetchScalarGridSpec(
            num_scalar_prefetch=1,
            grid=(deep // chunk,),
            in_specs=[whole(acts), whole(meta), whole(route)]
            + [pl.BlockSpec((COLS, chunk), lambda i, s: (0, i))] * 4,
            out_specs=whole(out),
            scratch_shapes=[pltpu.VMEM((lead * rows, 4 * COLS), BF)],
        ),
        out_shape=out,
        compiler_params=params(),
    )(spots, acts, meta, route, *mats)


def finish(parts_ref, token_ref, route_ref):
    deep = token_ref.shape[1]
    total = jnp.sum(parts_ref[...].astype(F32), axis=0)
    token_ref[...] = total[:, :deep].astype(BF)
    route = total[:, deep:]

    @pl.when(pl.program_id(0) == 0)
    def _():
        route_ref[...] = route

    @pl.when(pl.program_id(0) > 0)
    def _():
        route_ref[...] = route_ref[...] + route


def finish_call(parts, deep):
    _, rows, width = parts.shape
    return pl.pallas_call(
        finish,
        grid=(SIDE,),
        in_specs=[pl.BlockSpec((16, rows, width), lambda i: (i, 0, 0))],
        out_specs=[
            pl.BlockSpec((rows, deep), lambda i: (0, i)),
            pl.BlockSpec((rows, LANES), lambda i: (0, 0)),
        ],
        out_shape=[
            jax.ShapeDtypeStruct((rows, deep * SIDE), BF),
            jax.ShapeDtypeStruct((rows, LANES), F32),
        ],
        compiler_params=params(),
    )(parts)


def place(z, x, core):
    return (z % SIDE) * 8 + (x % SIDE) * 2 + core


def shift(arr, stage, by):
    pairs = []
    for z in range(SIDE):
        for x in range(SIDE):
            for core in range(2):
                along_x = core == stage
                goal = place(z, x + by, core) if along_x else place(z + by, x, core)
                pairs.append((place(z, x, core), goal))
    return lax.ppermute(arr, PLANE, pairs)


def swap(arr):
    return lax.ppermute(arr, "core", [(0, 1), (1, 0)])


def contract_rows(left, right):
    return lax.dot_general(left, right, (((0,), (0,)), ((), ())), preferred_element_type=F32)


def local(tokens, cotangent, routing, route_gates, gate_weight, up_weight, down_weight):
    tok_rows, _ = tokens.shape
    width = gate_weight.shape[2]
    own_mats = [w.reshape(COLS, width) for w in (gate_weight, up_weight, down_weight)]
    mats = own_mats + [swap(w) for w in own_mats]
    meta = jnp.concatenate([routing.astype(BF), route_gates], axis=1)
    meta = jnp.pad(meta, ((0, 0), (0, LANES - meta.shape[1])))
    cut = lambda a: jnp.swapaxes(a.reshape(tok_rows, SIDE, width), 0, 1)
    meta_all = jnp.broadcast_to(meta[None], (SIDE, tok_rows, LANES))
    send = jnp.concatenate([cut(tokens), meta_all, cut(cotangent)], axis=2)
    own = lax.all_to_all(send, "ep", 0, 0, tiled=True)
    near = [own] + [shift(own, 0, s) for s in range(1, SIDE)]
    lap = width + LANES
    x_0 = jnp.concatenate([p[:, :, :lap] for p in near], axis=1)
    y_0 = jnp.concatenate([p[:, :, lap:] for p in near], axis=1)
    x_1, x_3 = shift(x_0, 1, 1), shift(x_0, 1, 3)
    y_1, y_3 = shift(y_0, 1, 1), shift(y_0, 1, 3)
    x_2, y_2 = shift(x_1, 1, 1), shift(y_3, 1, 3)
    early = pre_call([x_0, x_1, x_3], [y_0, y_1, y_3], mats, 0, SIDE, None)
    pre = pre_call([x_2], [y_2], mats, SIDE - 1, SIDE, early)
    parts = lax.all_to_all(pre, "ep", 0, 0, tiled=True)
    stack = lambda ps: jnp.concatenate(ps, axis=1)
    meta_rows = stack([p[:, :, width:] for p in (x_0, x_1, x_3, x_2)])
    plane = lax.axis_index("ep").astype(jnp.int32)
    done, route = middle_call(plane.reshape(1), parts, meta_rows)
    acts = lax.all_to_all(done, "ep", 0, 0, tiled=True)
    z, x, core = (lax.axis_index(a).astype(jnp.int32) for a in PLANE)
    far = jnp.repeat(jnp.array([0, 1, 3, 2], jnp.int32), SIDE)
    close = jnp.tile(jnp.arange(SIDE, dtype=jnp.int32), SIDE)
    by_z = jnp.where(core == 0, far, close)
    by_x = jnp.where(core == 0, close, far)
    spots = ((z - by_z) % SIDE) * SIDE + (x - by_x) % SIDE
    spots = jnp.concatenate([spots, plane.reshape(1)])
    sent = terms_call(spots, acts, meta_rows, route, [mats[0], mats[1], mats[3], mats[4]])
    got = lax.all_to_all(sent.reshape(-1, tok_rows, lap), TORUS, 0, 0, tiled=True)
    wides = widen_call(acts, meta_rows)
    token_grad, route_sum = finish_call(got, width)
    route_grad = route_sum[:, :routing.shape[1]]
    x_rows = stack([p[:, :, :width] for p in (x_0, x_1, x_3, x_2)]).reshape(-1, width)
    y_rows = stack([y_0, y_1, y_3, y_2]).reshape(-1, width)
    grads = []
    for m in range(3):
        rows = y_rows if m == 2 else x_rows
        theirs = swap(contract_rows(wides[3 + m], rows).astype(BF))
        mine = contract_rows(wides[m], rows) + theirs.astype(F32)
        grads.append(mine.astype(BF).reshape(gate_weight.shape))
    return (token_grad, route_grad, *grads)


def solution(mesh):
    names = ("ep", "z", "x", "core")
    fine = Mesh(mesh.devices.reshape(SIDE, SIDE, SIDE, 2), names)
    rows = P(names, None)
    mats = P(None, PLANE, "ep")

    return jax.shard_map(
        local,
        mesh=fine,
        in_specs=(rows, rows, rows, rows, mats, mats, mats),
        out_specs=(rows, rows, mats, mats, mats),
        check_vma=False,
    )
```

profile of v0, /device:TPU:0, one launch (start us, length us, event | category | flops | bytes accessed | tf_op | source)
XLA Modules:
  0.0 175.9 jit_solution(13362647903959601236)
XLA Ops:
  0.6 0.7 convert_element_type.32
  1.3 0.7 pad_maximum_fusion.5
  2.0 0.1 copy.16
  2.1 1.7 pad_maximum_fusion.3
  3.8 4.6 %all-to-all-start = ((bf16[4,8,3712]{2,1,0:T(8,128)(2,1)}), bf16[4,8,3712]{2,1,0:T(8,128)(2,1)S(1)}, u32[]{:S(2)}, u32[]{:S(2)}) async-start(bf16[4,8,3712]{2,1,0:T(8,128)(2,1)} %pad_maximum_fusion.3), calls=%async_computation | async-start | bytes 475136 | tf_op jit(solution)/shard_map/all_to_all | solution.py:303
  8.3 0.5 collective-permute-start.8
  8.8 0.0 collective-permute-start.9
  8.8 6.0 %all-to-all-done = bf16[4,8,3712]{2,1,0:T(8,128)(2,1)S(1)} async-done(((bf16[4,8,3712]{2,1,0:T(8,128)(2,1)}), bf16[4,8,3712]{2,1,0:T(8,128)(2,1)S(1)}, u32[]{:S(2)}, u32[]{:S(2)}) %all-to-all-start) | async-done | bytes 237600 | tf_op jit(solution)/shard_map/all_to_all | solution.py:303
  14.9 2.8 %collective-permute-start.2 = (bf16[4,8,3712]{2,1,0:T(8,128)(2,1)S(1)}, bf16[4,8,3712]{2,1,0:T(8,128)(2,1)S(1)}, u32[]{:S(2)}, u32[]{:S(2)}) collective-permute-start(bf16[4,8,3712]{2,1,0:T(8,128)(2,1)S(1)} %all-to-all-done), channel_id=1, source_target_pairs={{0,6},{1,25},{2,0},{3,27},{4,2},{5,29},{6,4},{7,31},{8,14},{9,1},{... | collective-permute-start | bytes 712712 | tf_op jit(solution)/shard_map/ppermute | solution.py:282
  17.6 0.7 constant_dynamic-update-slice_fusion.6
  18.3 6.7 %collective-permute-done = bf16[4,8,3712]{2,1,0:T(8,128)(2,1)S(1)} collective-permute-done((bf16[4,8,3712]{2,1,0:T(8,128)(2,1)S(1)}, bf16[4,8,3712]{2,1,0:T(8,128)(2,1)S(1)}, u32[]{:S(2)}, u32[]{:S(2)}) %collective-permute-start) | collective-permute-done | bytes 237600 | tf_op jit(solution)/shard_map/ppermute | solution.py:282
  25.0 0.7 constant_dynamic-update-slice_fusion.5
  25.6 6.9 %collective-permute-done.1 = bf16[4,8,3712]{2,1,0:T(8,128)(2,1)S(1)} collective-permute-done((bf16[4,8,3712]{2,1,0:T(8,128)(2,1)S(1)}, bf16[4,8,3712]{2,1,0:T(8,128)(2,1)S(1)}, u32[]{:S(2)}, u32[]{:S(2)}) %collective-permute-start.1) | collective-permute-done | bytes 237600 | tf_op jit(solution)/shard_map/ppermute | solution.py:282
  32.6 0.7 constant_dynamic-update-slice_fusion.4
  33.2 0.0 collective-permute-done.2
  33.2 0.7 constant_dynamic-update-slice_fusion.3
  33.9 4.4 %collective-permute-start.5 = (bf16[4,32,1792]{2,1,0:T(8,128)(2,1)S(1)}, bf16[4,32,1792]{2,1,0:T(8,128)(2,1)S(1)}, u32[]{:S(2)}, u32[]{:S(2)}) collective-permute-start(bf16[4,32,1792]{2,1,0:T(8,128)(2,1)S(1)} %pad_maximum_fusion.2.refs_3_), channel_id=1, source_target_pairs={{0,24},{1,7},{2,26},{3,1},{4,28},{5,3},{6,30},{7,5},{8,0},{9,15},{... | collective-permute-start | bytes 1376264 | tf_op jit(solution)/shard_map/ppermute | solution.py:282
  38.5 5.9 %collective-permute-done.5.refs_5_ = bf16[4,32,1792]{2,1,0:T(8,128)(2,1)S(1)} collective-permute-done((bf16[4,32,1792]{2,1,0:T(8,128)(2,1)S(1)}, bf16[4,32,1792]{2,1,0:T(8,128)(2,1)S(1)}, u32[]{:S(2)}, u32[]{:S(2)}) %collective-permute-start.5) | collective-permute-done | bytes 458784 | tf_op jit(solution)/shard_map/ppermute | solution.py:282
  44.3 0.1 collective-permute-start.3
  44.4 3.6 %collective-permute-done.11.refs_4_ = bf16[4,32,1792]{2,1,0:T(8,128)(2,1)S(1)} collective-permute-done((bf16[4,32,1792]{2,1,0:T(8,128)(2,1)S(1)}, bf16[4,32,1792]{2,1,0:T(8,128)(2,1)S(1)}, u32[]{:S(2)}, u32[]{:S(2)}) %collective-permute-start.11) | collective-permute-done | bytes 458784 | tf_op jit(solution)/shard_map/ppermute | solution.py:282
  48.0 0.1 collective-permute-start.10
  48.1 6.7 %collective-permute-done.3.refs_1_ = bf16[4,32,1920]{2,1,0:T(8,128)(2,1)S(1)} collective-permute-done((bf16[4,32,1920]{2,1,0:T(8,128)(2,1)S(1)}, bf16[4,32,1920]{2,1,0:T(8,128)(2,1)S(1)}, u32[]{:S(2)}, u32[]{:S(2)}) %collective-permute-start.3) | collective-permute-done | bytes 491552 | tf_op jit(solution)/shard_map/ppermute | solution.py:282
  54.8 0.0 collective-permute-start.4
  54.9 2.0 %collective-permute-done.10.refs_2_ = bf16[4,32,1920]{2,1,0:T(8,128)(2,1)S(1)} collective-permute-done((bf16[4,32,1920]{2,1,0:T(8,128)(2,1)S(1)}, bf16[4,32,1920]{2,1,0:T(8,128)(2,1)S(1)}, u32[]{:S(2)}, u32[]{:S(2)}) %collective-permute-start.10) | collective-permute-done | bytes 491552 | tf_op jit(solution)/shard_map/ppermute | solution.py:282
  56.9 1.3 collective-permute-start.6
  58.2 0.0 collective-permute-done.7.refs_9_.refs_5_.refs_2_
  58.3 1.2 copy-done
  59.4 10.1 %shard_map.119.refs_8_ = bf16[4,128,768]{2,1,0:T(8,128)(2,1)} custom-call(bf16[4,32,1920]{2,1,0:T(8,128)(2,1)} %copy-done.3, bf16[4,32,1920]{2,1,0:T(8,128)(2,1)} %copy-done.6, bf16[4,32,1920]{2,1,0:T(8,128)(2,1)} %copy-done.8, bf16[4,32,1792]{2,1,0:T(8,128)(2,1)} %copy-done.18, bf16[4,32,1792]{2,1,0:T(8,128)(2,1)} %copy-done.14, ...), custom_call_target="tpu_custom_call" | custom-call | tf_op jit(solution)/shard_map/pallas_call | solution.py:78
  69.5 0.8 copy-done.16
  70.3 0.8 copy-done.9
  71.1 8.1 %shard_map.120 = bf16[4,128,768]{2,1,0:T(8,128)(2,1)} custom-call(bf16[4,32,1920]{2,1,0:T(8,128)(2,1)} %copy-done.9, bf16[4,32,1792]{2,1,0:T(8,128)(2,1)} %copy-done.16, bf16[512,1792]{1,0:T(8,128)(2,1)} %bitcast.31, bf16[512,1792]{1,0:T(8,128)(2,1)} %bitcast.35, bf16[512,1792]{1,0:T(8,128)(2,1)} %bitcast.40, ...), custom_call_target="tpu_custom_call", output_to_operand_aliasing={{}: (8, {})} | custom-call | tf_op jit(solution)/shard_map/pallas_call | solution.py:78
  79.2 3.6 %all-to-all-start.1 = ((bf16[4,128,768]{2,1,0:T(8,128)(2,1)}), bf16[4,128,768]{2,1,0:T(8,128)(2,1)S(1)}, u32[]{:S(2)}, u32[]{:S(2)}) async-start(bf16[4,128,768]{2,1,0:T(8,128)(2,1)} %shard_map.120), calls=%async_computation.1 | async-start | bytes 1572864 | tf_op jit(solution)/shard_map/all_to_all | solution.py:313
  82.9 0.1 select_subtract_fusion
  83.0 0.1 sub.20
  83.1 0.1 sub.23
  83.3 0.7 pad_maximum_fusion.4.meta_ref
  83.9 8.4 %all-to-all-done.1.parts_ref = bf16[4,128,768]{2,1,0:T(8,128)(2,1)S(1)} async-done(((bf16[4,128,768]{2,1,0:T(8,128)(2,1)}), bf16[4,128,768]{2,1,0:T(8,128)(2,1)S(1)}, u32[]{:S(2)}, u32[]{:S(2)}) %all-to-all-start.1) | async-done | bytes 786464 | tf_op jit(solution)/shard_map/all_to_all | solution.py:313
  92.3 0.9 copy-done.5
  93.2 2.3 %shard_map.121 = (bf16[4,128,768]{2,1,0:T(8,128)(2,1)}, bf16[128,128]{1,0:T(8,128)(2,1)}) custom-call(s32[1]{0:T(128)} %bitcast.plane_ref, bf16[4,128,768]{2,1,0:T(8,128)(2,1)} %copy-done.5, bf16[4,128,128]{2,1,0:T(8,128)(2,1)} %pad_maximum_fusion.4.meta_ref), custom_call_target="tpu_custom_call" | custom-call | tf_op jit(solution)/shard_map/pallas_call | solution.py:123
  95.5 3.5 %all-to-all-start.2 = ((bf16[4,128,768]{2,1,0:T(8,128)(2,1)}), bf16[4,128,768]{2,1,0:T(8,128)(2,1)S(1)}, u32[]{:S(2)}, u32[]{:S(2)}) async-start(bf16[4,128,768]{2,1,0:T(8,128)(2,1)} %get-tuple-element.15), calls=%async_computation.2 | async-start | bytes 1572864 | tf_op jit(solution)/shard_map/all_to_all | solution.py:318
  99.0 0.8 constant_dynamic-update-slice_fusion.2
  99.8 0.8 constant_dynamic-update-slice_fusion.1
  100.7 0.3 slice-done.1
  101.0 0.1 slice-done.3
  101.1 1.4 pad_maximum_fusion
  102.6 5.9 %all-to-all-done.2.acts_ref = bf16[4,128,768]{2,1,0:T(8,128)(2,1)S(1)} async-done(((bf16[4,128,768]{2,1,0:T(8,128)(2,1)}), bf16[4,128,768]{2,1,0:T(8,128)(2,1)S(1)}, u32[]{:S(2)}, u32[]{:S(2)}) %all-to-all-start.2) | async-done | bytes 786464 | tf_op jit(solution)/shard_map/all_to_all | solution.py:318
  108.5 0.9 copy-done.2
  109.4 4.1 %shard_map.124 = (bf16[512,512]{1,0:T(8,128)(2,1)}, bf16[512,512]{1,0:T(8,128)(2,1)}, bf16[512,512]{1,0:T(8,128)(2,1)}, bf16[512,512]{1,0:T(8,128)(2,1)}, bf16[5...) custom-call(bf16[4,128,768]{2,1,0:T(8,128)(2,1)} %copy-done.2, bf16[4,128,128]{2,1,0:T(8,128)(2,1)} %pad_maximum_fusion.4.meta_ref), custom_call_target="tpu_custom_call" | custom-call | tf_op jit(solution)/shard_map/pallas_call | solution.py:177
  113.5 4.2 %convolution_convert_fusion.2 = bf16[512,1792]{1,0:T(8,128)(2,1)} fusion(bf16[512,512]{1,0:T(8,128)(2,1)} %get-tuple-element.20, bf16[512,1792]{1,0:T(8,128)(2,1)} %bitcast.41), kind=kOutput, calls=%fused_computation.5 | convolution fusion | flops 940441600 | bytes 4194304 | tf_op jit(solution)/shard_map/dot_general | solution.py:290
  117.7 0.0 copy-start.19
  117.7 2.4 %convolution_convert_fusion.1 = bf16[512,1792]{1,0:T(8,128)(2,1)} fusion(bf16[512,512]{1,0:T(8,128)(2,1)S(1)} %copy-done.27, bf16[512,1792]{1,0:T(8,128)(2,1)S(1)} %bitcast.43), kind=kOutput, calls=%fused_computation.4 | convolution fusion | flops 940441600 | bytes 4194304 | tf_op jit(solution)/shard_map/dot_general | solution.py:290
  120.1 0.5 collective-permute-start.13
  120.6 2.4 %convolution_convert_fusion = bf16[512,1792]{1,0:T(8,128)(2,1)} fusion(bf16[512,512]{1,0:T(8,128)(2,1)S(1)} %copy-done.26, bf16[512,1792]{1,0:T(8,128)(2,1)S(1)} %bitcast.47), kind=kOutput, calls=%fused_computation.3 | convolution fusion | flops 940441600 | bytes 4194304 | tf_op jit(solution)/shard_map/dot_general | solution.py:290
  123.0 0.0 collective-permute-start.14
  123.1 0.6 pad_add_fusion.spots_ref
  123.7 11.1 %shard_map.122 = bf16[4,128,1920]{2,1,0:T(8,128)(2,1)} custom-call(s32[17]{0:T(128)} %pad_add_fusion.spots_ref, bf16[4,128,768]{2,1,0:T(8,128)(2,1)} %copy-done.2, bf16[4,128,128]{2,1,0:T(8,128)(2,1)} %pad_maximum_fusion.4.meta_ref, bf16[128,128]{1,0:T(8,128)(2,1)} %get-tuple-element.16.route_ref, bf16[512,1792]{1,0:T(8,128)(2,1)} %bitcast.32, ...), custom_call_target="tpu_custom_call" | custom-call | tf_op jit(solution)/shard_map/pallas_call | solution.py:222
  134.8 4.8 %all-to-all-start.3 = ((bf16[64,8,1920]{2,1,0:T(8,128)(2,1)}), bf16[64,8,1920]{2,1,0:T(8,128)(2,1)S(1)}, u32[]{:S(2)}, u32[]{:S(2)}) async-start(bf16[64,8,1920]{2,1,0:T(8,128)(2,1)} %bitcast.37), calls=%async_computation.3 | async-start | bytes 3932160 | tf_op jit(solution)/shard_map/all_to_all | solution.py:327
  139.7 4.6 %add_convert_fusion.2 = bf16[512,1792]{1,0:T(8,128)(2,1)} fusion(bf16[512,1792]{1,0:T(8,128)(2,1)} %collective-permute-done.12, bf16[512,512]{1,0:T(8,128)(2,1)S(1)} %copy-done.25, bf16[512,1792]{1,0:T(8,128)(2,1)} %bitcast.42), kind=kOutput, calls=%fused_computation.2 | convolution fusion | flops 942276608 | bytes 6029312 | tf_op jit(solution)/shard_map/dot_general | solution.py:290
  144.3 4.0 %add_convert_fusion.1 = bf16[512,1792]{1,0:T(8,128)(2,1)} fusion(bf16[512,1792]{1,0:T(8,128)(2,1)} %collective-permute-done.13, bf16[512,512]{1,0:T(8,128)(2,1)S(1)} %copy-done.24, bf16[512,1792]{1,0:T(8,128)(2,1)S(1)} %bitcast.44), kind=kOutput, calls=%fused_computation.1 | convolution fusion | flops 942276608 | bytes 6029312 | tf_op jit(solution)/shard_map/dot_general | solution.py:290
  148.3 3.9 %add_convert_fusion = bf16[512,1792]{1,0:T(8,128)(2,1)} fusion(bf16[512,1792]{1,0:T(8,128)(2,1)} %collective-permute-done.14, bf16[512,512]{1,0:T(8,128)(2,1)S(1)} %copy-done.23, bf16[512,1792]{1,0:T(8,128)(2,1)S(1)} %bitcast.48), kind=kOutput, calls=%fused_computation | convolution fusion | flops 942276608 | bytes 6029312 | tf_op jit(solution)/shard_map/dot_general | solution.py:290
  152.2 17.6 %all-to-all-done.3.parts_ref = bf16[64,8,1920]{2,1,0:T(8,128)(2,1)S(1)} async-done(((bf16[64,8,1920]{2,1,0:T(8,128)(2,1)}), bf16[64,8,1920]{2,1,0:T(8,128)(2,1)S(1)}, u32[]{:S(2)}, u32[]{:S(2)}) %all-to-all-start.3) | async-done | bytes 1966112 | tf_op jit(solution)/shard_map/all_to_all | solution.py:327
  169.8 1.3 copy-done.1
  171.1 3.5 %shard_map.123 = (bf16[8,7168]{1,0:T(8,128)(2,1)}, f32[8,128]{1,0:T(8,128)}) custom-call(bf16[64,8,1920]{2,1,0:T(8,128)(2,1)} %copy-done.1), custom_call_target="tpu_custom_call" | custom-call | tf_op jit(solution)/shard_map/pallas_call | solution.py:254
  174.6 1.3 copy.15
  (81 shorter events, 0.4 us)
Async XLA Ops:
  3.8 11.1 %all-to-all-start = ((bf16[4,8,3712]{2,1,0:T(8,128)(2,1)}), bf16[4,8,3712]{2,1,0:T(8,128)(2,1)S(1)}, u32[]{:S(2)}, u32[]{:S(2)}) async-start(bf16[4,8,3712]{2,1,0:T(8,128)(2,1)} %pad_maximum_fusion.3), calls=%async_computation | async-start | bytes 475136 | tf_op jit(solution)/shard_map/all_to_all | solution.py:303
  8.3 49.8 %collective-permute-start.7 = (bf16[512,1792]{1,0:T(8,128)(2,1)}, bf16[512,1792]{1,0:T(8,128)(2,1)S(1)}, u32[]{:S(2)}, u32[]{:S(2)}) collective-permute-start(bf16[512,1792]{1,0:T(8,128)(2,1)} %bitcast.29), channel_id=1, source_target_pairs={{0,1},{1,0},{2,3},{3,2},{4,5},{5,4},{6,7},{7,6},{8,9},{9,8},{10,11... | collective-permute-start | bytes 5505032 | tf_op jit(solution)/shard_map/ppermute | solution.py:286
  8.3 49.8 %collective-permute-start.8 = (bf16[512,1792]{1,0:T(8,128)(2,1)}, bf16[512,1792]{1,0:T(8,128)(2,1)}, u32[]{:S(2)}, u32[]{:S(2)}) collective-permute-start(bf16[512,1792]{1,0:T(8,128)(2,1)} %bitcast.33), channel_id=1, source_target_pairs={{0,1},{1,0},{2,3},{3,2},{4,5},{5,4},{6,7},{7,6},{8,9},{9,8},{10,11... | collective-permute-start | bytes 5505032 | tf_op jit(solution)/shard_map/ppermute | solution.py:286
  8.8 49.3 %collective-permute-start.9 = (bf16[512,1792]{1,0:T(8,128)(2,1)}, bf16[512,1792]{1,0:T(8,128)(2,1)}, u32[]{:S(2)}, u32[]{:S(2)}) collective-permute-start(bf16[512,1792]{1,0:T(8,128)(2,1)} %bitcast.38), channel_id=1, source_target_pairs={{0,1},{1,0},{2,3},{3,2},{4,5},{5,4},{6,7},{7,6},{8,9},{9,8},{10,11... | collective-permute-start | bytes 5505032 | tf_op jit(solution)/shard_map/ppermute | solution.py:286
  14.9 18.4 %collective-permute-start.2 = (bf16[4,8,3712]{2,1,0:T(8,128)(2,1)S(1)}, bf16[4,8,3712]{2,1,0:T(8,128)(2,1)S(1)}, u32[]{:S(2)}, u32[]{:S(2)}) collective-permute-start(bf16[4,8,3712]{2,1,0:T(8,128)(2,1)S(1)} %all-to-all-done), channel_id=1, source_target_pairs={{0,6},{1,25},{2,0},{3,27},{4,2},{5,29},{6,4},{7,31},{8,14},{9,1},{... | collective-permute-start | bytes 712712 | tf_op jit(solution)/shard_map/ppermute | solution.py:282
  17.6 7.3 %collective-permute-start = (bf16[4,8,3712]{2,1,0:T(8,128)(2,1)S(1)}, bf16[4,8,3712]{2,1,0:T(8,128)(2,1)S(1)}, u32[]{:S(2)}, u32[]{:S(2)}) collective-permute-start(bf16[4,8,3712]{2,1,0:T(8,128)(2,1)S(1)} %all-to-all-done), channel_id=1, source_target_pairs={{0,2},{1,9},{2,4},{3,11},{4,6},{5,13},{6,0},{7,15},{8,10},{9,17},{... | collective-permute-start | bytes 712712 | tf_op jit(solution)/shard_map/ppermute | solution.py:282
  25.0 7.6 %collective-permute-start.1 = (bf16[4,8,3712]{2,1,0:T(8,128)(2,1)S(1)}, bf16[4,8,3712]{2,1,0:T(8,128)(2,1)S(1)}, u32[]{:S(2)}, u32[]{:S(2)}) collective-permute-start(bf16[4,8,3712]{2,1,0:T(8,128)(2,1)S(1)} %all-to-all-done), channel_id=1, source_target_pairs={{0,4},{1,17},{2,6},{3,19},{4,0},{5,21},{6,2},{7,23},{8,12},{9,25},... | collective-permute-start | bytes 712712 | tf_op jit(solution)/shard_map/ppermute | solution.py:282
  33.9 24.3 %copy-start.18 = (bf16[4,32,1792]{2,1,0:T(8,128)(2,1)}, bf16[4,32,1792]{2,1,0:T(8,128)(2,1)S(1)}, u32[]{:S(2)}) copy-start(bf16[4,32,1792]{2,1,0:T(8,128)(2,1)S(1)} %pad_maximum_fusion.2.refs_3_) | copy-start | bytes 1376260
  33.9 10.4 %collective-permute-start.5 = (bf16[4,32,1792]{2,1,0:T(8,128)(2,1)S(1)}, bf16[4,32,1792]{2,1,0:T(8,128)(2,1)S(1)}, u32[]{:S(2)}, u32[]{:S(2)}) collective-permute-start(bf16[4,32,1792]{2,1,0:T(8,128)(2,1)S(1)} %pad_maximum_fusion.2.refs_3_), channel_id=1, source_target_pairs={{0,24},{1,7},{2,26},{3,1},{4,28},{5,3},{6,30},{7,5},{8,0},{9,15},{... | collective-permute-start | bytes 1376264 | tf_op jit(solution)/shard_map/ppermute | solution.py:282
  38.3 9.7 %collective-permute-start.11 = (bf16[4,32,1792]{2,1,0:T(8,128)(2,1)S(1)}, bf16[4,32,1792]{2,1,0:T(8,128)(2,1)S(1)}, u32[]{:S(2)}, u32[]{:S(2)}) collective-permute-start(bf16[4,32,1792]{2,1,0:T(8,128)(2,1)S(1)} %pad_maximum_fusion.2.refs_3_), channel_id=1, source_target_pairs={{0,8},{1,3},{2,10},{3,5},{4,12},{5,7},{6,14},{7,1},{8,16},{9,11},{... | collective-permute-start | bytes 1376264 | tf_op jit(solution)/shard_map/ppermute | solution.py:282
  38.5 19.7 %copy-start.3 = (bf16[4,32,1920]{2,1,0:T(8,128)(2,1)}, bf16[4,32,1920]{2,1,0:T(8,128)(2,1)S(1)}, u32[]{:S(2)}) copy-start(bf16[4,32,1920]{2,1,0:T(8,128)(2,1)S(1)} %pad_maximum_fusion.1.refs_0_) | copy-start | bytes 1474564
  44.3 13.9 %copy-start.12 = (bf16[4,32,1792]{2,1,0:T(8,128)(2,1)}, bf16[4,32,1792]{2,1,0:T(8,128)(2,1)S(1)}, u32[]{:S(2)}) copy-start(bf16[4,32,1792]{2,1,0:T(8,128)(2,1)S(1)} %collective-permute-done.5.refs_5_) | copy-start | bytes 1376260
  44.3 10.5 %collective-permute-start.3 = (bf16[4,32,1920]{2,1,0:T(8,128)(2,1)S(1)}, bf16[4,32,1920]{2,1,0:T(8,128)(2,1)S(1)}, u32[]{:S(2)}, u32[]{:S(2)}) collective-permute-start(bf16[4,32,1920]{2,1,0:T(8,128)(2,1)S(1)} %pad_maximum_fusion.1.refs_0_), channel_id=1, source_target_pairs={{0,8},{1,3},{2,10},{3,5},{4,12},{5,7},{6,14},{7,1},{8,16},{9,11},{... | collective-permute-start | bytes 1474568 | tf_op jit(solution)/shard_map/ppermute | solution.py:282
  48.0 10.2 %copy-start.14 = (bf16[4,32,1792]{2,1,0:T(8,128)(2,1)}, bf16[4,32,1792]{2,1,0:T(8,128)(2,1)S(1)}, u32[]{:S(2)}) copy-start(bf16[4,32,1792]{2,1,0:T(8,128)(2,1)S(1)} %collective-permute-done.11.refs_4_) | copy-start | bytes 1376260
  48.0 8.8 %collective-permute-start.10 = (bf16[4,32,1920]{2,1,0:T(8,128)(2,1)S(1)}, bf16[4,32,1920]{2,1,0:T(8,128)(2,1)S(1)}, u32[]{:S(2)}, u32[]{:S(2)}) collective-permute-start(bf16[4,32,1920]{2,1,0:T(8,128)(2,1)S(1)} %pad_maximum_fusion.1.refs_0_), channel_id=1, source_target_pairs={{0,24},{1,7},{2,26},{3,1},{4,28},{5,3},{6,30},{7,5},{8,0},{9,15},{... | collective-permute-start | bytes 1474568 | tf_op jit(solution)/shard_map/ppermute | solution.py:282
  54.8 3.4 %copy-start.6 = (bf16[4,32,1920]{2,1,0:T(8,128)(2,1)}, bf16[4,32,1920]{2,1,0:T(8,128)(2,1)S(1)}, u32[]{:S(2)}) copy-start(bf16[4,32,1920]{2,1,0:T(8,128)(2,1)S(1)} %collective-permute-done.3.refs_1_) | copy-start | bytes 1474564
  54.8 14.7 %collective-permute-start.4 = (bf16[4,32,1920]{2,1,0:T(8,128)(2,1)S(1)}, bf16[4,32,1920]{2,1,0:T(8,128)(2,1)S(1)}, u32[]{:S(2)}, u32[]{:S(2)}) collective-permute-start(bf16[4,32,1920]{2,1,0:T(8,128)(2,1)S(1)} %collective-permute-done.3.refs_1_), channel_id=1, source_target_pairs={{0,8},{1,3},{2,10},{3,5},{4,12},{5,7},{6,14},{7,1},{8,16},{9,11},{... | collective-permute-start | bytes 1474568 | tf_op jit(solution)/shard_map/ppermute | solution.py:282
  56.9 1.4 copy-start.8
  56.9 12.6 %collective-permute-start.6 = (bf16[4,32,1792]{2,1,0:T(8,128)(2,1)S(1)}, bf16[4,32,1792]{2,1,0:T(8,128)(2,1)S(1)}, u32[]{:S(2)}, u32[]{:S(2)}) collective-permute-start(bf16[4,32,1792]{2,1,0:T(8,128)(2,1)S(1)} %collective-permute-done.5.refs_5_), channel_id=1, source_target_pairs={{0,24},{1,7},{2,26},{3,1},{4,28},{5,3},{6,30},{7,5},{8,0},{9,15},{... | collective-permute-start | bytes 1376264 | tf_op jit(solution)/shard_map/ppermute | solution.py:282
  58.2 1.2 copy-start
  69.5 13.4 %copy-start.22 = (s32[4]{0:T(128)S(1)}, s32[4]{0:T(128)}, u32[]{:S(2)}) copy-start(s32[4]{0:T(128)} %constant.41.clone) | copy-start | bytes 52
  69.5 13.7 %copy-start.4 = (bf16[4,32,1920]{2,1,0:T(8,128)(2,1)S(1)}, bf16[4,32,1920]{2,1,0:T(8,128)(2,1)}, u32[]{:S(2)}) copy-start(bf16[4,32,1920]{2,1,0:T(8,128)(2,1)} %copy-done.3) | copy-start | bytes 1474564
  69.5 0.8 copy-start.16
  70.3 0.8 copy-start.9
  79.2 4.0 %copy-start.7 = (bf16[4,32,1920]{2,1,0:T(8,128)(2,1)S(1)}, bf16[4,32,1920]{2,1,0:T(8,128)(2,1)}, u32[]{:S(2)}) copy-start(bf16[4,32,1920]{2,1,0:T(8,128)(2,1)} %copy-done.6) | copy-start | bytes 1474564
  79.2 4.0 %slice-start = ((bf16[4,32,1920]{2,1,0:T(8,128)(2,1)}), bf16[4,32,128]{2,1,0:T(8,128)(2,1)S(1)}, s32[]{:S(2)}) async-start(bf16[4,32,1920]{2,1,0:T(8,128)(2,1)} %copy-done.8), calls=%async_computation.4 | async-start | bytes 65536 | tf_op jit(solution)/shard_map/slice | solution.py:315
  79.2 4.0 %slice-start.2 = ((bf16[4,32,1920]{2,1,0:T(8,128)(2,1)}), bf16[4,32,128]{2,1,0:T(8,128)(2,1)S(1)}, s32[]{:S(2)}) async-start(bf16[4,32,1920]{2,1,0:T(8,128)(2,1)} %copy-done.9), calls=%async_computation.6 | async-start | bytes 65536 | tf_op jit(solution)/shard_map/slice | solution.py:315
  79.2 13.1 %all-to-all-start.1 = ((bf16[4,128,768]{2,1,0:T(8,128)(2,1)}), bf16[4,128,768]{2,1,0:T(8,128)(2,1)S(1)}, u32[]{:S(2)}, u32[]{:S(2)}) async-start(bf16[4,128,768]{2,1,0:T(8,128)(2,1)} %shard_map.120), calls=%async_computation.1 | async-start | bytes 1572864 | tf_op jit(solution)/shard_map/all_to_all | solution.py:313
  83.2 15.8 %copy-start.15 = (bf16[4,32,1792]{2,1,0:T(8,128)(2,1)S(1)}, bf16[4,32,1792]{2,1,0:T(8,128)(2,1)}, u32[]{:S(2)}) copy-start(bf16[4,32,1792]{2,1,0:T(8,128)(2,1)} %copy-done.14) | copy-start | bytes 1376260
  83.3 16.6 %copy-start.13 = (bf16[4,32,1792]{2,1,0:T(8,128)(2,1)S(1)}, bf16[4,32,1792]{2,1,0:T(8,128)(2,1)}, u32[]{:S(2)}) copy-start(bf16[4,32,1792]{2,1,0:T(8,128)(2,1)} %copy-done.12) | copy-start | bytes 1376260
  92.3 0.9 copy-start.5
  95.5 13.0 %all-to-all-start.2 = ((bf16[4,128,768]{2,1,0:T(8,128)(2,1)}), bf16[4,128,768]{2,1,0:T(8,128)(2,1)S(1)}, u32[]{:S(2)}, u32[]{:S(2)}) async-start(bf16[4,128,768]{2,1,0:T(8,128)(2,1)} %get-tuple-element.15), calls=%async_computation.2 | async-start | bytes 1572864 | tf_op jit(solution)/shard_map/all_to_all | solution.py:318
  99.8 1.2 slice-start.1
  99.8 1.3 slice-start.3
  108.5 0.9 copy-start.2
  113.5 4.2 %copy-start.10 = (bf16[4,128,1792]{2,1,0:T(8,128)(2,1)S(1)}, bf16[4,128,1792]{2,1,0:T(8,128)(2,1)}, u32[]{:S(2)}) copy-start(bf16[4,128,1792]{2,1,0:T(8,128)(2,1)} %pad_maximum_fusion) | copy-start | bytes 5505028
  113.5 4.2 %copy-start.27 = (bf16[512,512]{1,0:T(8,128)(2,1)S(1)}, bf16[512,512]{1,0:T(8,128)(2,1)}, u32[]{:S(2)}) copy-start(bf16[512,512]{1,0:T(8,128)(2,1)} %get-tuple-element.22) | copy-start | bytes 1572868
  117.7 21.9 %collective-permute-start.12 = (bf16[512,1792]{1,0:T(8,128)(2,1)}, bf16[512,1792]{1,0:T(8,128)(2,1)}, u32[]{:S(2)}, u32[]{:S(2)}) collective-permute-start(bf16[512,1792]{1,0:T(8,128)(2,1)} %convolution_convert_fusion.2), channel_id=1, source_target_pairs={{0,1},{1,0},{2,3},{3,2},{4,5},{5,4},{6,7},{7,6},{8,9},{9,8},{10,11... | collective-permute-start | bytes 5505032 | tf_op jit(solution)/shard_map/ppermute | solution.py:286
  117.7 2.9 %copy-start.17 = (bf16[4,32,1792]{2,1,0:T(8,128)(2,1)S(1)}, bf16[4,32,1792]{2,1,0:T(8,128)(2,1)}, u32[]{:S(2)}) copy-start(bf16[4,32,1792]{2,1,0:T(8,128)(2,1)} %copy-done.16) | copy-start | bytes 1376260
  117.7 2.9 %copy-start.19 = (bf16[4,128,1792]{2,1,0:T(8,128)(2,1)S(1)}, bf16[4,128,1792]{2,1,0:T(8,128)(2,1)}, u32[]{:S(2)}) copy-start(bf16[4,128,1792]{2,1,0:T(8,128)(2,1)} %constant_dynamic-update-slice_fusion.1) | copy-start | bytes 5505028
  117.7 2.9 %copy-start.26 = (bf16[512,512]{1,0:T(8,128)(2,1)S(1)}, bf16[512,512]{1,0:T(8,128)(2,1)}, u32[]{:S(2)}) copy-start(bf16[512,512]{1,0:T(8,128)(2,1)} %get-tuple-element.24) | copy-start | bytes 1572868
  120.1 24.2 %collective-permute-start.13 = (bf16[512,1792]{1,0:T(8,128)(2,1)}, bf16[512,1792]{1,0:T(8,128)(2,1)}, u32[]{:S(2)}, u32[]{:S(2)}) collective-permute-start(bf16[512,1792]{1,0:T(8,128)(2,1)} %convolution_convert_fusion.1), channel_id=1, source_target_pairs={{0,1},{1,0},{2,3},{3,2},{4,5},{5,4},{6,7},{7,6},{8,9},{9,8},{10,11... | collective-permute-start | bytes 5505032 | tf_op jit(solution)/shard_map/ppermute | solution.py:286
  120.6 2.4 %copy-start.20 = (bf16[4,128,1792]{2,1,0:T(8,128)(2,1)}, bf16[4,128,1792]{2,1,0:T(8,128)(2,1)S(1)}, u32[]{:S(2)}) copy-start(bf16[4,128,1792]{2,1,0:T(8,128)(2,1)S(1)} %constant_dynamic-update-slice_fusion) | copy-start | bytes 5505028
  123.0 25.3 %collective-permute-start.14 = (bf16[512,1792]{1,0:T(8,128)(2,1)}, bf16[512,1792]{1,0:T(8,128)(2,1)}, u32[]{:S(2)}, u32[]{:S(2)}) collective-permute-start(bf16[512,1792]{1,0:T(8,128)(2,1)} %convolution_convert_fusion), channel_id=1, source_target_pairs={{0,1},{1,0},{2,3},{3,2},{4,5},{5,4},{6,7},{7,6},{8,9},{9,8},{10,11... | collective-permute-start | bytes 5505032 | tf_op jit(solution)/shard_map/ppermute | solution.py:286
  134.8 4.8 %copy-start.25 = (bf16[512,512]{1,0:T(8,128)(2,1)S(1)}, bf16[512,512]{1,0:T(8,128)(2,1)}, u32[]{:S(2)}) copy-start(bf16[512,512]{1,0:T(8,128)(2,1)} %get-tuple-element.19) | copy-start | bytes 1572868
  134.8 35.0 %all-to-all-start.3 = ((bf16[64,8,1920]{2,1,0:T(8,128)(2,1)}), bf16[64,8,1920]{2,1,0:T(8,128)(2,1)S(1)}, u32[]{:S(2)}, u32[]{:S(2)}) async-start(bf16[64,8,1920]{2,1,0:T(8,128)(2,1)} %bitcast.37), calls=%async_computation.3 | async-start | bytes 3932160 | tf_op jit(solution)/shard_map/all_to_all | solution.py:327
  139.6 4.6 %copy-start.11 = (bf16[4,128,1792]{2,1,0:T(8,128)(2,1)S(1)}, bf16[4,128,1792]{2,1,0:T(8,128)(2,1)}, u32[]{:S(2)}) copy-start(bf16[4,128,1792]{2,1,0:T(8,128)(2,1)} %pad_maximum_fusion) | copy-start | bytes 5505028
  139.7 4.6 %copy-start.24 = (bf16[512,512]{1,0:T(8,128)(2,1)S(1)}, bf16[512,512]{1,0:T(8,128)(2,1)}, u32[]{:S(2)}) copy-start(bf16[512,512]{1,0:T(8,128)(2,1)} %get-tuple-element.21) | copy-start | bytes 1572868
  144.3 4.1 %copy-start.21 = (bf16[4,128,1792]{2,1,0:T(8,128)(2,1)S(1)}, bf16[4,128,1792]{2,1,0:T(8,128)(2,1)}, u32[]{:S(2)}) copy-start(bf16[4,128,1792]{2,1,0:T(8,128)(2,1)} %copy-done.20) | copy-start | bytes 5505028
  144.3 4.1 %copy-start.23 = (bf16[512,512]{1,0:T(8,128)(2,1)S(1)}, bf16[512,512]{1,0:T(8,128)(2,1)}, u32[]{:S(2)}) copy-start(bf16[512,512]{1,0:T(8,128)(2,1)} %get-tuple-element.23) | copy-start | bytes 1572868
  169.8 1.3 copy-start.1
where the time goes:
time: 177 us; the launch traced here: 176 us
  waiting for transfers between devices  69.8 us (39%)
  Pallas kernels  39.2 us (22%)
  starting transfers between devices  26.2 us (15%)
  matrix products  21.4 us (12%)
  local copies, waits for them, and re-layouts  12.4 us (7%)
  other arithmetic  5.84 us (3%)
    ppermute x9, waiting for transfers between devices, shift(): return lax.ppermute(arr, PLANE, pairs)  31.8 us
    dot_general x6, matrix products, contract_rows(): lax.dot_general(left, right, (((0,), (0,)), ((), ())), preferred_element_...  21.4 us
    pallas_call x2, Pallas kernels, pre_call(): pl.pallas_call(pre_acts(count, width), grid=(steps,), in_specs=[whole(a)...  18.2 us
    all_to_all x1, waiting for transfers between devices, local(): lax.all_to_all(sent.reshape(-1, tok_rows, lap), TORUS, 0, 0, tiled=True)  17.6 us
    unnamed x64, local copies, waits for them, and re-layouts  11.6 us
    pallas_call x1, Pallas kernels, terms_call(): pl.pallas_call(terms, grid_spec=pltpu.PrefetchScalarGridSpec(num_scalar_p...  11.1 us
    ppermute x9, starting transfers between devices, shift(): return lax.ppermute(arr, PLANE, pairs)  8.62 us
    all_to_all x1, waiting for transfers between devices, local(): parts = lax.all_to_all(pre, 'ep', 0, 0, tiled=True)  8.42 us
  transfers between devices with their start and end apart: 19, of which 10 were waited for; matrix products, arithmetic and copies ran while one was open for 14% of the time, Pallas kernels for 12%

commit v1 on v0

v1 whole, which is shorter than its diff:
```python
import jax
import jax.numpy as jnp
from jax import lax
from jax.experimental import pallas as pl
from jax.experimental.pallas import tpu as pltpu
from jax.sharding import Mesh
from jax.sharding import PartitionSpec as P

BF = jnp.bfloat16
F32 = jnp.float32
EXPERTS = 8
HID = 64
COLS = EXPERTS * HID
LANES = 128
SIDE = 4
FAR = (1, 3, 0, 2)
PLANE = ("z", "x", "core")
TORUS = ("ep", "z", "x")


def params(mib):
    return pltpu.CompilerParams(vmem_limit_bytes=mib << 20)


def near_core(arr):
    return pltpu.with_memory_space_constraint(arr, pltpu.VMEM)


def far_off(arr):
    return pltpu.with_memory_space_constraint(arr, pltpu.HBM)


def in_core(count):
    return [pl.BlockSpec(memory_space=pltpu.VMEM)] * count


def first_half(rows):
    return lax.broadcasted_iota(jnp.int32, (rows, LANES), 1) < HID


def dot_t(rows, mat):
    return lax.dot_general(rows, mat, (((1,), (1,)), ((), ())), preferred_element_type=F32)


def flat(ref):
    lead, rows, width = ref.shape
    return ref[...].reshape(lead * rows, width)


def pack(tok_ref, cot_ref, route_ref, gates_ref, out_ref):
    rows, full = tok_ref.shape
    width = full // SIDE
    lap = width + LANES
    eye = lax.broadcasted_iota(jnp.int32, (rows, rows), 0) == lax.broadcasted_iota(
        jnp.int32, (rows, rows), 1
    )
    lane = lax.broadcasted_iota(jnp.int32, (rows, LANES), 1)
    meta = jnp.zeros((rows, LANES), F32)
    for n, ref in enumerate((route_ref, gates_ref)):
        vals = ref[...].astype(F32)
        for k in range(2):
            column = jnp.sum(jnp.where(eye, vals[k:k + 1, :], 0.0), axis=1, keepdims=True)
            meta = jnp.where(lane == 2 * n + k, column, meta)
    meta = meta.astype(BF)
    for j in range(SIDE):
        out_ref[j, :, :width] = tok_ref[:, j * width:(j + 1) * width]
        out_ref[j, :, width:lap] = meta
        out_ref[j, :, lap:] = cot_ref[:, j * width:(j + 1) * width]


def pack_call(tokens, cotangent, routing, gates, width):
    args = (tokens, cotangent, routing.T, gates.T)
    rows = tokens.shape[0]
    out = pltpu.HBM((SIDE, rows, 2 * width + LANES), BF)
    return pl.pallas_call(
        pack,
        grid=(1,),
        in_specs=[pl.BlockSpec(a.shape, lambda i: (0, 0)) for a in args],
        out_specs=pl.BlockSpec(out.shape, lambda i: (0, 0, 0)),
        out_shape=out,
        compiler_params=params(8),
    )(*map(far_off, args))


def load(*refs):
    count = len(refs) // 2
    mats, outs, sems = refs[:count], refs[count:2 * count], refs[-1]
    copies = [pltpu.make_async_copy(mats[m], outs[m], sems.at[m]) for m in range(count)]
    for copy in copies:
        copy.start()
    for copy in copies:
        copy.wait()


def load_call(mats):
    return pl.pallas_call(
        load,
        in_specs=[pl.BlockSpec(memory_space=pl.ANY)] * len(mats),
        out_specs=in_core(len(mats)),
        out_shape=[pltpu.VMEM(m.shape, BF) for m in mats],
        scratch_shapes=[pltpu.SemaphoreType.DMA((len(mats),))],
        compiler_params=params(2),
    )(*map(far_off, mats))


def stack(*refs):
    pieces, x_ref, y_ref = refs[:SIDE], refs[SIDE], refs[SIDE + 1]
    lap, rows = x_ref.shape[2], pieces[0].shape[1]
    for n, piece in enumerate(pieces):
        x_ref[:, n * rows:(n + 1) * rows, :] = piece[:, :, :lap]
        y_ref[:, n * rows:(n + 1) * rows, :] = piece[:, :, lap:]


def stack_call(pieces, lap):
    lead, rows, width = pieces[0].shape
    return pl.pallas_call(
        stack,
        in_specs=in_core(SIDE),
        out_specs=in_core(2),
        out_shape=[
            pltpu.VMEM((lead, SIDE * rows, lap), BF),
            pltpu.VMEM((lead, SIDE * rows, width - lap), BF),
        ],
        compiler_params=params(8),
    )(*map(near_core, pieces))


def pre_acts(count, first, width):
    def body(*refs):
        x_refs, y_refs, mats = refs[:count], refs[count:2 * count], refs[2 * count:2 * count + 6]
        out_ref, x_out, y_out, meta_out, sems = refs[-5:]
        lead, short_rows = x_refs[0].shape[0], x_refs[0].shape[1]
        copies = []
        for n in range(count):
            rows_at = pl.ds(first + n * short_rows, short_rows)
            jobs = (
                (x_refs[n].at[:, :, :width], x_out.at[:, rows_at, :]),
                (y_refs[n], y_out.at[:, rows_at, :]),
                (x_refs[n].at[:, :, width:], meta_out.at[:, rows_at, :]),
            )
            for k, (src, dst) in enumerate(jobs):
                copies.append(pltpu.make_async_copy(src, dst, sems.at[n, k]))
        for copy in copies:
            copy.start()
        x_all = jnp.concatenate([flat(r) for r in x_refs], axis=0)
        y = jnp.concatenate([flat(r) for r in y_refs], axis=0)
        rows = y.shape[0]
        x, meta = x_all[:, :width], x_all[:, width:].astype(F32)
        lane = lax.broadcasted_iota(jnp.int32, (rows, COLS), 1)
        owner = (lane // HID).astype(F32)
        hit_a, hit_b = owner == meta[:, 0:1], owner == meta[:, 1:2]
        low = first_half(rows)
        for m in range(6):
            full = dot_t(y if m % 3 == 2 else x, mats[m][...])
            sums = []
            for hit in (hit_a, hit_b):
                kept = jnp.where(hit, full, 0.0)
                short = sum(kept[:, g * LANES:(g + 1) * LANES] for g in range(COLS // LANES))
                sums.append(short + pltpu.roll(short, HID, 1))
            val = jnp.where(low, sums[0], sums[1]).astype(BF)
            for n in range(count):
                part = val[n * lead * short_rows:(n + 1) * lead * short_rows]
                part = part.reshape(lead, short_rows, LANES)
                out_ref[:, n * short_rows:(n + 1) * short_rows, m * LANES:(m + 1) * LANES] = part
        for copy in copies:
            copy.wait()

    return body


def pre_call(pieces, mats, first, total, into):
    count = len(pieces) // 2
    lead, rows, _ = pieces[0].shape
    width = mats[0].shape[1]
    outer = pl.BlockSpec(memory_space=pl.ANY)
    outs = [pltpu.HBM((lead, rows * total, w), BF) for w in (6 * LANES, width, width, LANES)]
    taken = len(pieces) + 6
    return pl.pallas_call(
        pre_acts(count, first * rows, width),
        grid=(1,),
        in_specs=in_core(taken) + [outer] * len(into),
        out_specs=[
            pl.BlockSpec((lead, rows * count, 6 * LANES), lambda i: (0, first // count, 0)),
            outer,
            outer,
            outer,
        ],
        out_shape=outs,
        scratch_shapes=[pltpu.SemaphoreType.DMA((count, 3))],
        input_output_aliases={taken + n: n for n in range(len(into))},
        compiler_params=params(12),
    )(*map(near_core, pieces), *map(near_core, mats), *map(far_off, into))


def middle(plane_ref, parts_ref, meta_ref, out_ref, route_ref):
    rows = parts_ref.shape[1]
    meta = meta_ref[...].reshape(rows, LANES).astype(F32)
    low = first_half(rows)
    factor = jnp.where(low, meta[:, 2:3], meta[:, 3:4])
    prod = jnp.zeros((rows, LANES), F32)
    for side in range(2):
        vals = []
        for m in range(3):
            at = (3 * side + m) * LANES
            vals.append(sum(parts_ref[j, :, at:at + LANES].astype(F32) for j in range(SIDE)))
        gate, upper, reverse = vals
        sigma = jax.nn.sigmoid(gate)
        act = gate * sigma
        hidden = (act * upper).astype(BF).astype(F32)
        back = factor * reverse
        d_gate = back * upper * sigma * (1.0 + gate * (1.0 - sigma))
        at = 3 * side * LANES
        for n, val in enumerate((d_gate, back * act, factor * hidden)):
            low_bits = val.astype(BF)
            for j in range(SIDE):
                out_ref[j, :, at + n * LANES:at + (n + 1) * LANES] = low_bits
        prod = prod + hidden * reverse
    term_a = jnp.sum(jnp.where(low, prod, 0.0), axis=1, keepdims=True)
    term_b = jnp.sum(jnp.where(low, 0.0, prod), axis=1, keepdims=True)
    lane = lax.broadcasted_iota(jnp.int32, (rows, LANES), 1)
    route_ref[...] = jnp.where(lane == 0, term_a, jnp.where(lane == 1, term_b, 0.0)).astype(BF)


def middle_call(plane, parts, meta):
    _, rows, width = parts.shape
    return pl.pallas_call(
        middle,
        grid_spec=pltpu.PrefetchScalarGridSpec(
            num_scalar_prefetch=1,
            grid=(1,),
            in_specs=[
                pl.BlockSpec(memory_space=pltpu.VMEM),
                pl.BlockSpec((1, rows, LANES), lambda i, s: (s[0], 0, 0)),
            ],
            out_specs=[
                pl.BlockSpec((SIDE, rows, width), lambda i, s: (0, 0, 0)),
                pl.BlockSpec((rows, LANES), lambda i, s: (0, 0)),
            ],
        ),
        out_shape=[
            pltpu.HBM((SIDE, rows, width), BF),
            jax.ShapeDtypeStruct((rows, LANES), BF),
        ],
        compiler_params=params(16),
    )(plane, near_core(parts), meta)


def spread(short, route_a, route_b, owner, low):
    turned = pltpu.roll(short, HID, 1)
    val_a = jnp.where(low, short, turned)
    val_b = jnp.where(low, turned, short)
    groups = COLS // LANES
    wide_a = jnp.concatenate([val_a] * groups, axis=1)
    wide_b = jnp.concatenate([val_b] * groups, axis=1)
    return jnp.where(owner == route_a, wide_a, jnp.where(owner == route_b, wide_b, 0.0))


def dense(acts, meta, picks):
    rows = meta.shape[0]
    lane = lax.broadcasted_iota(jnp.int32, (rows, COLS), 1)
    owner, low = (lane // HID).astype(F32), first_half(rows)
    return [
        spread(
            acts[:, m * LANES:(m + 1) * LANES], meta[:, 0:1], meta[:, 1:2], owner, low
        ).astype(BF)
        for m in picks
    ]


def widen(acts_ref, meta_ref, *outs):
    for out, val in zip(outs, dense(flat(acts_ref).astype(F32), flat(meta_ref).astype(F32), range(6))):
        out[...] = val


def widen_call(acts, meta):
    lead, rows, _ = acts.shape
    return pl.pallas_call(
        widen,
        in_specs=in_core(2),
        out_specs=in_core(6),
        out_shape=[pltpu.VMEM((lead * rows, COLS), BF)] * 6,
        compiler_params=params(8),
    )(near_core(acts), near_core(meta))


def goals(z, x, core):
    spots = []
    for b in range(16):
        far, close = FAR[b // SIDE], b % SIDE
        by_z = jnp.where(core == 0, far, close)
        by_x = jnp.where(core == 0, close, far)
        spots.append(((z - by_z) & 3) * SIDE + ((x - by_x) & 3))
    return spots


def terms(plane_ref, z_ref, x_ref, core_ref, acts_ref, meta_ref, route_ref, *refs):
    mats, sent_ref, wide_ref, out_ref, sort_ref, out_sems = refs[:4], *refs[4:]
    lead, rows, _ = acts_ref.shape
    deep = out_ref.shape[2] - LANES
    chunk = 256
    count = deep // chunk
    cuts = [slice(c * chunk, (c + 1) * chunk) for c in range(count)] + [slice(deep, deep + LANES)]
    stores = [
        pltpu.make_async_copy(out_ref.at[:, :, cut], sent_ref.at[:, :, cut], out_sems.at[c])
        for c, cut in enumerate(cuts)
    ]
    acts, meta = flat(acts_ref).astype(F32), flat(meta_ref).astype(F32)
    route = route_ref[...].astype(F32)
    width = acts.shape[1]
    spots = goals(z_ref[0], x_ref[0], core_ref[0])
    for j in range(lead):
        mine = jnp.where(j == plane_ref[0], 1.0, 0.0)
        for b in range(16):
            at = j * rows + b * 8
            spot = pl.ds(pl.multiple_of(j * rows + spots[b] * 8, 8), 8)
            sort_ref[spot, :width] = acts[at:at + 8]
            sort_ref[spot, width:width + LANES] = meta[at:at + 8]
            sort_ref[spot, width + LANES:] = route[b * 8:b * 8 + 8] * mine
    moved = sort_ref[:, :width], sort_ref[:, width:width + LANES]
    for n, val in enumerate(dense(*moved, (0, 1, 3, 4))):
        wide_ref[:, n * COLS:(n + 1) * COLS] = val
    out_ref[:, :, cuts[-1]] = sort_ref[:, width + LANES:].astype(BF).reshape(lead, rows, LANES)
    stores[-1].start()
    for c in range(count):
        mat = jnp.concatenate([m[:, cuts[c]] for m in mats], axis=0)
        total = jnp.dot(wide_ref[...], mat, preferred_element_type=F32)
        out_ref[:, :, cuts[c]] = total.astype(BF).reshape(lead, rows, chunk)
        stores[c].start()
    for copy in stores:
        copy.wait()


def terms_call(spots, acts, meta, route, mats):
    lead, rows, _ = acts.shape
    deep = mats[0].shape[1]
    out = (lead, rows, deep + LANES)
    chunk = 256
    outer = pl.BlockSpec(memory_space=pl.ANY)
    return pl.pallas_call(
        terms,
        grid_spec=pltpu.PrefetchScalarGridSpec(
            num_scalar_prefetch=4,
            grid=(1,),
            in_specs=in_core(7),
            out_specs=outer,
            scratch_shapes=[
                pltpu.VMEM((lead * rows, 4 * COLS), BF),
                pltpu.VMEM(out, BF),
                pltpu.VMEM((lead * rows, 8 * LANES), F32),
                pltpu.SemaphoreType.DMA((deep // chunk + 1,)),
            ],
        ),
        out_shape=pltpu.HBM(out, BF),
        compiler_params=params(16),
    )(*spots, *map(near_core, (acts, meta, route, *mats)))


def finish(parts_ref, token_ref, route_ref):
    rows, width = parts_ref.shape[1:]
    deep = width - LANES
    group = parts_ref.shape[0] // SIDE
    route = jnp.zeros((rows, LANES), F32)
    for j in range(SIDE):
        total = jnp.zeros((rows, width), F32)
        for n in range(group):
            total = total + parts_ref[j * group + n].astype(F32)
        token_ref[:, j * deep:(j + 1) * deep] = total[:, :deep].astype(BF)
        route = route + total[:, deep:]
    eye = lax.broadcasted_iota(jnp.int32, (rows, rows), 0) == lax.broadcasted_iota(
        jnp.int32, (rows, rows), 1
    )
    for k in range(2):
        column = route[:, k:k + 1]
        route_ref[k:k + 1, :] = jnp.sum(jnp.where(eye, column, 0.0), axis=0, keepdims=True)


def finish_call(parts, deep):
    _, rows, _ = parts.shape
    return pl.pallas_call(
        finish,
        in_specs=in_core(1),
        out_shape=[
            jax.ShapeDtypeStruct((rows, deep * SIDE), BF),
            jax.ShapeDtypeStruct((2, rows), F32),
        ],
        compiler_params=params(8),
    )(near_core(parts))


def place(z, x, core):
    return (z % SIDE) * 8 + (x % SIDE) * 2 + core


def shift(arr, stage, by):
    pairs = []
    for z in range(SIDE):
        for x in range(SIDE):
            for core in range(2):
                along_x = core == stage
                goal = place(z, x + by, core) if along_x else place(z + by, x, core)
                pairs.append((place(z, x, core), goal))
    return lax.ppermute(arr, PLANE, pairs)


def swap(arr):
    return lax.ppermute(arr, "core", [(0, 1), (1, 0)])


def contract_rows(left, right):
    return lax.dot_general(left, right, (((0,), (0,)), ((), ())), preferred_element_type=F32)


def local(tokens, cotangent, routing, route_gates, gate_weight, up_weight, down_weight):
    tok_rows, _ = tokens.shape
    width = gate_weight.shape[2]
    own_mats = [w.reshape(COLS, width) for w in (gate_weight, up_weight, down_weight)]
    their_mats = [swap(w) for w in own_mats]
    mats = load_call(own_mats + their_mats)
    send = pack_call(tokens, cotangent, routing, route_gates, width)
    own = lax.all_to_all(send, "ep", 0, 0, tiled=True)
    near = [own] + [shift(own, 0, s) for s in range(1, SIDE)]
    lap = width + LANES
    x_0, y_0 = stack_call(near, lap)
    x_1 = shift(x_0, 1, 1)
    y_3 = shift(y_0, 1, 3)
    x_3 = shift(x_0, 1, 3)
    y_1 = shift(y_0, 1, 1)
    x_2 = shift(x_1, 1, 1)
    y_2 = shift(y_3, 1, 3)
    plane, *spot = (
        lax.axis_index(a).astype(jnp.int32).reshape(1) for a in ("ep",) + PLANE
    )
    state = pre_call([x_0, y_0], mats, 2, SIDE, [])
    state = pre_call([x_1, x_3, y_1, y_3], mats, 0, SIDE, state)
    pre, x_rows, y_rows, meta_rows = pre_call([x_2, y_2], mats, 3, SIDE, state)
    parts = lax.all_to_all(pre, "ep", 0, 0, tiled=True)
    done, route = middle_call(plane, parts, meta_rows)
    acts = lax.all_to_all(done, "ep", 0, 0, tiled=True)
    sent = terms_call((plane, *spot), acts, meta_rows, route, mats[:2] + mats[3:5])
    got = lax.all_to_all(sent.reshape(-1, tok_rows, lap), TORUS, 0, 0, tiled=True)
    wides = widen_call(acts, meta_rows)
    token_grad, route_sum = finish_call(got, width)
    route_grad = route_sum.T
    x_rows, y_rows = (r.reshape(-1, width) for r in (x_rows, y_rows))
    grads = []
    for m in range(3):
        rows = y_rows if m == 2 else x_rows
        theirs = swap(contract_rows(wides[3 + m], rows).astype(BF))
        mine = contract_rows(wides[m], rows) + theirs.astype(F32)
        grads.append(mine.astype(BF).reshape(gate_weight.shape))
    return (token_grad, route_grad, *grads)


def solution(mesh):
    names = ("ep", "z", "x", "core")
    fine = Mesh(mesh.devices.reshape(SIDE, SIDE, SIDE, 2), names)
    rows = P(names, None)
    mats = P(None, PLANE, "ep")

    return jax.shard_map(
        local,
        mesh=fine,
        in_specs=(rows, rows, rows, rows, mats, mats, mats),
        out_specs=(rows, rows, mats, mats, mats),
        check_vma=False,
    )
```

time: 177 us -> 152 us (0.86)
  waiting for transfers between devices: 69.8 us -> 42 us
  blocking collectives: 0 us -> 24.5 us
  Pallas kernels: 39.2 us -> 28.3 us
  other arithmetic: 5.84 us -> 0 us
  local copies, waits for them, and re-layouts: 12.4 us -> 8.29 us
    all_to_all x0 -> x2, blocking collectives: none -> 24.5 us  [the longest x1 12.9 us: local(): acts = lax.all_to_all(done, 'ep', 0, 0, tiled=True)]
    ppermute x9, waiting for transfers between devices: 31.8 us -> 15.5 us  [shift(): return lax.ppermute(arr, PLANE, pairs)]
    all_to_all x2 -> x0, waiting for transfers between devices: 11.9 us -> none  [the longest x1 6.03 us: local(): own = lax.all_to_all(send, 'ep', 0, 0, tiled=True)]
    all_to_all x2 -> x0, starting transfers between devices: 8.07 us -> none  [the longest x1 4.57 us: local(): own = lax.all_to_all(send, 'ep', 0, 0, tiled=True)]
    ppermute x9, starting transfers between devices: 8.62 us -> 16.7 us  [shift(): return lax.ppermute(arr, PLANE, pairs)]
    pallas_call x1, Pallas kernels: 11.1 us -> 5.52 us  [terms_call(): pl.pallas_call(terms, grid_spec=pltpu.PrefetchScalarGridSpec(num_scalar_p...]
    concatenate x7 -> x0, other arithmetic: 5.07 us -> none  [the longest x2 2.06 us: local(): stack = lambda ps: jnp.concatenate(ps, axis=1)]
    pallas_call x4 -> x8, Pallas kernels: 25.8 us -> 21.7 us  [the longest x3 13.2 us: pre_call(): pl.pallas_call(pre_acts(count, first * rows, width), grid=(1,), in_specs=...]
  transfers between devices with their start and end apart: 19 -> 17, of which waited for: 10 -> 7; matrix products, arithmetic and copies ran while one was open for 14% -> 11% of each run, Pallas kernels for 12% -> 13%
where the time goes in v1:
time: 152 us
  waiting for transfers between devices  42 us (28%)
  Pallas kernels  28.3 us (19%)
  starting transfers between devices  27.9 us (18%)
  blocking collectives  24.5 us (16%)
  matrix products  19.7 us (13%)
  local copies, waits for them, and re-layouts  8.29 us (5%)
    dot_general x6, matrix products, contract_rows(): lax.dot_general(left, right, (((0,), (0,)), ((), ())), preferred_element_...  19.7 us
    all_to_all x1, waiting for transfers between devices, local(): lax.all_to_all(sent.reshape(-1, tok_rows, lap), TORUS, 0, 0, tiled=True)  17.2 us
    ppermute x9, starting transfers between devices, shift(): return lax.ppermute(arr, PLANE, pairs)  16.7 us
    ppermute x9, waiting for transfers between devices, shift(): return lax.ppermute(arr, PLANE, pairs)  15.5 us
    pallas_call x3, Pallas kernels, pre_call(): pl.pallas_call(pre_acts(count, first * rows, width), grid=(1,), in_specs=...  13.2 us
    all_to_all x1, blocking collectives, local(): acts = lax.all_to_all(done, 'ep', 0, 0, tiled=True)  12.9 us
    all_to_all x1, blocking collectives, local(): own = lax.all_to_all(send, 'ep', 0, 0, tiled=True)  11.6 us
    all_to_all x1, waiting for transfers between devices, local(): parts = lax.all_to_all(pre, 'ep', 0, 0, tiled=True)  9.27 us
  transfers between devices with their start and end apart: 17, of which 7 were waited for; matrix products, arithmetic and copies ran while one was open for 11% of the time, Pallas kernels for 13%

profile of v1, /device:TPU:0, one launch (start us, length us, event | category | flops | bytes accessed | tf_op | source)
XLA Modules:
  0.0 151.5 jit_solution(12705804878453430059)
XLA Ops:
  0.6 0.1 collective-permute-start.7
  0.7 0.5 collective-permute-start.8
  1.2 0.1 collective-permute-start.9
  1.3 1.7 %shard_map.110 = bf16[4,8,3712]{2,1,0:T(8,128)(2,1)} custom-call(bf16[8,7168]{1,0:T(8,128)(2,1)} %tok_ref.1, bf16[8,7168]{1,0:T(8,128)(2,1)} %cot_ref.1, s32[2,8]{1,0:T(2,128)} %bitcast.41, bf16[2,8]{1,0:T(2,128)(2,1)} %bitcast.42), custom_call_target="tpu_custom_call" | custom-call | tf_op jit(solution)/shard_map/pallas_call | solution.py:75
  3.0 11.6 %all_to_all.20.refs_0_ = bf16[4,8,3712]{2,1,0:T(8,128)(2,1)S(1)} all-to-all(bf16[4,8,3712]{2,1,0:T(8,128)(2,1)} %shard_map.110), channel_id=1, replica_groups=mesh['ep'=4,'z'=4,'x'=4,'core'=2] {'ep'}, dimensions={0} | all-to-all | bytes 475136 | tf_op jit(solution)/shard_map/all_to_all | solution.py:420
  14.6 1.5 collective-permute-start
  16.1 2.7 %collective-permute-start.1 = (bf16[4,8,3712]{2,1,0:T(8,128)(2,1)S(1)}, bf16[4,8,3712]{2,1,0:T(8,128)(2,1)S(1)}, u32[]{:S(2)}, u32[]{:S(2)}) collective-permute-start(bf16[4,8,3712]{2,1,0:T(8,128)(2,1)S(1)} %all_to_all.20.refs_0_), channel_id=1, source_target_pairs={{0,4},{1,17},{2,6},{3,19},{4,0},{5,21},{6,2},{7,23},{8,12},{9,25},... | collective-permute-start | bytes 712712 | tf_op jit(solution)/shard_map/ppermute | solution.py:402
  18.8 3.1 %collective-permute-done.refs_1_ = bf16[4,8,3712]{2,1,0:T(8,128)(2,1)S(1)} collective-permute-done((bf16[4,8,3712]{2,1,0:T(8,128)(2,1)S(1)}, bf16[4,8,3712]{2,1,0:T(8,128)(2,1)S(1)}, u32[]{:S(2)}, u32[]{:S(2)}) %collective-permute-start) | collective-permute-done | bytes 237600 | tf_op jit(solution)/shard_map/ppermute | solution.py:402
  21.9 1.5 %collective-permute-start.2 = (bf16[4,8,3712]{2,1,0:T(8,128)(2,1)S(1)}, bf16[4,8,3712]{2,1,0:T(8,128)(2,1)S(1)}, u32[]{:S(2)}, u32[]{:S(2)}) collective-permute-start(bf16[4,8,3712]{2,1,0:T(8,128)(2,1)S(1)} %all_to_all.20.refs_0_), channel_id=1, source_target_pairs={{0,6},{1,25},{2,0},{3,27},{4,2},{5,29},{6,4},{7,31},{8,14},{9,1},{... | collective-permute-start | bytes 712712 | tf_op jit(solution)/shard_map/ppermute | solution.py:402
  23.5 2.0 %collective-permute-done.1.refs_2_ = bf16[4,8,3712]{2,1,0:T(8,128)(2,1)S(1)} collective-permute-done((bf16[4,8,3712]{2,1,0:T(8,128)(2,1)S(1)}, bf16[4,8,3712]{2,1,0:T(8,128)(2,1)S(1)}, u32[]{:S(2)}, u32[]{:S(2)}) %collective-permute-start.1) | collective-permute-done | bytes 237600 | tf_op jit(solution)/shard_map/ppermute | solution.py:402
  25.5 2.6 %collective-permute-done.2.refs_3_ = bf16[4,8,3712]{2,1,0:T(8,128)(2,1)S(1)} collective-permute-done((bf16[4,8,3712]{2,1,0:T(8,128)(2,1)S(1)}, bf16[4,8,3712]{2,1,0:T(8,128)(2,1)S(1)}, u32[]{:S(2)}, u32[]{:S(2)}) %collective-permute-start.2) | collective-permute-done | bytes 237600 | tf_op jit(solution)/shard_map/ppermute | solution.py:402
  28.0 0.1 shard_map.111
  28.1 2.0 %collective-permute-start.3 = (bf16[4,32,1920]{2,1,0:T(8,128)(2,1)S(1)}, bf16[4,32,1920]{2,1,0:T(8,128)(2,1)S(1)}, u32[]{:S(2)}, u32[]{:S(2)}) collective-permute-start(bf16[4,32,1920]{2,1,0:T(8,128)(2,1)S(1)} %get-tuple-element.35.refs_0_), channel_id=1, source_target_pairs={{0,8},{1,3},{2,10},{3,5},{4,12},{5,7},{6,14},{7,1},{8,16},{9,11},{... | collective-permute-start | bytes 1474568 | tf_op jit(solution)/shard_map/ppermute | solution.py:402
  30.1 2.2 %collective-permute-start.5 = (bf16[4,32,1792]{2,1,0:T(8,128)(2,1)S(1)}, bf16[4,32,1792]{2,1,0:T(8,128)(2,1)S(1)}, u32[]{:S(2)}, u32[]{:S(2)}) collective-permute-start(bf16[4,32,1792]{2,1,0:T(8,128)(2,1)S(1)} %get-tuple-element.36.refs_1_), channel_id=1, source_target_pairs={{0,24},{1,7},{2,26},{3,1},{4,28},{5,3},{6,30},{7,5},{8,0},{9,15},{... | collective-permute-start | bytes 1376264 | tf_op jit(solution)/shard_map/ppermute | solution.py:402
  32.3 6.3 %collective-permute-done.5.refs_3_ = bf16[4,32,1792]{2,1,0:T(8,128)(2,1)S(1)} collective-permute-done((bf16[4,32,1792]{2,1,0:T(8,128)(2,1)S(1)}, bf16[4,32,1792]{2,1,0:T(8,128)(2,1)S(1)}, u32[]{:S(2)}, u32[]{:S(2)}) %collective-permute-start.5) | collective-permute-done | bytes 458784 | tf_op jit(solution)/shard_map/ppermute | solution.py:402
  38.6 3.4 %collective-permute-start.10 = (bf16[4,32,1920]{2,1,0:T(8,128)(2,1)S(1)}, bf16[4,32,1920]{2,1,0:T(8,128)(2,1)S(1)}, u32[]{:S(2)}, u32[]{:S(2)}) collective-permute-start(bf16[4,32,1920]{2,1,0:T(8,128)(2,1)S(1)} %get-tuple-element.35.refs_0_), channel_id=1, source_target_pairs={{0,24},{1,7},{2,26},{3,1},{4,28},{5,3},{6,30},{7,5},{8,0},{9,15},{... | collective-permute-start | bytes 1474568 | tf_op jit(solution)/shard_map/ppermute | solution.py:402
  42.0 0.0 collective-permute-done.3.refs_0_
  42.0 0.0 collective-permute-start.4
  42.0 0.0 collective-permute-done.7.refs_3_
  42.0 0.0 copy-start.14
  42.0 0.5 collective-permute-start.11
  42.5 0.0 collective-permute-done.8.refs_4_
  42.5 2.8 %collective-permute-start.6 = (bf16[4,32,1792]{2,1,0:T(8,128)(2,1)S(1)}, bf16[4,32,1792]{2,1,0:T(8,128)(2,1)S(1)}, u32[]{:S(2)}, u32[]{:S(2)}) collective-permute-start(bf16[4,32,1792]{2,1,0:T(8,128)(2,1)S(1)} %collective-permute-done.5.refs_3_), channel_id=1, source_target_pairs={{0,24},{1,7},{2,26},{3,1},{4,28},{5,3},{6,30},{7,5},{8,0},{9,15},{... | collective-permute-start | bytes 1376264 | tf_op jit(solution)/shard_map/ppermute | solution.py:402
  45.3 0.0 collective-permute-done.9.refs_5_
  45.3 0.0 copy-done.14
  45.3 0.0 copy-start.16
  45.4 1.2 copy-done.16
  46.6 4.2 %shard_map.112 = (bf16[512,1792]{1,0:T(8,128)(2,1)S(1)}, bf16[512,1792]{1,0:T(8,128)(2,1)S(1)}, bf16[512,1792]{1,0:T(8,128)(2,1)S(1)}, bf16[512,1792]{1,0:T(8,12...) custom-call(bf16[512,1792]{1,0:T(8,128)(2,1)} %bitcast.36, bf16[512,1792]{1,0:T(8,128)(2,1)} %bitcast.38, ...), custom_call_target="tpu_custom_call" | custom-call | tf_op jit(solution)/shard_map/pallas_call | solution.py:96
  50.8 0.0 copy-start
  50.9 4.5 %shard_map.113 = (bf16[4,128,768]{2,1,0:T(8,128)(2,1)}, bf16[4,128,1792]{2,1,0:T(8,128)(2,1)}, bf16[4,128,1792]{2,1,0:T(8,128)(2,1)}, bf16[4,128,128]{2,1,0:T(8,128)(2,1)}) custom-call(bf16[4,32,1920]{2,1,0:T(8,128)(2,1)S(1)} %get-tuple-element.35.refs_0_, bf16[4,32,1792]{2,1,0:T(8,128)(2,1)S(1)} %get-tuple-element.36.refs_1_, ...), custom_call_target="tpu_custom_call" | custom-call | tf_op jit(solution)/shard_map/pallas_call | solution.py:178
  55.4 1.6 %collective-permute-done.11.refs_2_ = bf16[4,32,1792]{2,1,0:T(8,128)(2,1)S(1)} collective-permute-done((bf16[4,32,1792]{2,1,0:T(8,128)(2,1)S(1)}, bf16[4,32,1792]{2,1,0:T(8,128)(2,1)S(1)}, u32[]{:S(2)}, u32[]{:S(2)}) %collective-permute-start.11) | collective-permute-done | bytes 458784 | tf_op jit(solution)/shard_map/ppermute | solution.py:402
  56.9 0.0 collective-permute-done.10.refs_1_
  56.9 4.2 %shard_map.114 = (bf16[4,128,768]{2,1,0:T(8,128)(2,1)}, bf16[4,128,1792]{2,1,0:T(8,128)(2,1)}, bf16[4,128,1792]{2,1,0:T(8,128)(2,1)}, bf16[4,128,128]{2,1,0:T(8,128)(2,1)}) custom-call(bf16[4,32,1920]{2,1,0:T(8,128)(2,1)S(1)} %collective-permute-done.3.refs_0_, ...), custom_call_target="tpu_custom_call", output_to_operand_aliasing={{0}: (10, {}), {1}: (11, {}), {2}: (12, {}), {3}: (13, {})} | custom-call | tf_op jit(solution)/shard_map/pallas_call | solution.py:178
  61.1 0.0 collective-permute-done.6.refs_1_
  61.1 0.0 collective-permute-done.4.refs_0_
  61.2 4.5 %shard_map.115 = (bf16[4,128,768]{2,1,0:T(8,128)(2,1)}, bf16[4,128,1792]{2,1,0:T(8,128)(2,1)}, bf16[4,128,1792]{2,1,0:T(8,128)(2,1)}, bf16[4,128,128]{2,1,0:T(8,128)(2,1)}) custom-call(bf16[4,32,1920]{2,1,0:T(8,128)(2,1)S(1)} %collective-permute-done.4.refs_0_, ...), custom_call_target="tpu_custom_call", output_to_operand_aliasing={{0}: (8, {}), {1}: (9, {}), {2}: (10, {}), {3}: (11, {})} | custom-call | tf_op jit(solution)/shard_map/pallas_call | solution.py:178
  65.7 3.7 %all-to-all-start.1 = ((bf16[4,128,768]{2,1,0:T(8,128)(2,1)}), bf16[4,128,768]{2,1,0:T(8,128)(2,1)S(1)}, u32[]{:S(2)}, u32[]{:S(2)}) async-start(bf16[4,128,768]{2,1,0:T(8,128)(2,1)} %get-tuple-element.51), calls=%async_computation.1 | async-start | bytes 1572864 | tf_op jit(solution)/shard_map/all_to_all | solution.py:436
  69.4 9.3 %all-to-all-done.1.parts_ref = bf16[4,128,768]{2,1,0:T(8,128)(2,1)S(1)} async-done(((bf16[4,128,768]{2,1,0:T(8,128)(2,1)}), bf16[4,128,768]{2,1,0:T(8,128)(2,1)S(1)}, u32[]{:S(2)}, u32[]{:S(2)}) %all-to-all-start.1) | async-done | bytes 786464 | tf_op jit(solution)/shard_map/all_to_all | solution.py:436
  78.7 0.9 copy-done.6
  79.6 1.1 shard_map.116
  80.7 12.9 %all_to_all.21.acts_ref = bf16[4,128,768]{2,1,0:T(8,128)(2,1)S(1)} all-to-all(bf16[4,128,768]{2,1,0:T(8,128)(2,1)} %get-tuple-element.53), channel_id=1, replica_groups=mesh['ep'=4,'z'=4,'x'=4,'core'=2] {'ep'}, dimensions={0} | all-to-all | bytes 1572864 | tf_op jit(solution)/shard_map/all_to_all | solution.py:438
  93.7 1.5 shard_map.119
  95.2 0.8 copy-done.8
  96.0 0.8 copy-done.10
  96.8 2.4 %convolution_convert_fusion = bf16[512,1792]{1,0:T(8,128)(2,1)} fusion(bf16[512,512]{1,0:T(8,128)(2,1)S(1)} %get-tuple-element.64, bf16[512,1792]{1,0:T(8,128)(2,1)S(1)} %bitcast.34), kind=kOutput, calls=%fused_computation.3 | convolution fusion | flops 940441600 | bytes 4194304 | tf_op jit(solution)/shard_map/dot_general | solution.py:410
  99.2 0.0 collective-permute-start.14
  99.2 2.4 %convolution_convert_fusion.1 = bf16[512,1792]{1,0:T(8,128)(2,1)} fusion(bf16[512,512]{1,0:T(8,128)(2,1)S(1)} %get-tuple-element.61, bf16[512,1792]{1,0:T(8,128)(2,1)S(1)} %bitcast.29), kind=kOutput, calls=%fused_computation.4 | convolution fusion | flops 940441600 | bytes 4194304 | tf_op jit(solution)/shard_map/dot_general | solution.py:410
  101.5 0.5 collective-permute-start.13
  102.0 2.4 %convolution_convert_fusion.2 = bf16[512,1792]{1,0:T(8,128)(2,1)} fusion(bf16[512,512]{1,0:T(8,128)(2,1)S(1)} %get-tuple-element.59, bf16[512,1792]{1,0:T(8,128)(2,1)S(1)} %bitcast.30), kind=kOutput, calls=%fused_computation.5 | convolution fusion | flops 940441600 | bytes 4194304 | tf_op jit(solution)/shard_map/dot_general | solution.py:410
  104.5 0.0 collective-permute-start.12
  104.5 1.5 copy-done.1
  106.0 1.5 copy-done.3
  107.5 1.5 copy-done.5
  109.0 5.5 %shard_map.117 = bf16[4,128,1920]{2,1,0:T(8,128)(2,1)} custom-call(s32[1]{0:T(128)} %bitcast.plane_ref, s32[1]{0:T(128)} %bitcast.1.z_ref, s32[1]{0:T(128)} %bitcast.2.x_ref, s32[1]{0:T(128)} %bitcast.3.core_ref, bf16[4,128,768]{2,1,0:T(8,128)(2,1)S(1)} %all_to_all.21.acts_ref, bf16[4,128,128]{2,1,0:T(8,128)(2,1)S(1)} %copy-done.7, ...), custom_call_target="tpu_custom_call" | custom-call | tf_op jit(solution)/shard_map/pallas_call | solution.py:339
  114.5 6.4 %all-to-all-start.3 = ((bf16[64,8,1920]{2,1,0:T(8,128)(2,1)}), bf16[64,8,1920]{2,1,0:T(8,128)(2,1)S(1)}, u32[]{:S(2)}, u32[]{:S(2)}) async-start(bf16[64,8,1920]{2,1,0:T(8,128)(2,1)} %bitcast.28), calls=%async_computation.3 | async-start | bytes 3932160 | tf_op jit(solution)/shard_map/all_to_all | solution.py:440
  120.9 0.0 collective-permute-done.14
  120.9 0.0 copy-start.12
  120.9 4.7 %add_convert_fusion = bf16[512,1792]{1,0:T(8,128)(2,1)} fusion(bf16[512,1792]{1,0:T(8,128)(2,1)} %collective-permute-done.14, bf16[512,512]{1,0:T(8,128)(2,1)} %copy-done.10, bf16[512,1792]{1,0:T(8,128)(2,1)} %bitcast.33), kind=kOutput, calls=%fused_computation | convolution fusion | flops 942276608 | bytes 6029312 | tf_op jit(solution)/shard_map/dot_general | solution.py:410
  125.6 0.0 collective-permute-done.13
  125.7 3.9 %add_convert_fusion.1 = bf16[512,1792]{1,0:T(8,128)(2,1)} fusion(bf16[512,1792]{1,0:T(8,128)(2,1)} %collective-permute-done.13, bf16[512,512]{1,0:T(8,128)(2,1)S(1)} %copy-done.9, bf16[512,1792]{1,0:T(8,128)(2,1)S(1)} %bitcast.31), kind=kOutput, calls=%fused_computation.1 | convolution fusion | flops 942276608 | bytes 6029312 | tf_op jit(solution)/shard_map/dot_general | solution.py:410
  129.5 0.0 collective-permute-done.12
  129.5 3.9 %add_convert_fusion.2 = bf16[512,1792]{1,0:T(8,128)(2,1)} fusion(bf16[512,1792]{1,0:T(8,128)(2,1)} %collective-permute-done.12, bf16[512,512]{1,0:T(8,128)(2,1)S(1)} %get-tuple-element.57, bf16[512,1792]{1,0:T(8,128)(2,1)S(1)} %bitcast.32), kind=kOutput, calls=%fused_computation.2 | convolution fusion | flops 942276608 | bytes 6029312 | tf_op jit(solution)/shard_map/dot_general | solution.py:410
  133.4 17.2 %all-to-all-done.3.parts_ref = bf16[64,8,1920]{2,1,0:T(8,128)(2,1)S(1)} async-done(((bf16[64,8,1920]{2,1,0:T(8,128)(2,1)}), bf16[64,8,1920]{2,1,0:T(8,128)(2,1)S(1)}, u32[]{:S(2)}, u32[]{:S(2)}) %all-to-all-start.3) | async-done | bytes 1966112 | tf_op jit(solution)/shard_map/all_to_all | solution.py:440
  150.6 0.9 shard_map.118
  (22 shorter events, 0.0 us)
Async XLA Ops:
  0.6 41.4 %collective-permute-start.7 = (bf16[512,1792]{1,0:T(8,128)(2,1)}, bf16[512,1792]{1,0:T(8,128)(2,1)S(1)}, u32[]{:S(2)}, u32[]{:S(2)}) collective-permute-start(bf16[512,1792]{1,0:T(8,128)(2,1)} %bitcast.35), channel_id=1, source_target_pairs={{0,1},{1,0},{2,3},{3,2},{4,5},{5,4},{6,7},{7,6},{8,9},{9,8},{10,11... | collective-permute-start | bytes 5505032 | tf_op jit(solution)/shard_map/ppermute | solution.py:406
  0.7 41.8 %collective-permute-start.8 = (bf16[512,1792]{1,0:T(8,128)(2,1)}, bf16[512,1792]{1,0:T(8,128)(2,1)S(1)}, u32[]{:S(2)}, u32[]{:S(2)}) collective-permute-start(bf16[512,1792]{1,0:T(8,128)(2,1)} %bitcast.37), channel_id=1, source_target_pairs={{0,1},{1,0},{2,3},{3,2},{4,5},{5,4},{6,7},{7,6},{8,9},{9,8},{10,11... | collective-permute-start | bytes 5505032 | tf_op jit(solution)/shard_map/ppermute | solution.py:406
  1.2 44.1 %collective-permute-start.9 = (bf16[512,1792]{1,0:T(8,128)(2,1)}, bf16[512,1792]{1,0:T(8,128)(2,1)S(1)}, u32[]{:S(2)}, u32[]{:S(2)}) collective-permute-start(bf16[512,1792]{1,0:T(8,128)(2,1)} %bitcast.39), channel_id=1, source_target_pairs={{0,1},{1,0},{2,3},{3,2},{4,5},{5,4},{6,7},{7,6},{8,9},{9,8},{10,11... | collective-permute-start | bytes 5505032 | tf_op jit(solution)/shard_map/ppermute | solution.py:406
  14.6 7.3 %collective-permute-start = (bf16[4,8,3712]{2,1,0:T(8,128)(2,1)S(1)}, bf16[4,8,3712]{2,1,0:T(8,128)(2,1)S(1)}, u32[]{:S(2)}, u32[]{:S(2)}) collective-permute-start(bf16[4,8,3712]{2,1,0:T(8,128)(2,1)S(1)} %all_to_all.20.refs_0_), channel_id=1, source_target_pairs={{0,2},{1,9},{2,4},{3,11},{4,6},{5,13},{6,0},{7,15},{8,10},{9,17},{... | collective-permute-start | bytes 712712 | tf_op jit(solution)/shard_map/ppermute | solution.py:402
  16.1 9.4 %collective-permute-start.1 = (bf16[4,8,3712]{2,1,0:T(8,128)(2,1)S(1)}, bf16[4,8,3712]{2,1,0:T(8,128)(2,1)S(1)}, u32[]{:S(2)}, u32[]{:S(2)}) collective-permute-start(bf16[4,8,3712]{2,1,0:T(8,128)(2,1)S(1)} %all_to_all.20.refs_0_), channel_id=1, source_target_pairs={{0,4},{1,17},{2,6},{3,19},{4,0},{5,21},{6,2},{7,23},{8,12},{9,25},... | collective-permute-start | bytes 712712 | tf_op jit(solution)/shard_map/ppermute | solution.py:402
  21.9 6.1 %collective-permute-start.2 = (bf16[4,8,3712]{2,1,0:T(8,128)(2,1)S(1)}, bf16[4,8,3712]{2,1,0:T(8,128)(2,1)S(1)}, u32[]{:S(2)}, u32[]{:S(2)}) collective-permute-start(bf16[4,8,3712]{2,1,0:T(8,128)(2,1)S(1)} %all_to_all.20.refs_0_), channel_id=1, source_target_pairs={{0,6},{1,25},{2,0},{3,27},{4,2},{5,29},{6,4},{7,31},{8,14},{9,1},{... | collective-permute-start | bytes 712712 | tf_op jit(solution)/shard_map/ppermute | solution.py:402
  28.1 13.9 %collective-permute-start.3 = (bf16[4,32,1920]{2,1,0:T(8,128)(2,1)S(1)}, bf16[4,32,1920]{2,1,0:T(8,128)(2,1)S(1)}, u32[]{:S(2)}, u32[]{:S(2)}) collective-permute-start(bf16[4,32,1920]{2,1,0:T(8,128)(2,1)S(1)} %get-tuple-element.35.refs_0_), channel_id=1, source_target_pairs={{0,8},{1,3},{2,10},{3,5},{4,12},{5,7},{6,14},{7,1},{8,16},{9,11},{... | collective-permute-start | bytes 1474568 | tf_op jit(solution)/shard_map/ppermute | solution.py:402
  30.1 8.5 %collective-permute-start.5 = (bf16[4,32,1792]{2,1,0:T(8,128)(2,1)S(1)}, bf16[4,32,1792]{2,1,0:T(8,128)(2,1)S(1)}, u32[]{:S(2)}, u32[]{:S(2)}) collective-permute-start(bf16[4,32,1792]{2,1,0:T(8,128)(2,1)S(1)} %get-tuple-element.36.refs_1_), channel_id=1, source_target_pairs={{0,24},{1,7},{2,26},{3,1},{4,28},{5,3},{6,30},{7,5},{8,0},{9,15},{... | collective-permute-start | bytes 1376264 | tf_op jit(solution)/shard_map/ppermute | solution.py:402
  38.6 18.4 %collective-permute-start.10 = (bf16[4,32,1920]{2,1,0:T(8,128)(2,1)S(1)}, bf16[4,32,1920]{2,1,0:T(8,128)(2,1)S(1)}, u32[]{:S(2)}, u32[]{:S(2)}) collective-permute-start(bf16[4,32,1920]{2,1,0:T(8,128)(2,1)S(1)} %get-tuple-element.35.refs_0_), channel_id=1, source_target_pairs={{0,24},{1,7},{2,26},{3,1},{4,28},{5,3},{6,30},{7,5},{8,0},{9,15},{... | collective-permute-start | bytes 1474568 | tf_op jit(solution)/shard_map/ppermute | solution.py:402
  42.0 19.2 %collective-permute-start.4 = (bf16[4,32,1920]{2,1,0:T(8,128)(2,1)S(1)}, bf16[4,32,1920]{2,1,0:T(8,128)(2,1)S(1)}, u32[]{:S(2)}, u32[]{:S(2)}) collective-permute-start(bf16[4,32,1920]{2,1,0:T(8,128)(2,1)S(1)} %collective-permute-done.3.refs_0_), channel_id=1, source_target_pairs={{0,8},{1,3},{2,10},{3,5},{4,12},{5,7},{6,14},{7,1},{8,16},{9,11},{... | collective-permute-start | bytes 1474568 | tf_op jit(solution)/shard_map/ppermute | solution.py:402
  42.0 3.3 %copy-start.14 = (bf16[512,1792]{1,0:T(8,128)(2,1)}, bf16[512,1792]{1,0:T(8,128)(2,1)S(1)}, u32[]{:S(2)}) copy-start(bf16[512,1792]{1,0:T(8,128)(2,1)S(1)} %collective-permute-done.7.refs_3_) | copy-start | bytes 5505028
  42.0 14.9 %collective-permute-start.11 = (bf16[4,32,1792]{2,1,0:T(8,128)(2,1)S(1)}, bf16[4,32,1792]{2,1,0:T(8,128)(2,1)S(1)}, u32[]{:S(2)}, u32[]{:S(2)}) collective-permute-start(bf16[4,32,1792]{2,1,0:T(8,128)(2,1)S(1)} %get-tuple-element.36.refs_1_), channel_id=1, source_target_pairs={{0,8},{1,3},{2,10},{3,5},{4,12},{5,7},{6,14},{7,1},{8,16},{9,11},{... | collective-permute-start | bytes 1376264 | tf_op jit(solution)/shard_map/ppermute | solution.py:402
  42.5 2.8 %copy-start.15 = (bf16[512,1792]{1,0:T(8,128)(2,1)}, bf16[512,1792]{1,0:T(8,128)(2,1)S(1)}, u32[]{:S(2)}) copy-start(bf16[512,1792]{1,0:T(8,128)(2,1)S(1)} %collective-permute-done.8.refs_4_) | copy-start | bytes 5505028
  42.5 18.6 %collective-permute-start.6 = (bf16[4,32,1792]{2,1,0:T(8,128)(2,1)S(1)}, bf16[4,32,1792]{2,1,0:T(8,128)(2,1)S(1)}, u32[]{:S(2)}, u32[]{:S(2)}) collective-permute-start(bf16[4,32,1792]{2,1,0:T(8,128)(2,1)S(1)} %collective-permute-done.5.refs_3_), channel_id=1, source_target_pairs={{0,24},{1,7},{2,26},{3,1},{4,28},{5,3},{6,30},{7,5},{8,0},{9,15},{... | collective-permute-start | bytes 1376264 | tf_op jit(solution)/shard_map/ppermute | solution.py:402
  45.3 1.2 copy-start.16
  50.8 10.3 %copy-start = (bf16[512,1792]{1,0:T(8,128)(2,1)}, bf16[512,1792]{1,0:T(8,128)(2,1)S(1)}, u32[]{:S(2)}) copy-start(bf16[512,1792]{1,0:T(8,128)(2,1)S(1)} %get-tuple-element.38.refs_3_.refs_5_.refs_1_) | copy-start | bytes 5505028
  50.8 10.3 %copy-start.2 = (bf16[512,1792]{1,0:T(8,128)(2,1)}, bf16[512,1792]{1,0:T(8,128)(2,1)S(1)}, u32[]{:S(2)}) copy-start(bf16[512,1792]{1,0:T(8,128)(2,1)S(1)} %get-tuple-element.40.refs_5_.refs_7_.refs_2_) | copy-start | bytes 5505028
  50.8 10.3 %copy-start.4 = (bf16[512,1792]{1,0:T(8,128)(2,1)}, bf16[512,1792]{1,0:T(8,128)(2,1)S(1)}, u32[]{:S(2)}) copy-start(bf16[512,1792]{1,0:T(8,128)(2,1)S(1)} %get-tuple-element.41.refs_6_.refs_8_.refs_3_) | copy-start | bytes 5505028
  65.7 13.0 %all-to-all-start.1 = ((bf16[4,128,768]{2,1,0:T(8,128)(2,1)}), bf16[4,128,768]{2,1,0:T(8,128)(2,1)S(1)}, u32[]{:S(2)}, u32[]{:S(2)}) async-start(bf16[4,128,768]{2,1,0:T(8,128)(2,1)} %get-tuple-element.51), calls=%async_computation.1 | async-start | bytes 1572864 | tf_op jit(solution)/shard_map/all_to_all | solution.py:436
  78.7 0.9 copy-start.6
  79.6 17.2 %copy-start.13 = (bf16[4,128,1792]{2,1,0:T(8,128)(2,1)S(1)}, bf16[4,128,1792]{2,1,0:T(8,128)(2,1)}, u32[]{:S(2)}) copy-start(bf16[4,128,1792]{2,1,0:T(8,128)(2,1)} %get-tuple-element.63) | copy-start | bytes 5505028
  95.2 0.8 copy-start.8
  96.0 0.8 copy-start.10
  96.8 2.4 %copy-start.11 = (bf16[4,128,1792]{2,1,0:T(8,128)(2,1)S(1)}, bf16[4,128,1792]{2,1,0:T(8,128)(2,1)}, u32[]{:S(2)}) copy-start(bf16[4,128,1792]{2,1,0:T(8,128)(2,1)} %get-tuple-element.58) | copy-start | bytes 5505028
  99.2 21.7 %collective-permute-start.14 = (bf16[512,1792]{1,0:T(8,128)(2,1)}, bf16[512,1792]{1,0:T(8,128)(2,1)}, u32[]{:S(2)}, u32[]{:S(2)}) collective-permute-start(bf16[512,1792]{1,0:T(8,128)(2,1)} %convolution_convert_fusion), channel_id=1, source_target_pairs={{0,1},{1,0},{2,3},{3,2},{4,5},{5,4},{6,7},{7,6},{8,9},{9,8},{10,11... | collective-permute-start | bytes 5505032 | tf_op jit(solution)/shard_map/ppermute | solution.py:406
  101.5 24.1 %collective-permute-start.13 = (bf16[512,1792]{1,0:T(8,128)(2,1)}, bf16[512,1792]{1,0:T(8,128)(2,1)}, u32[]{:S(2)}, u32[]{:S(2)}) collective-permute-start(bf16[512,1792]{1,0:T(8,128)(2,1)} %convolution_convert_fusion.1), channel_id=1, source_target_pairs={{0,1},{1,0},{2,3},{3,2},{4,5},{5,4},{6,7},{7,6},{8,9},{9,8},{10,11... | collective-permute-start | bytes 5505032 | tf_op jit(solution)/shard_map/ppermute | solution.py:406
  102.0 2.4 %copy-start.7 = (bf16[4,128,128]{2,1,0:T(8,128)(2,1)S(1)}, bf16[4,128,128]{2,1,0:T(8,128)(2,1)}, u32[]{:S(2)}) copy-start(bf16[4,128,128]{2,1,0:T(8,128)(2,1)} %get-tuple-element.52.meta_ref) | copy-start | bytes 393220
  104.5 25.1 %collective-permute-start.12 = (bf16[512,1792]{1,0:T(8,128)(2,1)}, bf16[512,1792]{1,0:T(8,128)(2,1)}, u32[]{:S(2)}, u32[]{:S(2)}) collective-permute-start(bf16[512,1792]{1,0:T(8,128)(2,1)} %convolution_convert_fusion.2), channel_id=1, source_target_pairs={{0,1},{1,0},{2,3},{3,2},{4,5},{5,4},{6,7},{7,6},{8,9},{9,8},{10,11... | collective-permute-start | bytes 5505032 | tf_op jit(solution)/shard_map/ppermute | solution.py:406
  104.5 1.5 copy-start.1
  106.0 1.5 copy-start.3
  107.5 1.5 copy-start.5
  114.5 36.1 %all-to-all-start.3 = ((bf16[64,8,1920]{2,1,0:T(8,128)(2,1)}), bf16[64,8,1920]{2,1,0:T(8,128)(2,1)S(1)}, u32[]{:S(2)}, u32[]{:S(2)}) async-start(bf16[64,8,1920]{2,1,0:T(8,128)(2,1)} %bitcast.28), calls=%async_computation.3 | async-start | bytes 3932160 | tf_op jit(solution)/shard_map/all_to_all | solution.py:440
  120.9 4.8 %copy-start.9 = (bf16[512,512]{1,0:T(8,128)(2,1)S(1)}, bf16[512,512]{1,0:T(8,128)(2,1)}, u32[]{:S(2)}) copy-start(bf16[512,512]{1,0:T(8,128)(2,1)} %copy-done.8) | copy-start | bytes 1572868
  120.9 4.8 %copy-start.12 = (bf16[4,128,1792]{2,1,0:T(8,128)(2,1)S(1)}, bf16[4,128,1792]{2,1,0:T(8,128)(2,1)}, u32[]{:S(2)}) copy-start(bf16[4,128,1792]{2,1,0:T(8,128)(2,1)} %get-tuple-element.58) | copy-start | bytes 5505028

commit v2 on v1

--- a/solution.py
+++ b/solution.py
@@ -47,7 +47,7 @@
     return ref[...].reshape(lead * rows, width)
 
 
-def pack(tok_ref, cot_ref, route_ref, gates_ref, out_ref):
+def pack(plane_ref, z_ref, chip_ref, core_ref, tok_ref, cot_ref, route_ref, gates_ref, out_ref):
     rows, full = tok_ref.shape
     width = full // SIDE
     lap = width + LANES
@@ -68,18 +68,21 @@
         out_ref[j, :, lap:] = cot_ref[:, j * width:(j + 1) * width]
 
 
-def pack_call(tokens, cotangent, routing, gates, width):
+def pack_call(spot, tokens, cotangent, routing, gates, width):
     args = (tokens, cotangent, routing.T, gates.T)
     rows = tokens.shape[0]
     out = pltpu.HBM((SIDE, rows, 2 * width + LANES), BF)
     return pl.pallas_call(
         pack,
-        grid=(1,),
-        in_specs=[pl.BlockSpec(a.shape, lambda i: (0, 0)) for a in args],
-        out_specs=pl.BlockSpec(out.shape, lambda i: (0, 0, 0)),
+        grid_spec=pltpu.PrefetchScalarGridSpec(
+            num_scalar_prefetch=4,
+            grid=(1,),
+            in_specs=[pl.BlockSpec(a.shape, lambda i, *s: (0, 0)) for a in args],
+            out_specs=pl.BlockSpec(out.shape, lambda i, *s: (0, 0, 0)),
+        ),
         out_shape=out,
         compiler_params=params(8),
-    )(*map(far_off, args))
+    )(*spot, *map(far_off, args))
 
 
 def load(*refs):
@@ -126,9 +129,9 @@
 
 
 def pre_acts(count, first, width):
-    def body(*refs):
+    def body(plane_ref, *refs):
         x_refs, y_refs, mats = refs[:count], refs[count:2 * count], refs[2 * count:2 * count + 6]
-        out_ref, x_out, y_out, meta_out, sems = refs[-5:]
+        *outs, x_out, y_out, meta_out, val_ref, sems, out_sems = refs[-10:]
         lead, short_rows = x_refs[0].shape[0], x_refs[0].shape[1]
         copies = []
         for n in range(count):
@@ -161,39 +164,51 @@
             for n in range(count):
                 part = val[n * lead * short_rows:(n + 1) * lead * short_rows]
                 part = part.reshape(lead, short_rows, LANES)
-                out_ref[:, n * short_rows:(n + 1) * short_rows, m * LANES:(m + 1) * LANES] = part
+                val_ref[:, n * short_rows:(n + 1) * short_rows, m * LANES:(m + 1) * LANES] = part
+        for k in range(lead):
+            copy = pltpu.make_async_copy(
+                val_ref.at[(plane_ref[0] + k) & 3],
+                outs[k].at[pl.ds(first, count * short_rows), :],
+                out_sems.at[k],
+            )
+            copy.start()
+            copies.append(copy)
         for copy in copies:
             copy.wait()
 
     return body
 
 
-def pre_call(pieces, mats, first, total, into):
+def pre_call(plane, pieces, mats, first, total, into):
     count = len(pieces) // 2
     lead, rows, _ = pieces[0].shape
     width = mats[0].shape[1]
     outer = pl.BlockSpec(memory_space=pl.ANY)
-    outs = [pltpu.HBM((lead, rows * total, w), BF) for w in (6 * LANES, width, width, LANES)]
+    outs = [pltpu.HBM((rows * total, 6 * LANES), BF)] * lead
+    outs = outs + [pltpu.HBM((lead, rows * total, w), BF) for w in (width, width, LANES)]
     taken = len(pieces) + 6
     return pl.pallas_call(
         pre_acts(count, first * rows, width),
-        grid=(1,),
-        in_specs=in_core(taken) + [outer] * len(into),
-        out_specs=[
-            pl.BlockSpec((lead, rows * count, 6 * LANES), lambda i: (0, first // count, 0)),
-            outer,
-            outer,
-            outer,
-        ],
+        grid_spec=pltpu.PrefetchScalarGridSpec(
+            num_scalar_prefetch=1,
+            grid=(1,),
+            in_specs=in_core(taken) + [outer] * len(into),
+            out_specs=[outer] * len(outs),
+            scratch_shapes=[
+                pltpu.VMEM((lead, rows * count, 6 * LANES), BF),
+                pltpu.SemaphoreType.DMA((count, 3)),
+                pltpu.SemaphoreType.DMA((lead,)),
+            ],
+        ),
         out_shape=outs,
-        scratch_shapes=[pltpu.SemaphoreType.DMA((count, 3))],
-        input_output_aliases={taken + n: n for n in range(len(into))},
-        compiler_params=params(12),
-    )(*map(near_core, pieces), *map(near_core, mats), *map(far_off, into))
-
-
-def middle(plane_ref, parts_ref, meta_ref, out_ref, route_ref):
-    rows = parts_ref.shape[1]
+        input_output_aliases={1 + taken + n: n for n in range(len(into))},
+        compiler_params=params(14),
+    )(plane, *map(near_core, pieces), *map(near_core, mats), *map(far_off, into))
+
+
+def middle(plane_ref, *refs):
+    parts, meta_ref, out_ref, route_ref = refs[:SIDE], *refs[SIDE:]
+    rows = out_ref.shape[0]
     meta = meta_ref[...].reshape(rows, LANES).astype(F32)
     low = first_half(rows)
     factor = jnp.where(low, meta[:, 2:3], meta[:, 3:4])
@@ -202,7 +217,7 @@
         vals = []
         for m in range(3):
             at = (3 * side + m) * LANES
-            vals.append(sum(parts_ref[j, :, at:at + LANES].astype(F32) for j in range(SIDE)))
+            vals.append(sum(part[:, at:at + LANES].astype(F32) for part in parts))
         gate, upper, reverse = vals
         sigma = jax.nn.sigmoid(gate)
         act = gate * sigma
@@ -211,9 +226,7 @@
         d_gate = back * upper * sigma * (1.0 + gate * (1.0 - sigma))
         at = 3 * side * LANES
         for n, val in enumerate((d_gate, back * act, factor * hidden)):
-            low_bits = val.astype(BF)
-            for j in range(SIDE):
-                out_ref[j, :, at + n * LANES:at + (n + 1) * LANES] = low_bits
+            out_ref[:, at + n * LANES:at + (n + 1) * LANES] = val.astype(BF)
         prod = prod + hidden * reverse
     term_a = jnp.sum(jnp.where(low, prod, 0.0), axis=1, keepdims=True)
     term_b = jnp.sum(jnp.where(low, 0.0, prod), axis=1, keepdims=True)
@@ -222,27 +235,20 @@
 
 
 def middle_call(plane, parts, meta):
-    _, rows, width = parts.shape
+    rows, width = parts[0].shape
     return pl.pallas_call(
         middle,
         grid_spec=pltpu.PrefetchScalarGridSpec(
             num_scalar_prefetch=1,
             grid=(1,),
-            in_specs=[
-                pl.BlockSpec(memory_space=pltpu.VMEM),
-                pl.BlockSpec((1, rows, LANES), lambda i, s: (s[0], 0, 0)),
-            ],
-            out_specs=[
-                pl.BlockSpec((SIDE, rows, width), lambda i, s: (0, 0, 0)),
-                pl.BlockSpec((rows, LANES), lambda i, s: (0, 0)),
-            ],
+            in_specs=[pl.BlockSpec((rows, width), lambda i, s: (0, 0))]
+            + in_core(SIDE - 1)
+            + [pl.BlockSpec((1, rows, LANES), lambda i, s: (s[0], 0, 0))],
+            out_specs=in_core(2),
         ),
-        out_shape=[
-            pltpu.HBM((SIDE, rows, width), BF),
-            jax.ShapeDtypeStruct((rows, LANES), BF),
-        ],
-        compiler_params=params(16),
-    )(plane, near_core(parts), meta)
+        out_shape=[pltpu.VMEM((rows, width), BF), pltpu.VMEM((rows, LANES), BF)],
+        compiler_params=params(6),
+    )(plane, far_off(parts[0]), *map(near_core, parts[1:]), far_off(meta))
 
 
 def spread(short, route_a, route_b, owner, low):
@@ -267,20 +273,29 @@
     ]
 
 
-def widen(acts_ref, meta_ref, *outs):
-    for out, val in zip(outs, dense(flat(acts_ref).astype(F32), flat(meta_ref).astype(F32), range(6))):
-        out[...] = val
-
-
-def widen_call(acts, meta):
-    lead, rows, _ = acts.shape
+def widen(plane_ref, *refs):
+    acts, meta_ref, outs = refs[:SIDE], refs[SIDE], refs[SIDE + 1:]
+    rows = acts[0].shape[0]
+    for k, ref in enumerate(acts):
+        home = (plane_ref[0] - k) & 3
+        vals = dense(ref[...].astype(F32), meta_ref[home].astype(F32), range(6))
+        for out, val in zip(outs, vals):
+            out[pl.ds(pl.multiple_of(home * rows, rows), rows), :] = val
+
+
+def widen_call(plane, acts, meta):
+    rows = acts[0].shape[0]
     return pl.pallas_call(
         widen,
-        in_specs=in_core(2),
-        out_specs=in_core(6),
-        out_shape=[pltpu.VMEM((lead * rows, COLS), BF)] * 6,
+        grid_spec=pltpu.PrefetchScalarGridSpec(
+            num_scalar_prefetch=1,
+            grid=(1,),
+            in_specs=in_core(SIDE + 1),
+            out_specs=in_core(6),
+        ),
+        out_shape=[pltpu.VMEM((SIDE * rows, COLS), BF)] * 6,
         compiler_params=params(8),
-    )(near_core(acts), near_core(meta))
+    )(plane, *map(near_core, (*acts, meta)))
 
 
 def goals(z, x, core):
@@ -293,9 +308,10 @@
     return spots
 
 
-def terms(plane_ref, z_ref, x_ref, core_ref, acts_ref, meta_ref, route_ref, *refs):
-    mats, sent_ref, wide_ref, out_ref, sort_ref, out_sems = refs[:4], *refs[4:]
-    lead, rows, _ = acts_ref.shape
+def terms(plane_ref, z_ref, x_ref, core_ref, *refs):
+    acts, meta_ref, route_ref, mats = refs[:SIDE], refs[SIDE], refs[SIDE + 1], refs[SIDE + 2:-5]
+    sent_ref, wide_ref, out_ref, sort_ref, out_sems = refs[-5:]
+    lead, rows = SIDE, acts[0].shape[0]
     deep = out_ref.shape[2] - LANES
     chunk = 256
     count = deep // chunk
@@ -304,18 +320,18 @@
         pltpu.make_async_copy(out_ref.at[:, :, cut], sent_ref.at[:, :, cut], out_sems.at[c])
         for c, cut in enumerate(cuts)
     ]
-    acts, meta = flat(acts_ref).astype(F32), flat(meta_ref).astype(F32)
-    route = route_ref[...].astype(F32)
-    width = acts.shape[1]
+    width = acts[0].shape[1]
     spots = goals(z_ref[0], x_ref[0], core_ref[0])
-    for j in range(lead):
-        mine = jnp.where(j == plane_ref[0], 1.0, 0.0)
+    for k in range(lead):
+        home = (plane_ref[0] - k) & 3
+        vals, meta = acts[k][...].astype(F32), meta_ref[home].astype(F32)
+        route = route_ref[...].astype(F32) if k == 0 else jnp.zeros((rows, LANES), F32)
         for b in range(16):
-            at = j * rows + b * 8
-            spot = pl.ds(pl.multiple_of(j * rows + spots[b] * 8, 8), 8)
-            sort_ref[spot, :width] = acts[at:at + 8]
+            at = b * 8
+            spot = pl.ds(pl.multiple_of(home * rows + spots[b] * 8, 8), 8)
+            sort_ref[spot, :width] = vals[at:at + 8]
             sort_ref[spot, width:width + LANES] = meta[at:at + 8]
-            sort_ref[spot, width + LANES:] = route[b * 8:b * 8 + 8] * mine
+            sort_ref[spot, width + LANES:] = route[at:at + 8]
     moved = sort_ref[:, :width], sort_ref[:, width:width + LANES]
     for n, val in enumerate(dense(*moved, (0, 1, 3, 4))):
         wide_ref[:, n * COLS:(n + 1) * COLS] = val
@@ -331,7 +347,7 @@
 
 
 def terms_call(spots, acts, meta, route, mats):
-    lead, rows, _ = acts.shape
+    lead, rows = SIDE, acts[0].shape[0]
     deep = mats[0].shape[1]
     out = (lead, rows, deep + LANES)
     chunk = 256
@@ -341,7 +357,7 @@
         grid_spec=pltpu.PrefetchScalarGridSpec(
             num_scalar_prefetch=4,
             grid=(1,),
-            in_specs=in_core(7),
+            in_specs=in_core(SIDE + 6),
             out_specs=outer,
             scratch_shapes=[
                 pltpu.VMEM((lead * rows, 4 * COLS), BF),
@@ -352,7 +368,7 @@
         ),
         out_shape=pltpu.HBM(out, BF),
         compiler_params=params(16),
-    )(*spots, *map(near_core, (acts, meta, route, *mats)))
+    )(*spots, *map(near_core, (*acts, meta, route, *mats)))
 
 
 def finish(parts_ref, token_ref, route_ref):
@@ -402,6 +418,10 @@
     return lax.ppermute(arr, PLANE, pairs)
 
 
+def turn(arr, by):
+    return lax.ppermute(arr, "ep", [(i, (i + by) % SIDE) for i in range(SIDE)])
+
+
 def swap(arr):
     return lax.ppermute(arr, "core", [(0, 1), (1, 0)])
 
@@ -416,7 +436,10 @@
     own_mats = [w.reshape(COLS, width) for w in (gate_weight, up_weight, down_weight)]
     their_mats = [swap(w) for w in own_mats]
     mats = load_call(own_mats + their_mats)
-    send = pack_call(tokens, cotangent, routing, route_gates, width)
+    plane, *spot = (
+        lax.axis_index(a).astype(jnp.int32).reshape(1) for a in ("ep",) + PLANE
+    )
+    send = pack_call((plane, *spot), tokens, cotangent, routing, route_gates, width)
     own = lax.all_to_all(send, "ep", 0, 0, tiled=True)
     near = [own] + [shift(own, 0, s) for s in range(1, SIDE)]
     lap = width + LANES
@@ -427,18 +450,16 @@
     y_1 = shift(y_0, 1, 1)
     x_2 = shift(x_1, 1, 1)
     y_2 = shift(y_3, 1, 3)
-    plane, *spot = (
-        lax.axis_index(a).astype(jnp.int32).reshape(1) for a in ("ep",) + PLANE
-    )
-    state = pre_call([x_0, y_0], mats, 2, SIDE, [])
-    state = pre_call([x_1, x_3, y_1, y_3], mats, 0, SIDE, state)
-    pre, x_rows, y_rows, meta_rows = pre_call([x_2, y_2], mats, 3, SIDE, state)
-    parts = lax.all_to_all(pre, "ep", 0, 0, tiled=True)
+    state = pre_call(plane, [x_0, y_0], mats, 2, SIDE, [])
+    state = pre_call(plane, [x_1, x_3, y_1, y_3], mats, 0, SIDE, state)
+    *parts, x_rows, y_rows, meta_rows = pre_call(plane, [x_2, y_2], mats, 3, SIDE, state)
+    parts = [parts[0]] + [turn(parts[k], k) for k in range(1, SIDE)]
     done, route = middle_call(plane, parts, meta_rows)
-    acts = lax.all_to_all(done, "ep", 0, 0, tiled=True)
-    sent = terms_call((plane, *spot), acts, meta_rows, route, mats[:2] + mats[3:5])
+    acts = [done] + [turn(done, k) for k in range(1, SIDE)]
+    pair_mats = load_call(own_mats[:2] + their_mats[:2])
+    sent = terms_call((plane, *spot), acts, meta_rows, route, pair_mats)
     got = lax.all_to_all(sent.reshape(-1, tok_rows, lap), TORUS, 0, 0, tiled=True)
-    wides = widen_call(acts, meta_rows)
+    wides = widen_call(plane, acts, meta_rows)
     token_grad, route_sum = finish_call(got, width)
     route_grad = route_sum.T
     x_rows, y_rows = (r.reshape(-1, width) for r in (x_rows, y_rows))

time: 152 us -> 149 us (0.980)
  blocking collectives: 24.5 us -> 11.6 us
  starting transfers between devices: 27.9 us -> 36.2 us
  local copies, waits for them, and re-layouts: 8.29 us -> 0.93 us
  waiting for transfers between devices: 42 us -> 46.8 us
  Pallas kernels: 28.3 us -> 31.5 us
    all_to_all x1 -> x0, blocking collectives: 12.9 us -> none  [local(): acts = lax.all_to_all(done, 'ep', 0, 0, tiled=True)]
    ppermute x0 -> x6, waiting for transfers between devices: none -> 12.7 us  [turn(): return lax.ppermute(arr, 'ep', [(i, (i + by) % SIDE) for i in range(SIDE)])]
    all_to_all x1 -> x0, waiting for transfers between devices: 9.27 us -> none  [local(): parts = lax.all_to_all(pre, 'ep', 0, 0, tiled=True)]
    ppermute x0 -> x6, starting transfers between devices: none -> 7.68 us  [turn(): return lax.ppermute(arr, 'ep', [(i, (i + by) % SIDE) for i in range(SIDE)])]
    unnamed x34 -> x10, local copies, waits for them, and re-layouts: 8.29 us -> 0.93 us
    all_to_all x1, starting transfers between devices: 6.37 us -> 10.6 us  [local(): lax.all_to_all(sent.reshape(-1, tok_rows, lap), TORUS, 0, 0, tiled=True)]
    all_to_all x1 -> x0, starting transfers between devices: 3.69 us -> none  [local(): parts = lax.all_to_all(pre, 'ep', 0, 0, tiled=True)]
    pallas_call x1 -> x2, Pallas kernels: 4.25 us -> 7.46 us  [load_call(): pl.pallas_call(load, in_specs=[pl.BlockSpec(memory_space=pl.ANY)] * len(m...]
  transfers between devices with their start and end apart: 17 -> 22, of which waited for: 7 -> 11; matrix products, arithmetic and copies ran while one was open for 11% -> 11% of each run, Pallas kernels for 13% -> 16%
where the time goes in v2:
time: 149 us
  waiting for transfers between devices  46.8 us (31%)
  starting transfers between devices  36.2 us (24%)
  Pallas kernels  31.5 us (21%)
  matrix products  21.1 us (14%)
  blocking collectives  11.6 us (8%)
    dot_general x6, matrix products, contract_rows(): lax.dot_general(left, right, (((0,), (0,)), ((), ())), preferred_element_...  21.1 us
    all_to_all x1, waiting for transfers between devices, local(): lax.all_to_all(sent.reshape(-1, tok_rows, lap), TORUS, 0, 0, tiled=True)  17.3 us
    ppermute x9, waiting for transfers between devices, shift(): return lax.ppermute(arr, PLANE, pairs)  16.8 us
    ppermute x9, starting transfers between devices, shift(): return lax.ppermute(arr, PLANE, pairs)  16.7 us
    pallas_call x3, Pallas kernels, pre_call(): pl.pallas_call(pre_acts(count, first * rows, width), grid_spec=pltpu.Pref...  13.3 us
    ppermute x6, waiting for transfers between devices, turn(): return lax.ppermute(arr, 'ep', [(i, (i + by) % SIDE) for i in range(SIDE)])  12.7 us
    all_to_all x1, blocking collectives, local(): own = lax.all_to_all(send, 'ep', 0, 0, tiled=True)  11.6 us
    all_to_all x1, starting transfers between devices, local(): lax.all_to_all(sent.reshape(-1, tok_rows, lap), TORUS, 0, 0, tiled=True)  10.6 us
  transfers between devices with their start and end apart: 22, of which 11 were waited for; matrix products, arithmetic and copies ran while one was open for 11% of the time, Pallas kernels for 16%

profile of v2, /device:TPU:0, one launch (start us, length us, event | category | flops | bytes accessed | tf_op | source)
XLA Modules:
  0.0 149.0 jit_solution(13924797844831979314)
XLA Ops:
  0.6 0.1 collective-permute-start.7
  0.7 0.5 collective-permute-start.8
  1.2 0.1 collective-permute-start.9
  1.3 1.7 %shard_map.110 = bf16[4,8,3712]{2,1,0:T(8,128)(2,1)} custom-call(s32[1]{0:T(128)} %bitcast.plane_ref, s32[1]{0:T(128)} %bitcast.1.z_ref, s32[1]{0:T(128)} %bitcast.2.chip_ref.x_ref, s32[1]{0:T(128)} %bitcast.3.core_ref, bf16[8,7168]{1,0:T(8,128)(2,1)} %tok_ref.1, bf16[8,7168]{1,0:T(8,128)(2,1)} %cot_ref.1, s32[2,8]{1,0:T(2,128)} %bitcast.43, ...), custom_call_target="tpu_custom_call" | custom-call | tf_op jit(solution)/shard_map/pallas_call | solution.py:75
  3.0 11.6 %all_to_all.10.refs_0_ = bf16[4,8,3712]{2,1,0:T(8,128)(2,1)S(1)} all-to-all(bf16[4,8,3712]{2,1,0:T(8,128)(2,1)} %shard_map.110), channel_id=1, replica_groups=mesh['ep'=4,'z'=4,'x'=4,'core'=2] {'ep'}, dimensions={0} | all-to-all | bytes 475136 | tf_op jit(solution)/shard_map/all_to_all | solution.py:443
  14.6 1.5 %collective-permute-start = (bf16[4,8,3712]{2,1,0:T(8,128)(2,1)S(1)}, bf16[4,8,3712]{2,1,0:T(8,128)(2,1)S(1)}, u32[]{:S(2)}, u32[]{:S(2)}) collective-permute-start(bf16[4,8,3712]{2,1,0:T(8,128)(2,1)S(1)} %all_to_all.10.refs_0_), channel_id=1, source_target_pairs={{0,2},{1,9},{2,4},{3,11},{4,6},{5,13},{6,0},{7,15},{8,10},{9,17},{... | collective-permute-start | bytes 712712 | tf_op jit(solution)/shard_map/ppermute | solution.py:418
  16.1 2.7 %collective-permute-start.1 = (bf16[4,8,3712]{2,1,0:T(8,128)(2,1)S(1)}, bf16[4,8,3712]{2,1,0:T(8,128)(2,1)S(1)}, u32[]{:S(2)}, u32[]{:S(2)}) collective-permute-start(bf16[4,8,3712]{2,1,0:T(8,128)(2,1)S(1)} %all_to_all.10.refs_0_), channel_id=1, source_target_pairs={{0,4},{1,17},{2,6},{3,19},{4,0},{5,21},{6,2},{7,23},{8,12},{9,25},... | collective-permute-start | bytes 712712 | tf_op jit(solution)/shard_map/ppermute | solution.py:418
  18.8 3.1 %collective-permute-done.refs_1_ = bf16[4,8,3712]{2,1,0:T(8,128)(2,1)S(1)} collective-permute-done((bf16[4,8,3712]{2,1,0:T(8,128)(2,1)S(1)}, bf16[4,8,3712]{2,1,0:T(8,128)(2,1)S(1)}, u32[]{:S(2)}, u32[]{:S(2)}) %collective-permute-start) | collective-permute-done | bytes 237600 | tf_op jit(solution)/shard_map/ppermute | solution.py:418
  21.9 1.5 %collective-permute-start.2 = (bf16[4,8,3712]{2,1,0:T(8,128)(2,1)S(1)}, bf16[4,8,3712]{2,1,0:T(8,128)(2,1)S(1)}, u32[]{:S(2)}, u32[]{:S(2)}) collective-permute-start(bf16[4,8,3712]{2,1,0:T(8,128)(2,1)S(1)} %all_to_all.10.refs_0_), channel_id=1, source_target_pairs={{0,6},{1,25},{2,0},{3,27},{4,2},{5,29},{6,4},{7,31},{8,14},{9,1},{... | collective-permute-start | bytes 712712 | tf_op jit(solution)/shard_map/ppermute | solution.py:418
  23.5 2.0 %collective-permute-done.1.refs_2_ = bf16[4,8,3712]{2,1,0:T(8,128)(2,1)S(1)} collective-permute-done((bf16[4,8,3712]{2,1,0:T(8,128)(2,1)S(1)}, bf16[4,8,3712]{2,1,0:T(8,128)(2,1)S(1)}, u32[]{:S(2)}, u32[]{:S(2)}) %collective-permute-start.1) | collective-permute-done | bytes 237600 | tf_op jit(solution)/shard_map/ppermute | solution.py:418
  25.5 2.6 %collective-permute-done.2.refs_3_ = bf16[4,8,3712]{2,1,0:T(8,128)(2,1)S(1)} collective-permute-done((bf16[4,8,3712]{2,1,0:T(8,128)(2,1)S(1)}, bf16[4,8,3712]{2,1,0:T(8,128)(2,1)S(1)}, u32[]{:S(2)}, u32[]{:S(2)}) %collective-permute-start.2) | collective-permute-done | bytes 237600 | tf_op jit(solution)/shard_map/ppermute | solution.py:418
  28.0 0.1 shard_map.111
  28.1 2.0 %collective-permute-start.3 = (bf16[4,32,1920]{2,1,0:T(8,128)(2,1)S(1)}, bf16[4,32,1920]{2,1,0:T(8,128)(2,1)S(1)}, u32[]{:S(2)}, u32[]{:S(2)}) collective-permute-start(bf16[4,32,1920]{2,1,0:T(8,128)(2,1)S(1)} %get-tuple-element.48.refs_0_), channel_id=1, source_target_pairs={{0,8},{1,3},{2,10},{3,5},{4,12},{5,7},{6,14},{7,1},{8,16},{9,11},{... | collective-permute-start | bytes 1474568 | tf_op jit(solution)/shard_map/ppermute | solution.py:418
  30.1 2.2 %collective-permute-start.5 = (bf16[4,32,1792]{2,1,0:T(8,128)(2,1)S(1)}, bf16[4,32,1792]{2,1,0:T(8,128)(2,1)S(1)}, u32[]{:S(2)}, u32[]{:S(2)}) collective-permute-start(bf16[4,32,1792]{2,1,0:T(8,128)(2,1)S(1)} %get-tuple-element.49.refs_1_), channel_id=1, source_target_pairs={{0,24},{1,7},{2,26},{3,1},{4,28},{5,3},{6,30},{7,5},{8,0},{9,15},{... | collective-permute-start | bytes 1376264 | tf_op jit(solution)/shard_map/ppermute | solution.py:418
  32.3 6.3 %collective-permute-done.5.refs_3_ = bf16[4,32,1792]{2,1,0:T(8,128)(2,1)S(1)} collective-permute-done((bf16[4,32,1792]{2,1,0:T(8,128)(2,1)S(1)}, bf16[4,32,1792]{2,1,0:T(8,128)(2,1)S(1)}, u32[]{:S(2)}, u32[]{:S(2)}) %collective-permute-start.5) | collective-permute-done | bytes 458784 | tf_op jit(solution)/shard_map/ppermute | solution.py:418
  38.6 3.4 %collective-permute-start.10 = (bf16[4,32,1920]{2,1,0:T(8,128)(2,1)S(1)}, bf16[4,32,1920]{2,1,0:T(8,128)(2,1)S(1)}, u32[]{:S(2)}, u32[]{:S(2)}) collective-permute-start(bf16[4,32,1920]{2,1,0:T(8,128)(2,1)S(1)} %get-tuple-element.48.refs_0_), channel_id=1, source_target_pairs={{0,24},{1,7},{2,26},{3,1},{4,28},{5,3},{6,30},{7,5},{8,0},{9,15},{... | collective-permute-start | bytes 1474568 | tf_op jit(solution)/shard_map/ppermute | solution.py:418
  42.0 0.0 collective-permute-done.3.refs_0_
  42.0 0.0 collective-permute-start.4
  42.0 0.0 collective-permute-done.7.refs_3_.refs_2_
  42.0 0.0 copy-start.4
  42.0 0.5 collective-permute-start.11
  42.5 0.0 collective-permute-done.8.refs_4_.refs_3_
  42.5 2.8 %collective-permute-start.6 = (bf16[4,32,1792]{2,1,0:T(8,128)(2,1)S(1)}, bf16[4,32,1792]{2,1,0:T(8,128)(2,1)S(1)}, u32[]{:S(2)}, u32[]{:S(2)}) collective-permute-start(bf16[4,32,1792]{2,1,0:T(8,128)(2,1)S(1)} %collective-permute-done.5.refs_3_), channel_id=1, source_target_pairs={{0,24},{1,7},{2,26},{3,1},{4,28},{5,3},{6,30},{7,5},{8,0},{9,15},{... | collective-permute-start | bytes 1376264 | tf_op jit(solution)/shard_map/ppermute | solution.py:418
  45.3 0.0 collective-permute-done.9.refs_5_
  45.3 4.2 %shard_map.112 = (bf16[512,1792]{1,0:T(8,128)(2,1)S(1)}, bf16[512,1792]{1,0:T(8,128)(2,1)S(1)}, bf16[512,1792]{1,0:T(8,128)(2,1)S(1)}, bf16[512,1792]{1,0:T(8,12...) custom-call(bf16[512,1792]{1,0:T(8,128)(2,1)} %bitcast.36, bf16[512,1792]{1,0:T(8,128)(2,1)} %bitcast.39, ...), custom_call_target="tpu_custom_call" | custom-call | tf_op jit(solution)/shard_map/pallas_call | solution.py:99
  49.6 4.5 %shard_map.113 = (bf16[128,768]{1,0:T(8,128)(2,1)}, bf16[128,768]{1,0:T(8,128)(2,1)}, bf16[128,768]{1,0:T(8,128)(2,1)}, bf16[128,768]{1,0:T(8,128)(2,1)}, bf16[4...) custom-call(s32[1]{0:T(128)} %bitcast.plane_ref, ...), custom_call_target="tpu_custom_call" | custom-call | tf_op jit(solution)/shard_map/pallas_call | solution.py:190
  54.1 2.8 %collective-permute-done.11.refs_2_ = bf16[4,32,1792]{2,1,0:T(8,128)(2,1)S(1)} collective-permute-done((bf16[4,32,1792]{2,1,0:T(8,128)(2,1)S(1)}, bf16[4,32,1792]{2,1,0:T(8,128)(2,1)S(1)}, u32[]{:S(2)}, u32[]{:S(2)}) %collective-permute-start.11) | collective-permute-done | bytes 458784 | tf_op jit(solution)/shard_map/ppermute | solution.py:418
  56.9 0.0 collective-permute-done.10.refs_1_
  56.9 4.2 %shard_map.114 = (bf16[128,768]{1,0:T(8,128)(2,1)}, bf16[128,768]{1,0:T(8,128)(2,1)}, bf16[128,768]{1,0:T(8,128)(2,1)}, bf16[128,768]{1,0:T(8,128)(2,1)}, bf16[4...) custom-call(s32[1]{0:T(128)} %bitcast.plane_ref, ...), custom_call_target="tpu_custom_call", output_to_operand_aliasing={{0}: (11, {}), {1}: (12, {}), {2}: (13, {}), {3}: (14, {}),... | custom-call | tf_op jit(solution)/shard_map/pallas_call | solution.py:190
  61.2 0.0 collective-permute-done.6.refs_1_
  61.2 4.6 %shard_map.115 = (bf16[128,768]{1,0:T(8,128)(2,1)}, bf16[128,768]{1,0:T(8,128)(2,1)}, bf16[128,768]{1,0:T(8,128)(2,1)}, bf16[128,768]{1,0:T(8,128)(2,1)}, bf16[4...) custom-call(s32[1]{0:T(128)} %bitcast.plane_ref, ...), custom_call_target="tpu_custom_call", output_to_operand_aliasing={{0}: (9, {}), {1}: (10, {}), {2}: (11, {}), {3}: (12, {}), ... | custom-call | tf_op jit(solution)/shard_map/pallas_call | solution.py:190
  65.7 0.6 collective-permute-start.12
  66.4 2.1 %collective-permute-start.13 = (bf16[128,768]{1,0:T(8,128)(2,1)}, bf16[128,768]{1,0:T(8,128)(2,1)S(1)}, u32[]{:S(2)}, u32[]{:S(2)}) collective-permute-start(bf16[128,768]{1,0:T(8,128)(2,1)} %get-tuple-element.72), channel_id=1, source_target_pairs={{0,64},{32,96},{64,0},{96,32},{1,65},{33,97},{65,1},{97,33},{2,66}... | collective-permute-start | bytes 589832 | tf_op jit(solution)/shard_map/ppermute | solution.py:422
  68.4 0.9 collective-permute-start.14
  69.3 5.7 %collective-permute-done.12.refs_1_ = bf16[128,768]{1,0:T(8,128)(2,1)S(1)} collective-permute-done((bf16[128,768]{1,0:T(8,128)(2,1)}, bf16[128,768]{1,0:T(8,128)(2,1)S(1)}, u32[]{:S(2)}, u32[]{:S(2)}) %collective-permute-start.12) | collective-permute-done | bytes 196640 | tf_op jit(solution)/shard_map/ppermute | solution.py:422
  75.0 0.0 collective-permute-done.13.refs_2_
  75.0 1.2 collective-permute-done.14.refs_3_
  76.2 1.2 shard_map.116
  77.4 0.1 collective-permute-start.15
  77.5 4.0 %collective-permute-start.16 = (bf16[128,768]{1,0:T(8,128)(2,1)S(1)}, bf16[128,768]{1,0:T(8,128)(2,1)S(1)}, u32[]{:S(2)}, u32[]{:S(2)}) collective-permute-start(bf16[128,768]{1,0:T(8,128)(2,1)S(1)} %get-tuple-element.75.refs_0_), channel_id=1, source_target_pairs={{0,64},{32,96},{64,0},{96,32},{1,65},{33,97},{65,1},{97,33},{2,66}... | collective-permute-start | bytes 589832 | tf_op jit(solution)/shard_map/ppermute | solution.py:422
  81.5 0.0 collective-permute-start.17
  81.5 2.9 %collective-permute-done.15.refs_1_ = bf16[128,768]{1,0:T(8,128)(2,1)S(1)} collective-permute-done((bf16[128,768]{1,0:T(8,128)(2,1)S(1)}, bf16[128,768]{1,0:T(8,128)(2,1)S(1)}, u32[]{:S(2)}, u32[]{:S(2)}) %collective-permute-start.15) | collective-permute-done | bytes 196640 | tf_op jit(solution)/shard_map/ppermute | solution.py:422
  84.3 2.9 %collective-permute-done.16.refs_2_ = bf16[128,768]{1,0:T(8,128)(2,1)S(1)} collective-permute-done((bf16[128,768]{1,0:T(8,128)(2,1)S(1)}, bf16[128,768]{1,0:T(8,128)(2,1)S(1)}, u32[]{:S(2)}, u32[]{:S(2)}) %collective-permute-start.16) | collective-permute-done | bytes 196640 | tf_op jit(solution)/shard_map/ppermute | solution.py:422
  87.2 0.1 collective-permute-done.17.refs_3_
  87.3 0.9 copy-done
  88.2 1.3 shard_map.120
  89.6 0.0 copy-start.2
  89.6 4.0 %convolution_convert_fusion = bf16[512,1792]{1,0:T(8,128)(2,1)} fusion(bf16[512,512]{1,0:T(8,128)(2,1)S(1)} %get-tuple-element.90, bf16[512,1792]{1,0:T(8,128)(2,1)} %bitcast.33), kind=kOutput, calls=%fused_computation.3 | convolution fusion | flops 940441600 | bytes 4194304 | tf_op jit(solution)/shard_map/dot_general | solution.py:430
  93.6 0.0 collective-permute-start.20
  93.6 2.4 %convolution_convert_fusion.1 = bf16[512,1792]{1,0:T(8,128)(2,1)} fusion(bf16[512,512]{1,0:T(8,128)(2,1)S(1)} %get-tuple-element.87, bf16[512,1792]{1,0:T(8,128)(2,1)S(1)} %bitcast.29), kind=kOutput, calls=%fused_computation.4 | convolution fusion | flops 940441600 | bytes 4194304 | tf_op jit(solution)/shard_map/dot_general | solution.py:430
  96.0 0.5 collective-permute-start.19
  96.5 2.4 %convolution_convert_fusion.2 = bf16[512,1792]{1,0:T(8,128)(2,1)} fusion(bf16[512,512]{1,0:T(8,128)(2,1)S(1)} %get-tuple-element.85, bf16[512,1792]{1,0:T(8,128)(2,1)S(1)} %bitcast.30), kind=kOutput, calls=%fused_computation.5 | convolution fusion | flops 940441600 | bytes 4194304 | tf_op jit(solution)/shard_map/dot_general | solution.py:430
  98.9 0.0 collective-permute-start.18
  98.9 3.2 %shard_map.117 = (bf16[512,1792]{1,0:T(8,128)(2,1)S(1)}, bf16[512,1792]{1,0:T(8,128)(2,1)S(1)}, bf16[512,1792]{1,0:T(8,128)(2,1)S(1)}, bf16[512,1792]{1,0:T(8,128)(2,1)S(1)}) custom-call(bf16[512,1792]{1,0:T(8,128)(2,1)} %bitcast.37, bf16[512,1792]{1,0:T(8,128)(2,1)} %bitcast.40, bf16[512,1792]{1,0:T(8,128)(2,1)} %copy-done.4, ...), custom_call_target="tpu_custom_call" | custom-call | tf_op jit(solution)/shard_map/pallas_call | solution.py:99
  102.1 5.6 %shard_map.118 = bf16[4,128,1920]{2,1,0:T(8,128)(2,1)} custom-call(s32[1]{0:T(128)} %bitcast.plane_ref, s32[1]{0:T(128)} %bitcast.1.z_ref, s32[1]{0:T(128)} %bitcast.2.chip_ref.x_ref, s32[1]{0:T(128)} %bitcast.3.core_ref, bf16[128,768]{1,0:T(8,128)(2,1)S(1)} %get-tuple-element.75.refs_0_, bf16[128,768]{1,0:T(8,128)(2,1)S(1)} %collective-permute-done.15.refs_1_, ...), custom_call_target="tpu_custom_call" | custom-call | tf_op jit(solution)/shard_map/pallas_call | solution.py:355
  107.7 10.6 %all-to-all-start.1 = ((bf16[64,8,1920]{2,1,0:T(8,128)(2,1)}), bf16[64,8,1920]{2,1,0:T(8,128)(2,1)S(1)}, u32[]{:S(2)}, u32[]{:S(2)}) async-start(bf16[64,8,1920]{2,1,0:T(8,128)(2,1)} %bitcast.28), calls=%async_computation.1 | async-start | bytes 3932160 | tf_op jit(solution)/shard_map/all_to_all | solution.py:461
  118.3 0.0 collective-permute-done.20
  118.3 0.0 copy-start.3
  118.3 4.6 %add_convert_fusion = bf16[512,1792]{1,0:T(8,128)(2,1)} fusion(bf16[512,1792]{1,0:T(8,128)(2,1)} %collective-permute-done.20, bf16[512,512]{1,0:T(8,128)(2,1)S(1)} %get-tuple-element.88, bf16[512,1792]{1,0:T(8,128)(2,1)} %bitcast.34), kind=kOutput, calls=%fused_computation | convolution fusion | flops 942276608 | bytes 6029312 | tf_op jit(solution)/shard_map/dot_general | solution.py:430
  122.9 0.0 collective-permute-done.19
  122.9 3.9 %add_convert_fusion.1 = bf16[512,1792]{1,0:T(8,128)(2,1)} fusion(bf16[512,1792]{1,0:T(8,128)(2,1)} %collective-permute-done.19, bf16[512,512]{1,0:T(8,128)(2,1)S(1)} %get-tuple-element.86, bf16[512,1792]{1,0:T(8,128)(2,1)S(1)} %bitcast.31), kind=kOutput, calls=%fused_computation.1 | convolution fusion | flops 942276608 | bytes 6029312 | tf_op jit(solution)/shard_map/dot_general | solution.py:430
  126.8 3.9 %add_convert_fusion.2 = bf16[512,1792]{1,0:T(8,128)(2,1)} fusion(bf16[512,1792]{1,0:T(8,128)(2,1)} %collective-permute-done.18, bf16[512,512]{1,0:T(8,128)(2,1)S(1)} %get-tuple-element.83, bf16[512,1792]{1,0:T(8,128)(2,1)S(1)} %bitcast.32), kind=kOutput, calls=%fused_computation.2 | convolution fusion | flops 942276608 | bytes 6029312 | tf_op jit(solution)/shard_map/dot_general | solution.py:430
  130.7 17.3 %all-to-all-done.1.parts_ref = bf16[64,8,1920]{2,1,0:T(8,128)(2,1)S(1)} async-done(((bf16[64,8,1920]{2,1,0:T(8,128)(2,1)}), bf16[64,8,1920]{2,1,0:T(8,128)(2,1)S(1)}, u32[]{:S(2)}, u32[]{:S(2)}) %all-to-all-start.1) | async-done | bytes 1966112 | tf_op jit(solution)/shard_map/all_to_all | solution.py:461
  148.1 0.9 shard_map.119
  (8 shorter events, 0.0 us)
Async XLA Ops:
  0.6 41.4 %collective-permute-start.7 = (bf16[512,1792]{1,0:T(8,128)(2,1)}, bf16[512,1792]{1,0:T(8,128)(2,1)S(1)}, u32[]{:S(2)}, u32[]{:S(2)}) collective-permute-start(bf16[512,1792]{1,0:T(8,128)(2,1)} %bitcast.35), channel_id=1, source_target_pairs={{0,1},{1,0},{2,3},{3,2},{4,5},{5,4},{6,7},{7,6},{8,9},{9,8},{10,11... | collective-permute-start | bytes 5505032 | tf_op jit(solution)/shard_map/ppermute | solution.py:426
  0.7 41.8 %collective-permute-start.8 = (bf16[512,1792]{1,0:T(8,128)(2,1)}, bf16[512,1792]{1,0:T(8,128)(2,1)}, u32[]{:S(2)}, u32[]{:S(2)}) collective-permute-start(bf16[512,1792]{1,0:T(8,128)(2,1)} %bitcast.38), channel_id=1, source_target_pairs={{0,1},{1,0},{2,3},{3,2},{4,5},{5,4},{6,7},{7,6},{8,9},{9,8},{10,11... | collective-permute-start | bytes 5505032 | tf_op jit(solution)/shard_map/ppermute | solution.py:426
  1.2 44.1 %collective-permute-start.9 = (bf16[512,1792]{1,0:T(8,128)(2,1)}, bf16[512,1792]{1,0:T(8,128)(2,1)}, u32[]{:S(2)}, u32[]{:S(2)}) collective-permute-start(bf16[512,1792]{1,0:T(8,128)(2,1)} %bitcast.41), channel_id=1, source_target_pairs={{0,1},{1,0},{2,3},{3,2},{4,5},{5,4},{6,7},{7,6},{8,9},{9,8},{10,11... | collective-permute-start | bytes 5505032 | tf_op jit(solution)/shard_map/ppermute | solution.py:426
  14.6 7.3 %collective-permute-start = (bf16[4,8,3712]{2,1,0:T(8,128)(2,1)S(1)}, bf16[4,8,3712]{2,1,0:T(8,128)(2,1)S(1)}, u32[]{:S(2)}, u32[]{:S(2)}) collective-permute-start(bf16[4,8,3712]{2,1,0:T(8,128)(2,1)S(1)} %all_to_all.10.refs_0_), channel_id=1, source_target_pairs={{0,2},{1,9},{2,4},{3,11},{4,6},{5,13},{6,0},{7,15},{8,10},{9,17},{... | collective-permute-start | bytes 712712 | tf_op jit(solution)/shard_map/ppermute | solution.py:418
  16.1 9.4 %collective-permute-start.1 = (bf16[4,8,3712]{2,1,0:T(8,128)(2,1)S(1)}, bf16[4,8,3712]{2,1,0:T(8,128)(2,1)S(1)}, u32[]{:S(2)}, u32[]{:S(2)}) collective-permute-start(bf16[4,8,3712]{2,1,0:T(8,128)(2,1)S(1)} %all_to_all.10.refs_0_), channel_id=1, source_target_pairs={{0,4},{1,17},{2,6},{3,19},{4,0},{5,21},{6,2},{7,23},{8,12},{9,25},... | collective-permute-start | bytes 712712 | tf_op jit(solution)/shard_map/ppermute | solution.py:418
  21.9 6.1 %collective-permute-start.2 = (bf16[4,8,3712]{2,1,0:T(8,128)(2,1)S(1)}, bf16[4,8,3712]{2,1,0:T(8,128)(2,1)S(1)}, u32[]{:S(2)}, u32[]{:S(2)}) collective-permute-start(bf16[4,8,3712]{2,1,0:T(8,128)(2,1)S(1)} %all_to_all.10.refs_0_), channel_id=1, source_target_pairs={{0,6},{1,25},{2,0},{3,27},{4,2},{5,29},{6,4},{7,31},{8,14},{9,1},{... | collective-permute-start | bytes 712712 | tf_op jit(solution)/shard_map/ppermute | solution.py:418
  28.1 13.9 %collective-permute-start.3 = (bf16[4,32,1920]{2,1,0:T(8,128)(2,1)S(1)}, bf16[4,32,1920]{2,1,0:T(8,128)(2,1)S(1)}, u32[]{:S(2)}, u32[]{:S(2)}) collective-permute-start(bf16[4,32,1920]{2,1,0:T(8,128)(2,1)S(1)} %get-tuple-element.48.refs_0_), channel_id=1, source_target_pairs={{0,8},{1,3},{2,10},{3,5},{4,12},{5,7},{6,14},{7,1},{8,16},{9,11},{... | collective-permute-start | bytes 1474568 | tf_op jit(solution)/shard_map/ppermute | solution.py:418
  30.1 8.5 %collective-permute-start.5 = (bf16[4,32,1792]{2,1,0:T(8,128)(2,1)S(1)}, bf16[4,32,1792]{2,1,0:T(8,128)(2,1)S(1)}, u32[]{:S(2)}, u32[]{:S(2)}) collective-permute-start(bf16[4,32,1792]{2,1,0:T(8,128)(2,1)S(1)} %get-tuple-element.49.refs_1_), channel_id=1, source_target_pairs={{0,24},{1,7},{2,26},{3,1},{4,28},{5,3},{6,30},{7,5},{8,0},{9,15},{... | collective-permute-start | bytes 1376264 | tf_op jit(solution)/shard_map/ppermute | solution.py:418
  38.6 18.4 %collective-permute-start.10 = (bf16[4,32,1920]{2,1,0:T(8,128)(2,1)S(1)}, bf16[4,32,1920]{2,1,0:T(8,128)(2,1)S(1)}, u32[]{:S(2)}, u32[]{:S(2)}) collective-permute-start(bf16[4,32,1920]{2,1,0:T(8,128)(2,1)S(1)} %get-tuple-element.48.refs_0_), channel_id=1, source_target_pairs={{0,24},{1,7},{2,26},{3,1},{4,28},{5,3},{6,30},{7,5},{8,0},{9,15},{... | collective-permute-start | bytes 1474568 | tf_op jit(solution)/shard_map/ppermute | solution.py:418
  42.0 19.2 %collective-permute-start.4 = (bf16[4,32,1920]{2,1,0:T(8,128)(2,1)S(1)}, bf16[4,32,1920]{2,1,0:T(8,128)(2,1)S(1)}, u32[]{:S(2)}, u32[]{:S(2)}) collective-permute-start(bf16[4,32,1920]{2,1,0:T(8,128)(2,1)S(1)} %collective-permute-done.3.refs_0_), channel_id=1, source_target_pairs={{0,8},{1,3},{2,10},{3,5},{4,12},{5,7},{6,14},{7,1},{8,16},{9,11},{... | collective-permute-start | bytes 1474568 | tf_op jit(solution)/shard_map/ppermute | solution.py:418
  42.0 3.3 %copy-start.4 = (bf16[512,1792]{1,0:T(8,128)(2,1)}, bf16[512,1792]{1,0:T(8,128)(2,1)S(1)}, u32[]{:S(2)}) copy-start(bf16[512,1792]{1,0:T(8,128)(2,1)S(1)} %collective-permute-done.7.refs_3_.refs_2_) | copy-start | bytes 5505028
  42.0 14.9 %collective-permute-start.11 = (bf16[4,32,1792]{2,1,0:T(8,128)(2,1)S(1)}, bf16[4,32,1792]{2,1,0:T(8,128)(2,1)S(1)}, u32[]{:S(2)}, u32[]{:S(2)}) collective-permute-start(bf16[4,32,1792]{2,1,0:T(8,128)(2,1)S(1)} %get-tuple-element.49.refs_1_), channel_id=1, source_target_pairs={{0,8},{1,3},{2,10},{3,5},{4,12},{5,7},{6,14},{7,1},{8,16},{9,11},{... | collective-permute-start | bytes 1376264 | tf_op jit(solution)/shard_map/ppermute | solution.py:418
  42.5 18.6 %collective-permute-start.6 = (bf16[4,32,1792]{2,1,0:T(8,128)(2,1)S(1)}, bf16[4,32,1792]{2,1,0:T(8,128)(2,1)S(1)}, u32[]{:S(2)}, u32[]{:S(2)}) collective-permute-start(bf16[4,32,1792]{2,1,0:T(8,128)(2,1)S(1)} %collective-permute-done.5.refs_3_), channel_id=1, source_target_pairs={{0,24},{1,7},{2,26},{3,1},{4,28},{5,3},{6,30},{7,5},{8,0},{9,15},{... | collective-permute-start | bytes 1376264 | tf_op jit(solution)/shard_map/ppermute | solution.py:418
  65.7 9.3 %collective-permute-start.12 = (bf16[128,768]{1,0:T(8,128)(2,1)}, bf16[128,768]{1,0:T(8,128)(2,1)S(1)}, u32[]{:S(2)}, u32[]{:S(2)}) collective-permute-start(bf16[128,768]{1,0:T(8,128)(2,1)} %get-tuple-element.71), channel_id=1, source_target_pairs={{0,32},{32,64},{64,96},{96,0},{1,33},{33,65},{65,97},{97,1},{2,34}... | collective-permute-start | bytes 589832 | tf_op jit(solution)/shard_map/ppermute | solution.py:422
  66.4 8.6 %collective-permute-start.13 = (bf16[128,768]{1,0:T(8,128)(2,1)}, bf16[128,768]{1,0:T(8,128)(2,1)S(1)}, u32[]{:S(2)}, u32[]{:S(2)}) collective-permute-start(bf16[128,768]{1,0:T(8,128)(2,1)} %get-tuple-element.72), channel_id=1, source_target_pairs={{0,64},{32,96},{64,0},{96,32},{1,65},{33,97},{65,1},{97,33},{2,66}... | collective-permute-start | bytes 589832 | tf_op jit(solution)/shard_map/ppermute | solution.py:422
  68.4 7.8 %collective-permute-start.14 = (bf16[128,768]{1,0:T(8,128)(2,1)}, bf16[128,768]{1,0:T(8,128)(2,1)S(1)}, u32[]{:S(2)}, u32[]{:S(2)}) collective-permute-start(bf16[128,768]{1,0:T(8,128)(2,1)} %get-tuple-element.73), channel_id=1, source_target_pairs={{0,96},{32,0},{64,32},{96,64},{1,97},{33,1},{65,33},{97,65},{2,98}... | collective-permute-start | bytes 589832 | tf_op jit(solution)/shard_map/ppermute | solution.py:422
  77.4 6.9 %collective-permute-start.15 = (bf16[128,768]{1,0:T(8,128)(2,1)S(1)}, bf16[128,768]{1,0:T(8,128)(2,1)S(1)}, u32[]{:S(2)}, u32[]{:S(2)}) collective-permute-start(bf16[128,768]{1,0:T(8,128)(2,1)S(1)} %get-tuple-element.75.refs_0_), channel_id=1, source_target_pairs={{0,32},{32,64},{64,96},{96,0},{1,33},{33,65},{65,97},{97,1},{2,34}... | collective-permute-start | bytes 589832 | tf_op jit(solution)/shard_map/ppermute | solution.py:422
  77.5 9.8 %collective-permute-start.16 = (bf16[128,768]{1,0:T(8,128)(2,1)S(1)}, bf16[128,768]{1,0:T(8,128)(2,1)S(1)}, u32[]{:S(2)}, u32[]{:S(2)}) collective-permute-start(bf16[128,768]{1,0:T(8,128)(2,1)S(1)} %get-tuple-element.75.refs_0_), channel_id=1, source_target_pairs={{0,64},{32,96},{64,0},{96,32},{1,65},{33,97},{65,1},{97,33},{2,66}... | collective-permute-start | bytes 589832 | tf_op jit(solution)/shard_map/ppermute | solution.py:422
  81.5 5.8 %collective-permute-start.17 = (bf16[128,768]{1,0:T(8,128)(2,1)S(1)}, bf16[128,768]{1,0:T(8,128)(2,1)S(1)}, u32[]{:S(2)}, u32[]{:S(2)}) collective-permute-start(bf16[128,768]{1,0:T(8,128)(2,1)S(1)} %get-tuple-element.75.refs_0_), channel_id=1, source_target_pairs={{0,96},{32,0},{64,32},{96,64},{1,97},{33,1},{65,33},{97,65},{2,98}... | collective-permute-start | bytes 589832 | tf_op jit(solution)/shard_map/ppermute | solution.py:422
  87.3 0.9 copy-start
  89.6 4.0 %copy-start.2 = (bf16[4,128,1792]{2,1,0:T(8,128)(2,1)S(1)}, bf16[4,128,1792]{2,1,0:T(8,128)(2,1)}, u32[]{:S(2)}) copy-start(bf16[4,128,1792]{2,1,0:T(8,128)(2,1)} %get-tuple-element.84) | copy-start | bytes 5505028
  93.6 24.7 %collective-permute-start.20 = (bf16[512,1792]{1,0:T(8,128)(2,1)}, bf16[512,1792]{1,0:T(8,128)(2,1)}, u32[]{:S(2)}, u32[]{:S(2)}) collective-permute-start(bf16[512,1792]{1,0:T(8,128)(2,1)} %convolution_convert_fusion), channel_id=1, source_target_pairs={{0,1},{1,0},{2,3},{3,2},{4,5},{5,4},{6,7},{7,6},{8,9},{9,8},{10,11... | collective-permute-start | bytes 5505032 | tf_op jit(solution)/shard_map/ppermute | solution.py:426
  96.0 26.9 %collective-permute-start.19 = (bf16[512,1792]{1,0:T(8,128)(2,1)}, bf16[512,1792]{1,0:T(8,128)(2,1)}, u32[]{:S(2)}, u32[]{:S(2)}) collective-permute-start(bf16[512,1792]{1,0:T(8,128)(2,1)} %convolution_convert_fusion.1), channel_id=1, source_target_pairs={{0,1},{1,0},{2,3},{3,2},{4,5},{5,4},{6,7},{7,6},{8,9},{9,8},{10,11... | collective-permute-start | bytes 5505032 | tf_op jit(solution)/shard_map/ppermute | solution.py:426
  98.9 3.2 %copy-start.1 = (bf16[4,128,128]{2,1,0:T(8,128)(2,1)S(1)}, bf16[4,128,128]{2,1,0:T(8,128)(2,1)}, u32[]{:S(2)}) copy-start(bf16[4,128,128]{2,1,0:T(8,128)(2,1)} %get-tuple-element.74.refs_4_) | copy-start | bytes 393220
  98.9 27.9 %collective-permute-start.18 = (bf16[512,1792]{1,0:T(8,128)(2,1)}, bf16[512,1792]{1,0:T(8,128)(2,1)}, u32[]{:S(2)}, u32[]{:S(2)}) collective-permute-start(bf16[512,1792]{1,0:T(8,128)(2,1)} %convolution_convert_fusion.2), channel_id=1, source_target_pairs={{0,1},{1,0},{2,3},{3,2},{4,5},{5,4},{6,7},{7,6},{8,9},{9,8},{10,11... | collective-permute-start | bytes 5505032 | tf_op jit(solution)/shard_map/ppermute | solution.py:426
  107.7 40.4 %all-to-all-start.1 = ((bf16[64,8,1920]{2,1,0:T(8,128)(2,1)}), bf16[64,8,1920]{2,1,0:T(8,128)(2,1)S(1)}, u32[]{:S(2)}, u32[]{:S(2)}) async-start(bf16[64,8,1920]{2,1,0:T(8,128)(2,1)} %bitcast.28), calls=%async_computation.1 | async-start | bytes 3932160 | tf_op jit(solution)/shard_map/all_to_all | solution.py:461
  118.3 4.6 %copy-start.3 = (bf16[4,128,1792]{2,1,0:T(8,128)(2,1)S(1)}, bf16[4,128,1792]{2,1,0:T(8,128)(2,1)}, u32[]{:S(2)}) copy-start(bf16[4,128,1792]{2,1,0:T(8,128)(2,1)} %get-tuple-element.84) | copy-start | bytes 5505028

commit v3 on v2

--- a/solution.py
+++ b/solution.py
@@ -40,6 +40,10 @@
 
 def dot_t(rows, mat):
     return lax.dot_general(rows, mat, (((1,), (1,)), ((), ())), preferred_element_type=F32)
+
+
+def dot_n(rows, mat):
+    return jnp.dot(rows, mat, preferred_element_type=F32)
 
 
 def flat(ref):
@@ -106,6 +110,22 @@
     )(*map(far_off, mats))
 
 
+def flip(*refs):
+    count = len(refs) // 2
+    for m in range(count):
+        refs[count + m][...] = refs[m][...].T
+
+
+def flip_call(mats):
+    return pl.pallas_call(
+        flip,
+        in_specs=in_core(len(mats)),
+        out_specs=in_core(len(mats)),
+        out_shape=[pltpu.VMEM(m.shape[::-1], BF) for m in mats],
+        compiler_params=params(8),
+    )(*map(near_core, mats))
+
+
 def stack(*refs):
     pieces, x_ref, y_ref = refs[:SIDE], refs[SIDE], refs[SIDE + 1]
     lap, rows = x_ref.shape[2], pieces[0].shape[1]
@@ -128,7 +148,7 @@
     )(*map(near_core, pieces))
 
 
-def pre_acts(count, first, width):
+def pre_acts(count, first, width, multiply):
     def body(plane_ref, *refs):
         x_refs, y_refs, mats = refs[:count], refs[count:2 * count], refs[2 * count:2 * count + 6]
         *outs, x_out, y_out, meta_out, val_ref, sems, out_sems = refs[-10:]
@@ -154,7 +174,7 @@
         hit_a, hit_b = owner == meta[:, 0:1], owner == meta[:, 1:2]
         low = first_half(rows)
         for m in range(6):
-            full = dot_t(y if m % 3 == 2 else x, mats[m][...])
+            full = multiply(y if m % 3 == 2 else x, mats[m][...])
             sums = []
             for hit in (hit_a, hit_b):
                 kept = jnp.where(hit, full, 0.0)
@@ -179,16 +199,16 @@
     return body
 
 
-def pre_call(plane, pieces, mats, first, total, into):
+def pre_call(plane, pieces, mats, multiply, first, total, into):
     count = len(pieces) // 2
     lead, rows, _ = pieces[0].shape
-    width = mats[0].shape[1]
+    width = pieces[-1].shape[2]
     outer = pl.BlockSpec(memory_space=pl.ANY)
     outs = [pltpu.HBM((rows * total, 6 * LANES), BF)] * lead
     outs = outs + [pltpu.HBM((lead, rows * total, w), BF) for w in (width, width, LANES)]
     taken = len(pieces) + 6
     return pl.pallas_call(
-        pre_acts(count, first * rows, width),
+        pre_acts(count, first * rows, width, multiply),
         grid_spec=pltpu.PrefetchScalarGridSpec(
             num_scalar_prefetch=1,
             grid=(1,),
@@ -450,9 +470,10 @@
     y_1 = shift(y_0, 1, 1)
     x_2 = shift(x_1, 1, 1)
     y_2 = shift(y_3, 1, 3)
-    state = pre_call(plane, [x_0, y_0], mats, 2, SIDE, [])
-    state = pre_call(plane, [x_1, x_3, y_1, y_3], mats, 0, SIDE, state)
-    *parts, x_rows, y_rows, meta_rows = pre_call(plane, [x_2, y_2], mats, 3, SIDE, state)
+    state = pre_call(plane, [x_0, y_0], mats, dot_t, 2, SIDE, [])
+    flipped = flip_call(mats)
+    state = pre_call(plane, [x_1, x_3, y_1, y_3], flipped, dot_n, 0, SIDE, state)
+    *parts, x_rows, y_rows, meta_rows = pre_call(plane, [x_2, y_2], flipped, dot_n, 3, SIDE, state)
     parts = [parts[0]] + [turn(parts[k], k) for k in range(1, SIDE)]
     done, route = middle_call(plane, parts, meta_rows)
     acts = [done] + [turn(done, k) for k in range(1, SIDE)]

time: 149 us -> 148 us (level)
  waiting for transfers between devices: 46.8 us -> 43.7 us
    ppermute x9, waiting for transfers between devices: 16.8 us -> 13.9 us  [shift(): return lax.ppermute(arr, PLANE, pairs)]
    pallas_call x3 -> x4, Pallas kernels: 13.3 us -> 14.2 us  [the longest x3 11.3 us: pre_call(): pl.pallas_call(pre_acts(count, first * rows, width, multiply), grid_spec=...]
  transfers between devices with their start and end apart: 22 -> 22, of which waited for: 11 -> 9; matrix products, arithmetic and copies ran while one was open for 11% -> 12% of each run, Pallas kernels for 16% -> 18%
where the time goes in v3:
time: 148 us; the launch traced here: 147 us
  waiting for transfers between devices  43.7 us (30%)
  starting transfers between devices  36.7 us (25%)
  Pallas kernels  32.4 us (22%)
  matrix products  21.1 us (14%)
  blocking collectives  11.6 us (8%)
    dot_general x6, matrix products, contract_rows(): lax.dot_general(left, right, (((0,), (0,)), ((), ())), preferred_element_...  21.1 us
    all_to_all x1, waiting for transfers between devices, local(): lax.all_to_all(sent.reshape(-1, tok_rows, lap), TORUS, 0, 0, tiled=True)  17.3 us
    ppermute x9, starting transfers between devices, shift(): return lax.ppermute(arr, PLANE, pairs)  16.9 us
    ppermute x9, waiting for transfers between devices, shift(): return lax.ppermute(arr, PLANE, pairs)  13.9 us
    ppermute x6, waiting for transfers between devices, turn(): return lax.ppermute(arr, 'ep', [(i, (i + by) % SIDE) for i in range(SIDE)])  12.4 us
    all_to_all x1, blocking collectives, local(): own = lax.all_to_all(send, 'ep', 0, 0, tiled=True)  11.6 us
    pallas_call x3, Pallas kernels, pre_call(): pl.pallas_call(pre_acts(count, first * rows, width, multiply), grid_spec=...  11.3 us
    all_to_all x1, starting transfers between devices, local(): lax.all_to_all(sent.reshape(-1, tok_rows, lap), TORUS, 0, 0, tiled=True)  10.9 us
  transfers between devices with their start and end apart: 22, of which 9 were waited for; matrix products, arithmetic and copies ran while one was open for 12% of the time, Pallas kernels for 18%

profile of v3, /device:TPU:0, one launch (start us, length us, event | category | flops | bytes accessed | tf_op | source)
XLA Modules:
  0.0 147.1 jit_solution(3279041605712284996)
XLA Ops:
  0.6 0.1 collective-permute-start.7
  0.7 0.5 collective-permute-start.8
  1.2 0.1 collective-permute-start.9
  1.3 1.7 %shard_map.110 = bf16[4,8,3712]{2,1,0:T(8,128)(2,1)} custom-call(s32[1]{0:T(128)} %bitcast.plane_ref, s32[1]{0:T(128)} %bitcast.1.z_ref, s32[1]{0:T(128)} %bitcast.2.chip_ref.x_ref, s32[1]{0:T(128)} %bitcast.3.core_ref, bf16[8,7168]{1,0:T(8,128)(2,1)} %tok_ref.1, bf16[8,7168]{1,0:T(8,128)(2,1)} %cot_ref.1, s32[2,8]{1,0:T(2,128)} %bitcast.43, ...), custom_call_target="tpu_custom_call" | custom-call | tf_op jit(solution)/shard_map/pallas_call | solution.py:79
  3.0 11.6 %all_to_all.10.refs_0_ = bf16[4,8,3712]{2,1,0:T(8,128)(2,1)S(1)} all-to-all(bf16[4,8,3712]{2,1,0:T(8,128)(2,1)} %shard_map.110), channel_id=1, replica_groups=mesh['ep'=4,'z'=4,'x'=4,'core'=2] {'ep'}, dimensions={0} | all-to-all | bytes 475136 | tf_op jit(solution)/shard_map/all_to_all | solution.py:463
  14.6 1.5 %collective-permute-start = (bf16[4,8,3712]{2,1,0:T(8,128)(2,1)S(1)}, bf16[4,8,3712]{2,1,0:T(8,128)(2,1)S(1)}, u32[]{:S(2)}, u32[]{:S(2)}) collective-permute-start(bf16[4,8,3712]{2,1,0:T(8,128)(2,1)S(1)} %all_to_all.10.refs_0_), channel_id=1, source_target_pairs={{0,2},{1,9},{2,4},{3,11},{4,6},{5,13},{6,0},{7,15},{8,10},{9,17},{... | collective-permute-start | bytes 712712 | tf_op jit(solution)/shard_map/ppermute | solution.py:438
  16.1 2.7 %collective-permute-start.1 = (bf16[4,8,3712]{2,1,0:T(8,128)(2,1)S(1)}, bf16[4,8,3712]{2,1,0:T(8,128)(2,1)S(1)}, u32[]{:S(2)}, u32[]{:S(2)}) collective-permute-start(bf16[4,8,3712]{2,1,0:T(8,128)(2,1)S(1)} %all_to_all.10.refs_0_), channel_id=1, source_target_pairs={{0,4},{1,17},{2,6},{3,19},{4,0},{5,21},{6,2},{7,23},{8,12},{9,25},... | collective-permute-start | bytes 712712 | tf_op jit(solution)/shard_map/ppermute | solution.py:438
  18.8 3.1 %collective-permute-done.refs_1_ = bf16[4,8,3712]{2,1,0:T(8,128)(2,1)S(1)} collective-permute-done((bf16[4,8,3712]{2,1,0:T(8,128)(2,1)S(1)}, bf16[4,8,3712]{2,1,0:T(8,128)(2,1)S(1)}, u32[]{:S(2)}, u32[]{:S(2)}) %collective-permute-start) | collective-permute-done | bytes 237600 | tf_op jit(solution)/shard_map/ppermute | solution.py:438
  21.9 1.5 %collective-permute-start.2 = (bf16[4,8,3712]{2,1,0:T(8,128)(2,1)S(1)}, bf16[4,8,3712]{2,1,0:T(8,128)(2,1)S(1)}, u32[]{:S(2)}, u32[]{:S(2)}) collective-permute-start(bf16[4,8,3712]{2,1,0:T(8,128)(2,1)S(1)} %all_to_all.10.refs_0_), channel_id=1, source_target_pairs={{0,6},{1,25},{2,0},{3,27},{4,2},{5,29},{6,4},{7,31},{8,14},{9,1},{... | collective-permute-start | bytes 712712 | tf_op jit(solution)/shard_map/ppermute | solution.py:438
  23.5 2.0 %collective-permute-done.1.refs_2_ = bf16[4,8,3712]{2,1,0:T(8,128)(2,1)S(1)} collective-permute-done((bf16[4,8,3712]{2,1,0:T(8,128)(2,1)S(1)}, bf16[4,8,3712]{2,1,0:T(8,128)(2,1)S(1)}, u32[]{:S(2)}, u32[]{:S(2)}) %collective-permute-start.1) | collective-permute-done | bytes 237600 | tf_op jit(solution)/shard_map/ppermute | solution.py:438
  25.5 2.6 %collective-permute-done.2.refs_3_ = bf16[4,8,3712]{2,1,0:T(8,128)(2,1)S(1)} collective-permute-done((bf16[4,8,3712]{2,1,0:T(8,128)(2,1)S(1)}, bf16[4,8,3712]{2,1,0:T(8,128)(2,1)S(1)}, u32[]{:S(2)}, u32[]{:S(2)}) %collective-permute-start.2) | collective-permute-done | bytes 237600 | tf_op jit(solution)/shard_map/ppermute | solution.py:438
  28.0 0.1 shard_map.111
  28.1 2.0 %collective-permute-start.3 = (bf16[4,32,1920]{2,1,0:T(8,128)(2,1)S(1)}, bf16[4,32,1920]{2,1,0:T(8,128)(2,1)S(1)}, u32[]{:S(2)}, u32[]{:S(2)}) collective-permute-start(bf16[4,32,1920]{2,1,0:T(8,128)(2,1)S(1)} %get-tuple-element.54.refs_0_), channel_id=1, source_target_pairs={{0,8},{1,3},{2,10},{3,5},{4,12},{5,7},{6,14},{7,1},{8,16},{9,11},{... | collective-permute-start | bytes 1474568 | tf_op jit(solution)/shard_map/ppermute | solution.py:438
  30.1 2.2 %collective-permute-start.5 = (bf16[4,32,1792]{2,1,0:T(8,128)(2,1)S(1)}, bf16[4,32,1792]{2,1,0:T(8,128)(2,1)S(1)}, u32[]{:S(2)}, u32[]{:S(2)}) collective-permute-start(bf16[4,32,1792]{2,1,0:T(8,128)(2,1)S(1)} %get-tuple-element.55.refs_1_), channel_id=1, source_target_pairs={{0,24},{1,7},{2,26},{3,1},{4,28},{5,3},{6,30},{7,5},{8,0},{9,15},{... | collective-permute-start | bytes 1376264 | tf_op jit(solution)/shard_map/ppermute | solution.py:438
  32.3 6.3 %collective-permute-done.5.refs_3_ = bf16[4,32,1792]{2,1,0:T(8,128)(2,1)S(1)} collective-permute-done((bf16[4,32,1792]{2,1,0:T(8,128)(2,1)S(1)}, bf16[4,32,1792]{2,1,0:T(8,128)(2,1)S(1)}, u32[]{:S(2)}, u32[]{:S(2)}) %collective-permute-start.5) | collective-permute-done | bytes 458784 | tf_op jit(solution)/shard_map/ppermute | solution.py:438
  38.6 3.4 %collective-permute-start.10 = (bf16[4,32,1920]{2,1,0:T(8,128)(2,1)S(1)}, bf16[4,32,1920]{2,1,0:T(8,128)(2,1)S(1)}, u32[]{:S(2)}, u32[]{:S(2)}) collective-permute-start(bf16[4,32,1920]{2,1,0:T(8,128)(2,1)S(1)} %get-tuple-element.54.refs_0_), channel_id=1, source_target_pairs={{0,24},{1,7},{2,26},{3,1},{4,28},{5,3},{6,30},{7,5},{8,0},{9,15},{... | collective-permute-start | bytes 1474568 | tf_op jit(solution)/shard_map/ppermute | solution.py:438
  42.0 0.0 collective-permute-done.3.refs_0_
  42.0 0.0 collective-permute-start.4
  42.0 0.0 collective-permute-done.7.refs_3_.refs_2_
  42.0 0.0 copy-start.4
  42.0 0.5 collective-permute-start.11
  42.5 0.0 collective-permute-done.8.refs_4_.refs_3_
  42.5 3.0 %collective-permute-start.6 = (bf16[4,32,1792]{2,1,0:T(8,128)(2,1)S(1)}, bf16[4,32,1792]{2,1,0:T(8,128)(2,1)S(1)}, u32[]{:S(2)}, u32[]{:S(2)}) collective-permute-start(bf16[4,32,1792]{2,1,0:T(8,128)(2,1)S(1)} %collective-permute-done.5.refs_3_), channel_id=1, source_target_pairs={{0,24},{1,7},{2,26},{3,1},{4,28},{5,3},{6,30},{7,5},{8,0},{9,15},{... | collective-permute-start | bytes 1376264 | tf_op jit(solution)/shard_map/ppermute | solution.py:438
  45.5 0.0 collective-permute-done.9.refs_5_
  45.5 4.2 %shard_map.112 = (bf16[512,1792]{1,0:T(8,128)(2,1)S(1)}, bf16[512,1792]{1,0:T(8,128)(2,1)S(1)}, bf16[512,1792]{1,0:T(8,128)(2,1)S(1)}, bf16[512,1792]{1,0:T(8,12...) custom-call(bf16[512,1792]{1,0:T(8,128)(2,1)} %bitcast.36, bf16[512,1792]{1,0:T(8,128)(2,1)} %bitcast.39, ...), custom_call_target="tpu_custom_call" | custom-call | tf_op jit(solution)/shard_map/pallas_call | solution.py:103
  49.8 4.6 %shard_map.114 = (bf16[128,768]{1,0:T(8,128)(2,1)}, bf16[128,768]{1,0:T(8,128)(2,1)}, bf16[128,768]{1,0:T(8,128)(2,1)}, bf16[128,768]{1,0:T(8,128)(2,1)}, bf16[4...) custom-call(s32[1]{0:T(128)} %bitcast.plane_ref, ...), custom_call_target="tpu_custom_call" | custom-call | tf_op jit(solution)/shard_map/pallas_call | solution.py:210
  54.3 2.9 %shard_map.113 = (bf16[1792,512]{1,0:T(8,128)(2,1)S(1)}, bf16[1792,512]{1,0:T(8,128)(2,1)S(1)}, bf16[1792,512]{1,0:T(8,128)(2,1)S(1)}, bf16[1792,512]{1,0:T(8,12...) custom-call(bf16[512,1792]{1,0:T(8,128)(2,1)S(1)} %get-tuple-element.56.refs_0_.refs_2_, ...), custom_call_target="tpu_custom_call" | custom-call | tf_op jit(solution)/shard_map/pallas_call | solution.py:120
  57.2 0.0 collective-permute-done.11.refs_2_
  57.2 4.2 %shard_map.115 = (bf16[128,768]{1,0:T(8,128)(2,1)}, bf16[128,768]{1,0:T(8,128)(2,1)}, bf16[128,768]{1,0:T(8,128)(2,1)}, bf16[128,768]{1,0:T(8,128)(2,1)}, bf16[4...) custom-call(s32[1]{0:T(128)} %bitcast.plane_ref, ...), custom_call_target="tpu_custom_call", output_to_operand_aliasing={{0}: (11, {}), {1}: (12, {}), {2}: (13, {}), {3}: (14, {}),... | custom-call | tf_op jit(solution)/shard_map/pallas_call | solution.py:210
  61.4 0.0 collective-permute-done.4.refs_0_
  61.4 2.6 %shard_map.116 = (bf16[128,768]{1,0:T(8,128)(2,1)}, bf16[128,768]{1,0:T(8,128)(2,1)}, bf16[128,768]{1,0:T(8,128)(2,1)}, bf16[128,768]{1,0:T(8,128)(2,1)}, bf16[4...) custom-call(s32[1]{0:T(128)} %bitcast.plane_ref, ...), custom_call_target="tpu_custom_call", output_to_operand_aliasing={{0}: (9, {}), {1}: (10, {}), {2}: (11, {}), {3}: (12, {}), ... | custom-call | tf_op jit(solution)/shard_map/pallas_call | solution.py:210
  64.0 0.6 collective-permute-start.12
  64.7 2.1 %collective-permute-start.13 = (bf16[128,768]{1,0:T(8,128)(2,1)}, bf16[128,768]{1,0:T(8,128)(2,1)S(1)}, u32[]{:S(2)}, u32[]{:S(2)}) collective-permute-start(bf16[128,768]{1,0:T(8,128)(2,1)} %get-tuple-element.84), channel_id=1, source_target_pairs={{0,64},{32,96},{64,0},{96,32},{1,65},{33,97},{65,1},{97,33},{2,66}... | collective-permute-start | bytes 589832 | tf_op jit(solution)/shard_map/ppermute | solution.py:442
  66.7 0.9 collective-permute-start.14
  67.6 5.7 %collective-permute-done.12.refs_1_ = bf16[128,768]{1,0:T(8,128)(2,1)S(1)} collective-permute-done((bf16[128,768]{1,0:T(8,128)(2,1)}, bf16[128,768]{1,0:T(8,128)(2,1)S(1)}, u32[]{:S(2)}, u32[]{:S(2)}) %collective-permute-start.12) | collective-permute-done | bytes 196640 | tf_op jit(solution)/shard_map/ppermute | solution.py:442
  73.3 0.0 collective-permute-done.13.refs_2_
  73.3 0.9 collective-permute-done.14.refs_3_
  74.2 1.2 shard_map.117
  75.4 0.3 collective-permute-start.15
  75.7 3.8 %collective-permute-start.16 = (bf16[128,768]{1,0:T(8,128)(2,1)S(1)}, bf16[128,768]{1,0:T(8,128)(2,1)S(1)}, u32[]{:S(2)}, u32[]{:S(2)}) collective-permute-start(bf16[128,768]{1,0:T(8,128)(2,1)S(1)} %get-tuple-element.87.refs_0_), channel_id=1, source_target_pairs={{0,64},{32,96},{64,0},{96,32},{1,65},{33,97},{65,1},{97,33},{2,66}... | collective-permute-start | bytes 589832 | tf_op jit(solution)/shard_map/ppermute | solution.py:442
  79.5 0.0 collective-permute-start.17
  79.5 2.8 %collective-permute-done.15.refs_1_ = bf16[128,768]{1,0:T(8,128)(2,1)S(1)} collective-permute-done((bf16[128,768]{1,0:T(8,128)(2,1)S(1)}, bf16[128,768]{1,0:T(8,128)(2,1)S(1)}, u32[]{:S(2)}, u32[]{:S(2)}) %collective-permute-start.15) | collective-permute-done | bytes 196640 | tf_op jit(solution)/shard_map/ppermute | solution.py:442
  82.3 2.9 %collective-permute-done.16.refs_2_ = bf16[128,768]{1,0:T(8,128)(2,1)S(1)} collective-permute-done((bf16[128,768]{1,0:T(8,128)(2,1)S(1)}, bf16[128,768]{1,0:T(8,128)(2,1)S(1)}, u32[]{:S(2)}, u32[]{:S(2)}) %collective-permute-start.16) | collective-permute-done | bytes 196640 | tf_op jit(solution)/shard_map/ppermute | solution.py:442
  85.3 0.0 collective-permute-done.17.refs_3_
  85.3 0.9 copy-done
  86.2 1.3 shard_map.121
  87.6 0.0 copy-start.2
  87.6 4.0 %convolution_convert_fusion = bf16[512,1792]{1,0:T(8,128)(2,1)} fusion(bf16[512,512]{1,0:T(8,128)(2,1)S(1)} %get-tuple-element.102, bf16[512,1792]{1,0:T(8,128)(2,1)} %bitcast.33), kind=kOutput, calls=%fused_computation.3 | convolution fusion | flops 940441600 | bytes 4194304 | tf_op jit(solution)/shard_map/dot_general | solution.py:450
  91.6 0.0 collective-permute-start.20
  91.6 2.4 %convolution_convert_fusion.1 = bf16[512,1792]{1,0:T(8,128)(2,1)} fusion(bf16[512,512]{1,0:T(8,128)(2,1)S(1)} %get-tuple-element.99, bf16[512,1792]{1,0:T(8,128)(2,1)S(1)} %bitcast.29), kind=kOutput, calls=%fused_computation.4 | convolution fusion | flops 940441600 | bytes 4194304 | tf_op jit(solution)/shard_map/dot_general | solution.py:450
  94.0 0.5 collective-permute-start.19
  94.5 2.4 %convolution_convert_fusion.2 = bf16[512,1792]{1,0:T(8,128)(2,1)} fusion(bf16[512,512]{1,0:T(8,128)(2,1)S(1)} %get-tuple-element.97, bf16[512,1792]{1,0:T(8,128)(2,1)S(1)} %bitcast.30), kind=kOutput, calls=%fused_computation.5 | convolution fusion | flops 940441600 | bytes 4194304 | tf_op jit(solution)/shard_map/dot_general | solution.py:450
  96.9 0.0 collective-permute-start.18
  96.9 3.2 %shard_map.118 = (bf16[512,1792]{1,0:T(8,128)(2,1)S(1)}, bf16[512,1792]{1,0:T(8,128)(2,1)S(1)}, bf16[512,1792]{1,0:T(8,128)(2,1)S(1)}, bf16[512,1792]{1,0:T(8,128)(2,1)S(1)}) custom-call(bf16[512,1792]{1,0:T(8,128)(2,1)} %bitcast.37, bf16[512,1792]{1,0:T(8,128)(2,1)} %bitcast.40, bf16[512,1792]{1,0:T(8,128)(2,1)} %copy-done.4, ...), custom_call_target="tpu_custom_call" | custom-call | tf_op jit(solution)/shard_map/pallas_call | solution.py:103
  100.1 5.5 %shard_map.119 = bf16[4,128,1920]{2,1,0:T(8,128)(2,1)} custom-call(s32[1]{0:T(128)} %bitcast.plane_ref, s32[1]{0:T(128)} %bitcast.1.z_ref, s32[1]{0:T(128)} %bitcast.2.chip_ref.x_ref, s32[1]{0:T(128)} %bitcast.3.core_ref, bf16[128,768]{1,0:T(8,128)(2,1)S(1)} %get-tuple-element.87.refs_0_, bf16[128,768]{1,0:T(8,128)(2,1)S(1)} %collective-permute-done.15.refs_1_, ...), custom_call_target="tpu_custom_call" | custom-call | tf_op jit(solution)/shard_map/pallas_call | solution.py:375
  105.6 10.9 %all-to-all-start.1 = ((bf16[64,8,1920]{2,1,0:T(8,128)(2,1)}), bf16[64,8,1920]{2,1,0:T(8,128)(2,1)S(1)}, u32[]{:S(2)}, u32[]{:S(2)}) async-start(bf16[64,8,1920]{2,1,0:T(8,128)(2,1)} %bitcast.28), calls=%async_computation.1 | async-start | bytes 3932160 | tf_op jit(solution)/shard_map/all_to_all | solution.py:482
  116.6 0.0 copy-start.3
  116.6 4.6 %add_convert_fusion = bf16[512,1792]{1,0:T(8,128)(2,1)} fusion(bf16[512,1792]{1,0:T(8,128)(2,1)} %collective-permute-done.20, bf16[512,512]{1,0:T(8,128)(2,1)S(1)} %get-tuple-element.100, bf16[512,1792]{1,0:T(8,128)(2,1)} %bitcast.34), kind=kOutput, calls=%fused_computation | convolution fusion | flops 942276608 | bytes 6029312 | tf_op jit(solution)/shard_map/dot_general | solution.py:450
  121.1 0.0 collective-permute-done.19
  121.1 3.9 %add_convert_fusion.1 = bf16[512,1792]{1,0:T(8,128)(2,1)} fusion(bf16[512,1792]{1,0:T(8,128)(2,1)} %collective-permute-done.19, bf16[512,512]{1,0:T(8,128)(2,1)S(1)} %get-tuple-element.98, bf16[512,1792]{1,0:T(8,128)(2,1)S(1)} %bitcast.31), kind=kOutput, calls=%fused_computation.1 | convolution fusion | flops 942276608 | bytes 6029312 | tf_op jit(solution)/shard_map/dot_general | solution.py:450
  125.0 0.0 collective-permute-done.18
  125.0 3.9 %add_convert_fusion.2 = bf16[512,1792]{1,0:T(8,128)(2,1)} fusion(bf16[512,1792]{1,0:T(8,128)(2,1)} %collective-permute-done.18, bf16[512,512]{1,0:T(8,128)(2,1)S(1)} %get-tuple-element.95, bf16[512,1792]{1,0:T(8,128)(2,1)S(1)} %bitcast.32), kind=kOutput, calls=%fused_computation.2 | convolution fusion | flops 942276608 | bytes 6029312 | tf_op jit(solution)/shard_map/dot_general | solution.py:450
  128.9 17.3 %all-to-all-done.1.parts_ref = bf16[64,8,1920]{2,1,0:T(8,128)(2,1)S(1)} async-done(((bf16[64,8,1920]{2,1,0:T(8,128)(2,1)}), bf16[64,8,1920]{2,1,0:T(8,128)(2,1)S(1)}, u32[]{:S(2)}, u32[]{:S(2)}) %all-to-all-start.1) | async-done | bytes 1966112 | tf_op jit(solution)/shard_map/all_to_all | solution.py:482
  146.2 0.9 shard_map.120
  (9 shorter events, 0.0 us)
Async XLA Ops:
  0.6 41.4 %collective-permute-start.7 = (bf16[512,1792]{1,0:T(8,128)(2,1)}, bf16[512,1792]{1,0:T(8,128)(2,1)S(1)}, u32[]{:S(2)}, u32[]{:S(2)}) collective-permute-start(bf16[512,1792]{1,0:T(8,128)(2,1)} %bitcast.35), channel_id=1, source_target_pairs={{0,1},{1,0},{2,3},{3,2},{4,5},{5,4},{6,7},{7,6},{8,9},{9,8},{10,11... | collective-permute-start | bytes 5505032 | tf_op jit(solution)/shard_map/ppermute | solution.py:446
  0.7 41.8 %collective-permute-start.8 = (bf16[512,1792]{1,0:T(8,128)(2,1)}, bf16[512,1792]{1,0:T(8,128)(2,1)}, u32[]{:S(2)}, u32[]{:S(2)}) collective-permute-start(bf16[512,1792]{1,0:T(8,128)(2,1)} %bitcast.38), channel_id=1, source_target_pairs={{0,1},{1,0},{2,3},{3,2},{4,5},{5,4},{6,7},{7,6},{8,9},{9,8},{10,11... | collective-permute-start | bytes 5505032 | tf_op jit(solution)/shard_map/ppermute | solution.py:446
  1.2 44.3 %collective-permute-start.9 = (bf16[512,1792]{1,0:T(8,128)(2,1)}, bf16[512,1792]{1,0:T(8,128)(2,1)}, u32[]{:S(2)}, u32[]{:S(2)}) collective-permute-start(bf16[512,1792]{1,0:T(8,128)(2,1)} %bitcast.41), channel_id=1, source_target_pairs={{0,1},{1,0},{2,3},{3,2},{4,5},{5,4},{6,7},{7,6},{8,9},{9,8},{10,11... | collective-permute-start | bytes 5505032 | tf_op jit(solution)/shard_map/ppermute | solution.py:446
  14.6 7.3 %collective-permute-start = (bf16[4,8,3712]{2,1,0:T(8,128)(2,1)S(1)}, bf16[4,8,3712]{2,1,0:T(8,128)(2,1)S(1)}, u32[]{:S(2)}, u32[]{:S(2)}) collective-permute-start(bf16[4,8,3712]{2,1,0:T(8,128)(2,1)S(1)} %all_to_all.10.refs_0_), channel_id=1, source_target_pairs={{0,2},{1,9},{2,4},{3,11},{4,6},{5,13},{6,0},{7,15},{8,10},{9,17},{... | collective-permute-start | bytes 712712 | tf_op jit(solution)/shard_map/ppermute | solution.py:438
  16.1 9.4 %collective-permute-start.1 = (bf16[4,8,3712]{2,1,0:T(8,128)(2,1)S(1)}, bf16[4,8,3712]{2,1,0:T(8,128)(2,1)S(1)}, u32[]{:S(2)}, u32[]{:S(2)}) collective-permute-start(bf16[4,8,3712]{2,1,0:T(8,128)(2,1)S(1)} %all_to_all.10.refs_0_), channel_id=1, source_target_pairs={{0,4},{1,17},{2,6},{3,19},{4,0},{5,21},{6,2},{7,23},{8,12},{9,25},... | collective-permute-start | bytes 712712 | tf_op jit(solution)/shard_map/ppermute | solution.py:438
  21.9 6.1 %collective-permute-start.2 = (bf16[4,8,3712]{2,1,0:T(8,128)(2,1)S(1)}, bf16[4,8,3712]{2,1,0:T(8,128)(2,1)S(1)}, u32[]{:S(2)}, u32[]{:S(2)}) collective-permute-start(bf16[4,8,3712]{2,1,0:T(8,128)(2,1)S(1)} %all_to_all.10.refs_0_), channel_id=1, source_target_pairs={{0,6},{1,25},{2,0},{3,27},{4,2},{5,29},{6,4},{7,31},{8,14},{9,1},{... | collective-permute-start | bytes 712712 | tf_op jit(solution)/shard_map/ppermute | solution.py:438
  28.1 13.9 %collective-permute-start.3 = (bf16[4,32,1920]{2,1,0:T(8,128)(2,1)S(1)}, bf16[4,32,1920]{2,1,0:T(8,128)(2,1)S(1)}, u32[]{:S(2)}, u32[]{:S(2)}) collective-permute-start(bf16[4,32,1920]{2,1,0:T(8,128)(2,1)S(1)} %get-tuple-element.54.refs_0_), channel_id=1, source_target_pairs={{0,8},{1,3},{2,10},{3,5},{4,12},{5,7},{6,14},{7,1},{8,16},{9,11},{... | collective-permute-start | bytes 1474568 | tf_op jit(solution)/shard_map/ppermute | solution.py:438
  30.1 8.5 %collective-permute-start.5 = (bf16[4,32,1792]{2,1,0:T(8,128)(2,1)S(1)}, bf16[4,32,1792]{2,1,0:T(8,128)(2,1)S(1)}, u32[]{:S(2)}, u32[]{:S(2)}) collective-permute-start(bf16[4,32,1792]{2,1,0:T(8,128)(2,1)S(1)} %get-tuple-element.55.refs_1_), channel_id=1, source_target_pairs={{0,24},{1,7},{2,26},{3,1},{4,28},{5,3},{6,30},{7,5},{8,0},{9,15},{... | collective-permute-start | bytes 1376264 | tf_op jit(solution)/shard_map/ppermute | solution.py:438
  38.6 18.7 %collective-permute-start.10 = (bf16[4,32,1920]{2,1,0:T(8,128)(2,1)S(1)}, bf16[4,32,1920]{2,1,0:T(8,128)(2,1)S(1)}, u32[]{:S(2)}, u32[]{:S(2)}) collective-permute-start(bf16[4,32,1920]{2,1,0:T(8,128)(2,1)S(1)} %get-tuple-element.54.refs_0_), channel_id=1, source_target_pairs={{0,24},{1,7},{2,26},{3,1},{4,28},{5,3},{6,30},{7,5},{8,0},{9,15},{... | collective-permute-start | bytes 1474568 | tf_op jit(solution)/shard_map/ppermute | solution.py:438
  42.0 19.5 %collective-permute-start.4 = (bf16[4,32,1920]{2,1,0:T(8,128)(2,1)S(1)}, bf16[4,32,1920]{2,1,0:T(8,128)(2,1)S(1)}, u32[]{:S(2)}, u32[]{:S(2)}) collective-permute-start(bf16[4,32,1920]{2,1,0:T(8,128)(2,1)S(1)} %collective-permute-done.3.refs_0_), channel_id=1, source_target_pairs={{0,8},{1,3},{2,10},{3,5},{4,12},{5,7},{6,14},{7,1},{8,16},{9,11},{... | collective-permute-start | bytes 1474568 | tf_op jit(solution)/shard_map/ppermute | solution.py:438
  42.0 3.5 %copy-start.4 = (bf16[512,1792]{1,0:T(8,128)(2,1)}, bf16[512,1792]{1,0:T(8,128)(2,1)S(1)}, u32[]{:S(2)}) copy-start(bf16[512,1792]{1,0:T(8,128)(2,1)S(1)} %collective-permute-done.7.refs_3_.refs_2_) | copy-start | bytes 5505028
  42.0 15.2 %collective-permute-start.11 = (bf16[4,32,1792]{2,1,0:T(8,128)(2,1)S(1)}, bf16[4,32,1792]{2,1,0:T(8,128)(2,1)S(1)}, u32[]{:S(2)}, u32[]{:S(2)}) collective-permute-start(bf16[4,32,1792]{2,1,0:T(8,128)(2,1)S(1)} %get-tuple-element.55.refs_1_), channel_id=1, source_target_pairs={{0,8},{1,3},{2,10},{3,5},{4,12},{5,7},{6,14},{7,1},{8,16},{9,11},{... | collective-permute-start | bytes 1376264 | tf_op jit(solution)/shard_map/ppermute | solution.py:438
  42.5 18.9 %collective-permute-start.6 = (bf16[4,32,1792]{2,1,0:T(8,128)(2,1)S(1)}, bf16[4,32,1792]{2,1,0:T(8,128)(2,1)S(1)}, u32[]{:S(2)}, u32[]{:S(2)}) collective-permute-start(bf16[4,32,1792]{2,1,0:T(8,128)(2,1)S(1)} %collective-permute-done.5.refs_3_), channel_id=1, source_target_pairs={{0,24},{1,7},{2,26},{3,1},{4,28},{5,3},{6,30},{7,5},{8,0},{9,15},{... | collective-permute-start | bytes 1376264 | tf_op jit(solution)/shard_map/ppermute | solution.py:438
  64.0 9.3 %collective-permute-start.12 = (bf16[128,768]{1,0:T(8,128)(2,1)}, bf16[128,768]{1,0:T(8,128)(2,1)S(1)}, u32[]{:S(2)}, u32[]{:S(2)}) collective-permute-start(bf16[128,768]{1,0:T(8,128)(2,1)} %get-tuple-element.83), channel_id=1, source_target_pairs={{0,32},{32,64},{64,96},{96,0},{1,33},{33,65},{65,97},{97,1},{2,34}... | collective-permute-start | bytes 589832 | tf_op jit(solution)/shard_map/ppermute | solution.py:442
  64.7 8.6 %collective-permute-start.13 = (bf16[128,768]{1,0:T(8,128)(2,1)}, bf16[128,768]{1,0:T(8,128)(2,1)S(1)}, u32[]{:S(2)}, u32[]{:S(2)}) collective-permute-start(bf16[128,768]{1,0:T(8,128)(2,1)} %get-tuple-element.84), channel_id=1, source_target_pairs={{0,64},{32,96},{64,0},{96,32},{1,65},{33,97},{65,1},{97,33},{2,66}... | collective-permute-start | bytes 589832 | tf_op jit(solution)/shard_map/ppermute | solution.py:442
  66.7 7.5 %collective-permute-start.14 = (bf16[128,768]{1,0:T(8,128)(2,1)}, bf16[128,768]{1,0:T(8,128)(2,1)S(1)}, u32[]{:S(2)}, u32[]{:S(2)}) collective-permute-start(bf16[128,768]{1,0:T(8,128)(2,1)} %get-tuple-element.85), channel_id=1, source_target_pairs={{0,96},{32,0},{64,32},{96,64},{1,97},{33,1},{65,33},{97,65},{2,98}... | collective-permute-start | bytes 589832 | tf_op jit(solution)/shard_map/ppermute | solution.py:442
  75.4 6.9 %collective-permute-start.15 = (bf16[128,768]{1,0:T(8,128)(2,1)S(1)}, bf16[128,768]{1,0:T(8,128)(2,1)S(1)}, u32[]{:S(2)}, u32[]{:S(2)}) collective-permute-start(bf16[128,768]{1,0:T(8,128)(2,1)S(1)} %get-tuple-element.87.refs_0_), channel_id=1, source_target_pairs={{0,32},{32,64},{64,96},{96,0},{1,33},{33,65},{65,97},{97,1},{2,34}... | collective-permute-start | bytes 589832 | tf_op jit(solution)/shard_map/ppermute | solution.py:442
  75.7 9.6 %collective-permute-start.16 = (bf16[128,768]{1,0:T(8,128)(2,1)S(1)}, bf16[128,768]{1,0:T(8,128)(2,1)S(1)}, u32[]{:S(2)}, u32[]{:S(2)}) collective-permute-start(bf16[128,768]{1,0:T(8,128)(2,1)S(1)} %get-tuple-element.87.refs_0_), channel_id=1, source_target_pairs={{0,64},{32,96},{64,0},{96,32},{1,65},{33,97},{65,1},{97,33},{2,66}... | collective-permute-start | bytes 589832 | tf_op jit(solution)/shard_map/ppermute | solution.py:442
  79.5 5.8 %collective-permute-start.17 = (bf16[128,768]{1,0:T(8,128)(2,1)S(1)}, bf16[128,768]{1,0:T(8,128)(2,1)S(1)}, u32[]{:S(2)}, u32[]{:S(2)}) collective-permute-start(bf16[128,768]{1,0:T(8,128)(2,1)S(1)} %get-tuple-element.87.refs_0_), channel_id=1, source_target_pairs={{0,96},{32,0},{64,32},{96,64},{1,97},{33,1},{65,33},{97,65},{2,98}... | collective-permute-start | bytes 589832 | tf_op jit(solution)/shard_map/ppermute | solution.py:442
  85.3 0.9 copy-start
  87.6 4.0 %copy-start.2 = (bf16[4,128,1792]{2,1,0:T(8,128)(2,1)S(1)}, bf16[4,128,1792]{2,1,0:T(8,128)(2,1)}, u32[]{:S(2)}) copy-start(bf16[4,128,1792]{2,1,0:T(8,128)(2,1)} %get-tuple-element.96) | copy-start | bytes 5505028
  91.6 25.0 %collective-permute-start.20 = (bf16[512,1792]{1,0:T(8,128)(2,1)}, bf16[512,1792]{1,0:T(8,128)(2,1)}, u32[]{:S(2)}, u32[]{:S(2)}) collective-permute-start(bf16[512,1792]{1,0:T(8,128)(2,1)} %convolution_convert_fusion), channel_id=1, source_target_pairs={{0,1},{1,0},{2,3},{3,2},{4,5},{5,4},{6,7},{7,6},{8,9},{9,8},{10,11... | collective-permute-start | bytes 5505032 | tf_op jit(solution)/shard_map/ppermute | solution.py:446
  94.0 27.2 %collective-permute-start.19 = (bf16[512,1792]{1,0:T(8,128)(2,1)}, bf16[512,1792]{1,0:T(8,128)(2,1)}, u32[]{:S(2)}, u32[]{:S(2)}) collective-permute-start(bf16[512,1792]{1,0:T(8,128)(2,1)} %convolution_convert_fusion.1), channel_id=1, source_target_pairs={{0,1},{1,0},{2,3},{3,2},{4,5},{5,4},{6,7},{7,6},{8,9},{9,8},{10,11... | collective-permute-start | bytes 5505032 | tf_op jit(solution)/shard_map/ppermute | solution.py:446
  96.9 3.2 %copy-start.1 = (bf16[4,128,128]{2,1,0:T(8,128)(2,1)S(1)}, bf16[4,128,128]{2,1,0:T(8,128)(2,1)}, u32[]{:S(2)}) copy-start(bf16[4,128,128]{2,1,0:T(8,128)(2,1)} %get-tuple-element.86.refs_4_) | copy-start | bytes 393220
  96.9 28.2 %collective-permute-start.18 = (bf16[512,1792]{1,0:T(8,128)(2,1)}, bf16[512,1792]{1,0:T(8,128)(2,1)}, u32[]{:S(2)}, u32[]{:S(2)}) collective-permute-start(bf16[512,1792]{1,0:T(8,128)(2,1)} %convolution_convert_fusion.2), channel_id=1, source_target_pairs={{0,1},{1,0},{2,3},{3,2},{4,5},{5,4},{6,7},{7,6},{8,9},{9,8},{10,11... | collective-permute-start | bytes 5505032 | tf_op jit(solution)/shard_map/ppermute | solution.py:446
  105.6 40.6 %all-to-all-start.1 = ((bf16[64,8,1920]{2,1,0:T(8,128)(2,1)}), bf16[64,8,1920]{2,1,0:T(8,128)(2,1)S(1)}, u32[]{:S(2)}, u32[]{:S(2)}) async-start(bf16[64,8,1920]{2,1,0:T(8,128)(2,1)} %bitcast.28), calls=%async_computation.1 | async-start | bytes 3932160 | tf_op jit(solution)/shard_map/all_to_all | solution.py:482
  116.6 4.6 %copy-start.3 = (bf16[4,128,1792]{2,1,0:T(8,128)(2,1)S(1)}, bf16[4,128,1792]{2,1,0:T(8,128)(2,1)}, u32[]{:S(2)}) copy-start(bf16[4,128,1792]{2,1,0:T(8,128)(2,1)} %get-tuple-element.96) | copy-start | bytes 5505028

commit v4 on v3

--- a/solution.py
+++ b/solution.py
@@ -15,7 +15,7 @@
 SIDE = 4
 FAR = (1, 3, 0, 2)
 PLANE = ("z", "x", "core")
-TORUS = ("ep", "z", "x")
+TORUS = ("ep", "x", "z")
 
 
 def params(mib):
@@ -227,7 +227,7 @@
 
 
 def middle(plane_ref, *refs):
-    parts, meta_ref, out_ref, route_ref = refs[:SIDE], *refs[SIDE:]
+    parts, meta_ref, out_ref, scaled_ref, route_ref = refs[:SIDE], *refs[SIDE:]
     rows = out_ref.shape[0]
     meta = meta_ref[...].reshape(rows, LANES).astype(F32)
     low = first_half(rows)
@@ -244,9 +244,10 @@
         hidden = (act * upper).astype(BF).astype(F32)
         back = factor * reverse
         d_gate = back * upper * sigma * (1.0 + gate * (1.0 - sigma))
-        at = 3 * side * LANES
-        for n, val in enumerate((d_gate, back * act, factor * hidden)):
-            out_ref[:, at + n * LANES:at + (n + 1) * LANES] = val.astype(BF)
+        for n, val in enumerate((d_gate, back * act)):
+            at = (2 * side + n) * LANES
+            out_ref[:, at:at + LANES] = val.astype(BF)
+        scaled_ref[:, side * LANES:(side + 1) * LANES] = (factor * hidden).astype(BF)
         prod = prod + hidden * reverse
     term_a = jnp.sum(jnp.where(low, prod, 0.0), axis=1, keepdims=True)
     term_b = jnp.sum(jnp.where(low, 0.0, prod), axis=1, keepdims=True)
@@ -264,9 +265,9 @@
             in_specs=[pl.BlockSpec((rows, width), lambda i, s: (0, 0))]
             + in_core(SIDE - 1)
             + [pl.BlockSpec((1, rows, LANES), lambda i, s: (s[0], 0, 0))],
-            out_specs=in_core(2),
+            out_specs=in_core(3),
         ),
-        out_shape=[pltpu.VMEM((rows, width), BF), pltpu.VMEM((rows, LANES), BF)],
+        out_shape=[pltpu.VMEM((rows, w), BF) for w in (4 * LANES, 2 * LANES, LANES)],
         compiler_params=params(6),
     )(plane, far_off(parts[0]), *map(near_core, parts[1:]), far_off(meta))
 
@@ -294,28 +295,30 @@
 
 
 def widen(plane_ref, *refs):
-    acts, meta_ref, outs = refs[:SIDE], refs[SIDE], refs[SIDE + 1:]
+    acts, scales, meta_ref, outs = refs[:SIDE], refs[SIDE:-7], refs[-7], refs[-6:]
     rows = acts[0].shape[0]
-    for k, ref in enumerate(acts):
+    for k in range(SIDE):
         home = (plane_ref[0] - k) & 3
-        vals = dense(ref[...].astype(F32), meta_ref[home].astype(F32), range(6))
+        meta = meta_ref[home].astype(F32)
+        vals = dense(acts[k][...].astype(F32), meta, range(4))
+        vals += dense(scales[k][...].astype(F32), meta, range(2))
         for out, val in zip(outs, vals):
             out[pl.ds(pl.multiple_of(home * rows, rows), rows), :] = val
 
 
-def widen_call(plane, acts, meta):
+def widen_call(plane, acts, scales, meta):
     rows = acts[0].shape[0]
     return pl.pallas_call(
         widen,
         grid_spec=pltpu.PrefetchScalarGridSpec(
             num_scalar_prefetch=1,
             grid=(1,),
-            in_specs=in_core(SIDE + 1),
+            in_specs=in_core(2 * SIDE + 1),
             out_specs=in_core(6),
         ),
         out_shape=[pltpu.VMEM((SIDE * rows, COLS), BF)] * 6,
         compiler_params=params(8),
-    )(plane, *map(near_core, (*acts, meta)))
+    )(plane, *map(near_core, (*acts, *scales, meta)))
 
 
 def goals(z, x, core):
@@ -324,7 +327,7 @@
         far, close = FAR[b // SIDE], b % SIDE
         by_z = jnp.where(core == 0, far, close)
         by_x = jnp.where(core == 0, close, far)
-        spots.append(((z - by_z) & 3) * SIDE + ((x - by_x) & 3))
+        spots.append(((x - by_x) & 3) * SIDE + ((z - by_z) & 3))
     return spots
 
 
@@ -353,7 +356,7 @@
             sort_ref[spot, width:width + LANES] = meta[at:at + 8]
             sort_ref[spot, width + LANES:] = route[at:at + 8]
     moved = sort_ref[:, :width], sort_ref[:, width:width + LANES]
-    for n, val in enumerate(dense(*moved, (0, 1, 3, 4))):
+    for n, val in enumerate(dense(*moved, range(4))):
         wide_ref[:, n * COLS:(n + 1) * COLS] = val
     out_ref[:, :, cuts[-1]] = sort_ref[:, width + LANES:].astype(BF).reshape(lead, rows, LANES)
     stores[-1].start()
@@ -382,7 +385,7 @@
             scratch_shapes=[
                 pltpu.VMEM((lead * rows, 4 * COLS), BF),
                 pltpu.VMEM(out, BF),
-                pltpu.VMEM((lead * rows, 8 * LANES), F32),
+                pltpu.VMEM((lead * rows, 6 * LANES), F32),
                 pltpu.SemaphoreType.DMA((deep // chunk + 1,)),
             ],
         ),
@@ -475,20 +478,21 @@
     state = pre_call(plane, [x_1, x_3, y_1, y_3], flipped, dot_n, 0, SIDE, state)
     *parts, x_rows, y_rows, meta_rows = pre_call(plane, [x_2, y_2], flipped, dot_n, 3, SIDE, state)
     parts = [parts[0]] + [turn(parts[k], k) for k in range(1, SIDE)]
-    done, route = middle_call(plane, parts, meta_rows)
+    done, scaled, route = middle_call(plane, parts, meta_rows)
     acts = [done] + [turn(done, k) for k in range(1, SIDE)]
+    scales = [scaled] + [turn(scaled, k) for k in range(1, SIDE)]
     pair_mats = load_call(own_mats[:2] + their_mats[:2])
     sent = terms_call((plane, *spot), acts, meta_rows, route, pair_mats)
     got = lax.all_to_all(sent.reshape(-1, tok_rows, lap), TORUS, 0, 0, tiled=True)
-    wides = widen_call(plane, acts, meta_rows)
+    wides = widen_call(plane, acts, scales, meta_rows)
     token_grad, route_sum = finish_call(got, width)
     route_grad = route_sum.T
     x_rows, y_rows = (r.reshape(-1, width) for r in (x_rows, y_rows))
     grads = []
     for m in range(3):
         rows = y_rows if m == 2 else x_rows
-        theirs = swap(contract_rows(wides[3 + m], rows).astype(BF))
-        mine = contract_rows(wides[m], rows) + theirs.astype(F32)
+        theirs = swap(contract_rows(wides[(2, 3, 5)[m]], rows).astype(BF))
+        mine = contract_rows(wides[(0, 1, 4)[m]], rows) + theirs.astype(F32)
         grads.append(mine.astype(BF).reshape(gate_weight.shape))
     return (token_grad, route_grad, *grads)
 

time: 148 us -> 147 us (level)
  waiting for transfers between devices: 43.7 us -> 39.9 us
  starting transfers between devices: 36.7 us -> 40.3 us
    ppermute x6 -> x9, starting transfers between devices: 7.72 us -> 13.1 us  [turn(): return lax.ppermute(arr, 'ep', [(i, (i + by) % SIDE) for i in range(SIDE)])]
    ppermute x6 -> x9, waiting for transfers between devices: 12.4 us -> 9.67 us  [turn(): return lax.ppermute(arr, 'ep', [(i, (i + by) % SIDE) for i in range(SIDE)])]
    all_to_all x1, starting transfers between devices: 10.9 us -> 9.23 us  [local(): lax.all_to_all(sent.reshape(-1, tok_rows, lap), TORUS, 0, 0, tiled=True)]
  transfers between devices with their start and end apart: 22 -> 25, of which waited for: 9 -> 8; matrix products, arithmetic and copies ran while one was open for 12% -> 12% of each run, Pallas kernels for 18% -> 18%
where the time goes in v4:
time: 147 us
  starting transfers between devices  40.3 us (27%)
  waiting for transfers between devices  39.9 us (27%)
  Pallas kernels  32.4 us (22%)
  matrix products  21.1 us (14%)
  blocking collectives  11.6 us (8%)
    dot_general x6, matrix products, contract_rows(): lax.dot_general(left, right, (((0,), (0,)), ((), ())), preferred_element_...  21.1 us
    ppermute x9, starting transfers between devices, shift(): return lax.ppermute(arr, PLANE, pairs)  16.9 us
    all_to_all x1, waiting for transfers between devices, local(): lax.all_to_all(sent.reshape(-1, tok_rows, lap), TORUS, 0, 0, tiled=True)  16.2 us
    ppermute x9, waiting for transfers between devices, shift(): return lax.ppermute(arr, PLANE, pairs)  13.9 us
    ppermute x9, starting transfers between devices, turn(): return lax.ppermute(arr, 'ep', [(i, (i + by) % SIDE) for i in range(SIDE)])  13.1 us
    all_to_all x1, blocking collectives, local(): own = lax.all_to_all(send, 'ep', 0, 0, tiled=True)  11.6 us
    pallas_call x3, Pallas kernels, pre_call(): pl.pallas_call(pre_acts(count, first * rows, width, multiply), grid_spec=...  11.3 us
    ppermute x9, waiting for transfers between devices, turn(): return lax.ppermute(arr, 'ep', [(i, (i + by) % SIDE) for i in range(SIDE)])  9.67 us
  transfers between devices with their start and end apart: 25, of which 8 were waited for; matrix products, arithmetic and copies ran while one was open for 12% of the time, Pallas kernels for 18%

profile of v4, /device:TPU:0, one launch (start us, length us, event | category | flops | bytes accessed | tf_op | source)
XLA Modules:
  0.0 147.0 jit_solution(5111158248992044324)
XLA Ops:
  0.6 0.1 collective-permute-start.7
  0.7 0.5 collective-permute-start.8
  1.2 0.1 collective-permute-start.9
  1.3 1.7 %shard_map.110 = bf16[4,8,3712]{2,1,0:T(8,128)(2,1)} custom-call(s32[1]{0:T(128)} %bitcast.plane_ref, s32[1]{0:T(128)} %bitcast.1.z_ref, s32[1]{0:T(128)} %bitcast.2.chip_ref.x_ref, s32[1]{0:T(128)} %bitcast.3.core_ref, bf16[8,7168]{1,0:T(8,128)(2,1)} %tok_ref.1, bf16[8,7168]{1,0:T(8,128)(2,1)} %cot_ref.1, s32[2,8]{1,0:T(2,128)} %bitcast.43, ...), custom_call_target="tpu_custom_call" | custom-call | tf_op jit(solution)/shard_map/pallas_call | solution.py:79
  3.0 11.6 %all_to_all.10.refs_0_ = bf16[4,8,3712]{2,1,0:T(8,128)(2,1)S(1)} all-to-all(bf16[4,8,3712]{2,1,0:T(8,128)(2,1)} %shard_map.110), channel_id=1, replica_groups=mesh['ep'=4,'z'=4,'x'=4,'core'=2] {'ep'}, dimensions={0} | all-to-all | bytes 475136 | tf_op jit(solution)/shard_map/all_to_all | solution.py:466
  14.6 1.5 %collective-permute-start = (bf16[4,8,3712]{2,1,0:T(8,128)(2,1)S(1)}, bf16[4,8,3712]{2,1,0:T(8,128)(2,1)S(1)}, u32[]{:S(2)}, u32[]{:S(2)}) collective-permute-start(bf16[4,8,3712]{2,1,0:T(8,128)(2,1)S(1)} %all_to_all.10.refs_0_), channel_id=1, source_target_pairs={{0,2},{1,9},{2,4},{3,11},{4,6},{5,13},{6,0},{7,15},{8,10},{9,17},{... | collective-permute-start | bytes 712712 | tf_op jit(solution)/shard_map/ppermute | solution.py:441
  16.1 2.7 %collective-permute-start.1 = (bf16[4,8,3712]{2,1,0:T(8,128)(2,1)S(1)}, bf16[4,8,3712]{2,1,0:T(8,128)(2,1)S(1)}, u32[]{:S(2)}, u32[]{:S(2)}) collective-permute-start(bf16[4,8,3712]{2,1,0:T(8,128)(2,1)S(1)} %all_to_all.10.refs_0_), channel_id=1, source_target_pairs={{0,4},{1,17},{2,6},{3,19},{4,0},{5,21},{6,2},{7,23},{8,12},{9,25},... | collective-permute-start | bytes 712712 | tf_op jit(solution)/shard_map/ppermute | solution.py:441
  18.8 3.1 %collective-permute-done.refs_1_ = bf16[4,8,3712]{2,1,0:T(8,128)(2,1)S(1)} collective-permute-done((bf16[4,8,3712]{2,1,0:T(8,128)(2,1)S(1)}, bf16[4,8,3712]{2,1,0:T(8,128)(2,1)S(1)}, u32[]{:S(2)}, u32[]{:S(2)}) %collective-permute-start) | collective-permute-done | bytes 237600 | tf_op jit(solution)/shard_map/ppermute | solution.py:441
  21.9 1.5 %collective-permute-start.2 = (bf16[4,8,3712]{2,1,0:T(8,128)(2,1)S(1)}, bf16[4,8,3712]{2,1,0:T(8,128)(2,1)S(1)}, u32[]{:S(2)}, u32[]{:S(2)}) collective-permute-start(bf16[4,8,3712]{2,1,0:T(8,128)(2,1)S(1)} %all_to_all.10.refs_0_), channel_id=1, source_target_pairs={{0,6},{1,25},{2,0},{3,27},{4,2},{5,29},{6,4},{7,31},{8,14},{9,1},{... | collective-permute-start | bytes 712712 | tf_op jit(solution)/shard_map/ppermute | solution.py:441
  23.5 2.0 %collective-permute-done.1.refs_2_ = bf16[4,8,3712]{2,1,0:T(8,128)(2,1)S(1)} collective-permute-done((bf16[4,8,3712]{2,1,0:T(8,128)(2,1)S(1)}, bf16[4,8,3712]{2,1,0:T(8,128)(2,1)S(1)}, u32[]{:S(2)}, u32[]{:S(2)}) %collective-permute-start.1) | collective-permute-done | bytes 237600 | tf_op jit(solution)/shard_map/ppermute | solution.py:441
  25.5 2.6 %collective-permute-done.2.refs_3_ = bf16[4,8,3712]{2,1,0:T(8,128)(2,1)S(1)} collective-permute-done((bf16[4,8,3712]{2,1,0:T(8,128)(2,1)S(1)}, bf16[4,8,3712]{2,1,0:T(8,128)(2,1)S(1)}, u32[]{:S(2)}, u32[]{:S(2)}) %collective-permute-start.2) | collective-permute-done | bytes 237600 | tf_op jit(solution)/shard_map/ppermute | solution.py:441
  28.0 0.1 shard_map.111
  28.1 2.0 %collective-permute-start.3 = (bf16[4,32,1920]{2,1,0:T(8,128)(2,1)S(1)}, bf16[4,32,1920]{2,1,0:T(8,128)(2,1)S(1)}, u32[]{:S(2)}, u32[]{:S(2)}) collective-permute-start(bf16[4,32,1920]{2,1,0:T(8,128)(2,1)S(1)} %get-tuple-element.55.refs_0_), channel_id=1, source_target_pairs={{0,8},{1,3},{2,10},{3,5},{4,12},{5,7},{6,14},{7,1},{8,16},{9,11},{... | collective-permute-start | bytes 1474568 | tf_op jit(solution)/shard_map/ppermute | solution.py:441
  30.1 2.2 %collective-permute-start.5 = (bf16[4,32,1792]{2,1,0:T(8,128)(2,1)S(1)}, bf16[4,32,1792]{2,1,0:T(8,128)(2,1)S(1)}, u32[]{:S(2)}, u32[]{:S(2)}) collective-permute-start(bf16[4,32,1792]{2,1,0:T(8,128)(2,1)S(1)} %get-tuple-element.56.refs_1_), channel_id=1, source_target_pairs={{0,24},{1,7},{2,26},{3,1},{4,28},{5,3},{6,30},{7,5},{8,0},{9,15},{... | collective-permute-start | bytes 1376264 | tf_op jit(solution)/shard_map/ppermute | solution.py:441
  32.3 6.3 %collective-permute-done.5.refs_3_ = bf16[4,32,1792]{2,1,0:T(8,128)(2,1)S(1)} collective-permute-done((bf16[4,32,1792]{2,1,0:T(8,128)(2,1)S(1)}, bf16[4,32,1792]{2,1,0:T(8,128)(2,1)S(1)}, u32[]{:S(2)}, u32[]{:S(2)}) %collective-permute-start.5) | collective-permute-done | bytes 458784 | tf_op jit(solution)/shard_map/ppermute | solution.py:441
  38.6 3.4 %collective-permute-start.10 = (bf16[4,32,1920]{2,1,0:T(8,128)(2,1)S(1)}, bf16[4,32,1920]{2,1,0:T(8,128)(2,1)S(1)}, u32[]{:S(2)}, u32[]{:S(2)}) collective-permute-start(bf16[4,32,1920]{2,1,0:T(8,128)(2,1)S(1)} %get-tuple-element.55.refs_0_), channel_id=1, source_target_pairs={{0,24},{1,7},{2,26},{3,1},{4,28},{5,3},{6,30},{7,5},{8,0},{9,15},{... | collective-permute-start | bytes 1474568 | tf_op jit(solution)/shard_map/ppermute | solution.py:441
  42.0 0.0 collective-permute-start.4
  42.0 0.0 collective-permute-done.7.refs_3_.refs_2_
  42.0 0.0 copy-start.4
  42.0 0.5 collective-permute-start.11
  42.5 0.0 collective-permute-done.8.refs_4_.refs_3_
  42.5 3.0 %collective-permute-start.6 = (bf16[4,32,1792]{2,1,0:T(8,128)(2,1)S(1)}, bf16[4,32,1792]{2,1,0:T(8,128)(2,1)S(1)}, u32[]{:S(2)}, u32[]{:S(2)}) collective-permute-start(bf16[4,32,1792]{2,1,0:T(8,128)(2,1)S(1)} %collective-permute-done.5.refs_3_), channel_id=1, source_target_pairs={{0,24},{1,7},{2,26},{3,1},{4,28},{5,3},{6,30},{7,5},{8,0},{9,15},{... | collective-permute-start | bytes 1376264 | tf_op jit(solution)/shard_map/ppermute | solution.py:441
  45.5 4.2 %shard_map.112 = (bf16[512,1792]{1,0:T(8,128)(2,1)S(1)}, bf16[512,1792]{1,0:T(8,128)(2,1)S(1)}, bf16[512,1792]{1,0:T(8,128)(2,1)S(1)}, bf16[512,1792]{1,0:T(8,12...) custom-call(bf16[512,1792]{1,0:T(8,128)(2,1)} %bitcast.36, bf16[512,1792]{1,0:T(8,128)(2,1)} %bitcast.39, ...), custom_call_target="tpu_custom_call" | custom-call | tf_op jit(solution)/shard_map/pallas_call | solution.py:103
  49.8 4.6 %shard_map.114 = (bf16[128,768]{1,0:T(8,128)(2,1)}, bf16[128,768]{1,0:T(8,128)(2,1)}, bf16[128,768]{1,0:T(8,128)(2,1)}, bf16[128,768]{1,0:T(8,128)(2,1)}, bf16[4...) custom-call(s32[1]{0:T(128)} %bitcast.plane_ref, ...), custom_call_target="tpu_custom_call" | custom-call | tf_op jit(solution)/shard_map/pallas_call | solution.py:210
  54.3 2.9 %shard_map.113 = (bf16[1792,512]{1,0:T(8,128)(2,1)S(1)}, bf16[1792,512]{1,0:T(8,128)(2,1)S(1)}, bf16[1792,512]{1,0:T(8,128)(2,1)S(1)}, bf16[1792,512]{1,0:T(8,12...) custom-call(bf16[512,1792]{1,0:T(8,128)(2,1)S(1)} %get-tuple-element.57.refs_0_.refs_2_, ...), custom_call_target="tpu_custom_call" | custom-call | tf_op jit(solution)/shard_map/pallas_call | solution.py:120
  57.2 0.0 collective-permute-done.10.refs_1_
  57.2 4.2 %shard_map.115 = (bf16[128,768]{1,0:T(8,128)(2,1)}, bf16[128,768]{1,0:T(8,128)(2,1)}, bf16[128,768]{1,0:T(8,128)(2,1)}, bf16[128,768]{1,0:T(8,128)(2,1)}, bf16[4...) custom-call(s32[1]{0:T(128)} %bitcast.plane_ref, ...), custom_call_target="tpu_custom_call", output_to_operand_aliasing={{0}: (11, {}), {1}: (12, {}), {2}: (13, {}), {3}: (14, {}),... | custom-call | tf_op jit(solution)/shard_map/pallas_call | solution.py:210
  61.5 0.0 collective-permute-done.4.refs_0_
  61.5 2.6 %shard_map.116 = (bf16[128,768]{1,0:T(8,128)(2,1)}, bf16[128,768]{1,0:T(8,128)(2,1)}, bf16[128,768]{1,0:T(8,128)(2,1)}, bf16[128,768]{1,0:T(8,128)(2,1)}, bf16[4...) custom-call(s32[1]{0:T(128)} %bitcast.plane_ref, ...), custom_call_target="tpu_custom_call", output_to_operand_aliasing={{0}: (9, {}), {1}: (10, {}), {2}: (11, {}), {3}: (12, {}), ... | custom-call | tf_op jit(solution)/shard_map/pallas_call | solution.py:210
  64.1 0.6 collective-permute-start.12
  64.7 2.1 %collective-permute-start.13 = (bf16[128,768]{1,0:T(8,128)(2,1)}, bf16[128,768]{1,0:T(8,128)(2,1)S(1)}, u32[]{:S(2)}, u32[]{:S(2)}) collective-permute-start(bf16[128,768]{1,0:T(8,128)(2,1)} %get-tuple-element.85), channel_id=1, source_target_pairs={{0,64},{32,96},{64,0},{96,32},{1,65},{33,97},{65,1},{97,33},{2,66}... | collective-permute-start | bytes 589832 | tf_op jit(solution)/shard_map/ppermute | solution.py:445
  66.8 0.9 collective-permute-start.14
  67.6 5.7 %collective-permute-done.12.refs_1_ = bf16[128,768]{1,0:T(8,128)(2,1)S(1)} collective-permute-done((bf16[128,768]{1,0:T(8,128)(2,1)}, bf16[128,768]{1,0:T(8,128)(2,1)S(1)}, u32[]{:S(2)}, u32[]{:S(2)}) %collective-permute-start.12) | collective-permute-done | bytes 196640 | tf_op jit(solution)/shard_map/ppermute | solution.py:445
  73.3 0.9 collective-permute-done.14.refs_3_
  74.2 1.2 shard_map.117
  75.4 0.3 collective-permute-start.18
  75.7 0.6 collective-permute-start.15
  76.3 3.9 %collective-permute-start.16 = (bf16[128,512]{1,0:T(8,128)(2,1)S(1)}, bf16[128,512]{1,0:T(8,128)(2,1)S(1)}, u32[]{:S(2)}, u32[]{:S(2)}) collective-permute-start(bf16[128,512]{1,0:T(8,128)(2,1)S(1)} %get-tuple-element.88.refs_0_), channel_id=1, source_target_pairs={{0,64},{32,96},{64,0},{96,32},{1,65},{33,97},{65,1},{97,33},{2,66}... | collective-permute-start | bytes 393224 | tf_op jit(solution)/shard_map/ppermute | solution.py:445
  80.2 2.0 %collective-permute-start.17 = (bf16[128,512]{1,0:T(8,128)(2,1)S(1)}, bf16[128,512]{1,0:T(8,128)(2,1)S(1)}, u32[]{:S(2)}, u32[]{:S(2)}) collective-permute-start(bf16[128,512]{1,0:T(8,128)(2,1)S(1)} %get-tuple-element.88.refs_0_), channel_id=1, source_target_pairs={{0,96},{32,0},{64,32},{96,64},{1,97},{33,1},{65,33},{97,65},{2,98}... | collective-permute-start | bytes 393224 | tf_op jit(solution)/shard_map/ppermute | solution.py:445
  82.2 0.0 collective-permute-start.19
  82.2 0.0 collective-permute-done.18.refs_5_
  82.2 2.7 %collective-permute-start.20 = (bf16[128,256]{1,0:T(8,128)(2,1)S(1)}, bf16[128,256]{1,0:T(8,128)(2,1)S(1)}, u32[]{:S(2)}, u32[]{:S(2)}) collective-permute-start(bf16[128,256]{1,0:T(8,128)(2,1)S(1)} %get-tuple-element.96.refs_4_), channel_id=1, source_target_pairs={{0,96},{32,0},{64,32},{96,64},{1,97},{33,1},{65,33},{97,65},{2,98}... | collective-permute-start | bytes 196616 | tf_op jit(solution)/shard_map/ppermute | solution.py:445
  84.9 3.1 %collective-permute-done.19.refs_6_ = bf16[128,256]{1,0:T(8,128)(2,1)S(1)} collective-permute-done((bf16[128,256]{1,0:T(8,128)(2,1)S(1)}, bf16[128,256]{1,0:T(8,128)(2,1)S(1)}, u32[]{:S(2)}, u32[]{:S(2)}) %collective-permute-start.19) | collective-permute-done | bytes 65568 | tf_op jit(solution)/shard_map/ppermute | solution.py:445
  88.0 0.0 collective-permute-done.17.refs_3_
  88.0 0.9 copy-done
  88.9 1.3 shard_map.121
  90.2 0.0 copy-start.2
  90.2 4.0 %convolution_convert_fusion = bf16[512,1792]{1,0:T(8,128)(2,1)} fusion(bf16[512,512]{1,0:T(8,128)(2,1)S(1)} %get-tuple-element.104, bf16[512,1792]{1,0:T(8,128)(2,1)} %bitcast.33), kind=kOutput, calls=%fused_computation.3 | convolution fusion | flops 940441600 | bytes 4194304 | tf_op jit(solution)/shard_map/dot_general | solution.py:453
  94.2 0.0 collective-permute-start.23
  94.2 2.4 %convolution_convert_fusion.1 = bf16[512,1792]{1,0:T(8,128)(2,1)} fusion(bf16[512,512]{1,0:T(8,128)(2,1)S(1)} %get-tuple-element.101, bf16[512,1792]{1,0:T(8,128)(2,1)S(1)} %bitcast.29), kind=kOutput, calls=%fused_computation.4 | convolution fusion | flops 940441600 | bytes 4194304 | tf_op jit(solution)/shard_map/dot_general | solution.py:453
  96.6 0.5 collective-permute-start.22
  97.1 2.4 %convolution_convert_fusion.2 = bf16[512,1792]{1,0:T(8,128)(2,1)} fusion(bf16[512,512]{1,0:T(8,128)(2,1)S(1)} %get-tuple-element.99, bf16[512,1792]{1,0:T(8,128)(2,1)S(1)} %bitcast.30), kind=kOutput, calls=%fused_computation.5 | convolution fusion | flops 940441600 | bytes 4194304 | tf_op jit(solution)/shard_map/dot_general | solution.py:453
  99.5 0.0 collective-permute-start.21
  99.5 3.2 %shard_map.118 = (bf16[512,1792]{1,0:T(8,128)(2,1)S(1)}, bf16[512,1792]{1,0:T(8,128)(2,1)S(1)}, bf16[512,1792]{1,0:T(8,128)(2,1)S(1)}, bf16[512,1792]{1,0:T(8,128)(2,1)S(1)}) custom-call(bf16[512,1792]{1,0:T(8,128)(2,1)} %bitcast.37, bf16[512,1792]{1,0:T(8,128)(2,1)} %bitcast.40, bf16[512,1792]{1,0:T(8,128)(2,1)} %copy-done.4, ...), custom_call_target="tpu_custom_call" | custom-call | tf_op jit(solution)/shard_map/pallas_call | solution.py:103
  102.8 5.5 %shard_map.119 = bf16[4,128,1920]{2,1,0:T(8,128)(2,1)} custom-call(s32[1]{0:T(128)} %bitcast.plane_ref, s32[1]{0:T(128)} %bitcast.1.z_ref, s32[1]{0:T(128)} %bitcast.2.chip_ref.x_ref, s32[1]{0:T(128)} %bitcast.3.core_ref, bf16[128,512]{1,0:T(8,128)(2,1)S(1)} %get-tuple-element.88.refs_0_, bf16[128,512]{1,0:T(8,128)(2,1)S(1)} %collective-permute-done.15.refs_1_, ...), custom_call_target="tpu_custom_call" | custom-call | tf_op jit(solution)/shard_map/pallas_call | solution.py:378
  108.2 9.2 %all-to-all-start.1 = ((bf16[64,8,1920]{2,1,0:T(8,128)(2,1)}), bf16[64,8,1920]{2,1,0:T(8,128)(2,1)S(1)}, u32[]{:S(2)}, u32[]{:S(2)}) async-start(bf16[64,8,1920]{2,1,0:T(8,128)(2,1)} %bitcast.28), calls=%async_computation.1 | async-start | bytes 3932160 | tf_op jit(solution)/shard_map/all_to_all | solution.py:486
  117.5 0.0 collective-permute-done.23
  117.5 0.0 copy-start.3
  117.5 4.6 %add_convert_fusion = bf16[512,1792]{1,0:T(8,128)(2,1)} fusion(bf16[512,1792]{1,0:T(8,128)(2,1)} %collective-permute-done.23, bf16[512,512]{1,0:T(8,128)(2,1)S(1)} %get-tuple-element.102, bf16[512,1792]{1,0:T(8,128)(2,1)} %bitcast.34), kind=kOutput, calls=%fused_computation | convolution fusion | flops 942276608 | bytes 6029312 | tf_op jit(solution)/shard_map/dot_general | solution.py:453
  122.1 0.0 collective-permute-done.22
  122.1 3.9 %add_convert_fusion.1 = bf16[512,1792]{1,0:T(8,128)(2,1)} fusion(bf16[512,1792]{1,0:T(8,128)(2,1)} %collective-permute-done.22, bf16[512,512]{1,0:T(8,128)(2,1)S(1)} %get-tuple-element.100, bf16[512,1792]{1,0:T(8,128)(2,1)S(1)} %bitcast.31), kind=kOutput, calls=%fused_computation.1 | convolution fusion | flops 942276608 | bytes 6029312 | tf_op jit(solution)/shard_map/dot_general | solution.py:453
  126.0 3.9 %add_convert_fusion.2 = bf16[512,1792]{1,0:T(8,128)(2,1)} fusion(bf16[512,1792]{1,0:T(8,128)(2,1)} %collective-permute-done.21, bf16[512,512]{1,0:T(8,128)(2,1)S(1)} %get-tuple-element.97, bf16[512,1792]{1,0:T(8,128)(2,1)S(1)} %bitcast.32), kind=kOutput, calls=%fused_computation.2 | convolution fusion | flops 942276608 | bytes 6029312 | tf_op jit(solution)/shard_map/dot_general | solution.py:453
  129.9 16.2 %all-to-all-done.1.parts_ref = bf16[64,8,1920]{2,1,0:T(8,128)(2,1)S(1)} async-done(((bf16[64,8,1920]{2,1,0:T(8,128)(2,1)}), bf16[64,8,1920]{2,1,0:T(8,128)(2,1)S(1)}, u32[]{:S(2)}, u32[]{:S(2)}) %all-to-all-start.1) | async-done | bytes 1966112 | tf_op jit(solution)/shard_map/all_to_all | solution.py:486
  146.1 0.9 shard_map.120
  (15 shorter events, 0.0 us)
Async XLA Ops:
  0.6 41.4 %collective-permute-start.7 = (bf16[512,1792]{1,0:T(8,128)(2,1)}, bf16[512,1792]{1,0:T(8,128)(2,1)S(1)}, u32[]{:S(2)}, u32[]{:S(2)}) collective-permute-start(bf16[512,1792]{1,0:T(8,128)(2,1)} %bitcast.35), channel_id=1, source_target_pairs={{0,1},{1,0},{2,3},{3,2},{4,5},{5,4},{6,7},{7,6},{8,9},{9,8},{10,11... | collective-permute-start | bytes 5505032 | tf_op jit(solution)/shard_map/ppermute | solution.py:449
  0.7 41.8 %collective-permute-start.8 = (bf16[512,1792]{1,0:T(8,128)(2,1)}, bf16[512,1792]{1,0:T(8,128)(2,1)}, u32[]{:S(2)}, u32[]{:S(2)}) collective-permute-start(bf16[512,1792]{1,0:T(8,128)(2,1)} %bitcast.38), channel_id=1, source_target_pairs={{0,1},{1,0},{2,3},{3,2},{4,5},{5,4},{6,7},{7,6},{8,9},{9,8},{10,11... | collective-permute-start | bytes 5505032 | tf_op jit(solution)/shard_map/ppermute | solution.py:449
  1.2 44.3 %collective-permute-start.9 = (bf16[512,1792]{1,0:T(8,128)(2,1)}, bf16[512,1792]{1,0:T(8,128)(2,1)}, u32[]{:S(2)}, u32[]{:S(2)}) collective-permute-start(bf16[512,1792]{1,0:T(8,128)(2,1)} %bitcast.41), channel_id=1, source_target_pairs={{0,1},{1,0},{2,3},{3,2},{4,5},{5,4},{6,7},{7,6},{8,9},{9,8},{10,11... | collective-permute-start | bytes 5505032 | tf_op jit(solution)/shard_map/ppermute | solution.py:449
  14.6 7.3 %collective-permute-start = (bf16[4,8,3712]{2,1,0:T(8,128)(2,1)S(1)}, bf16[4,8,3712]{2,1,0:T(8,128)(2,1)S(1)}, u32[]{:S(2)}, u32[]{:S(2)}) collective-permute-start(bf16[4,8,3712]{2,1,0:T(8,128)(2,1)S(1)} %all_to_all.10.refs_0_), channel_id=1, source_target_pairs={{0,2},{1,9},{2,4},{3,11},{4,6},{5,13},{6,0},{7,15},{8,10},{9,17},{... | collective-permute-start | bytes 712712 | tf_op jit(solution)/shard_map/ppermute | solution.py:441
  16.1 9.4 %collective-permute-start.1 = (bf16[4,8,3712]{2,1,0:T(8,128)(2,1)S(1)}, bf16[4,8,3712]{2,1,0:T(8,128)(2,1)S(1)}, u32[]{:S(2)}, u32[]{:S(2)}) collective-permute-start(bf16[4,8,3712]{2,1,0:T(8,128)(2,1)S(1)} %all_to_all.10.refs_0_), channel_id=1, source_target_pairs={{0,4},{1,17},{2,6},{3,19},{4,0},{5,21},{6,2},{7,23},{8,12},{9,25},... | collective-permute-start | bytes 712712 | tf_op jit(solution)/shard_map/ppermute | solution.py:441
  21.9 6.1 %collective-permute-start.2 = (bf16[4,8,3712]{2,1,0:T(8,128)(2,1)S(1)}, bf16[4,8,3712]{2,1,0:T(8,128)(2,1)S(1)}, u32[]{:S(2)}, u32[]{:S(2)}) collective-permute-start(bf16[4,8,3712]{2,1,0:T(8,128)(2,1)S(1)} %all_to_all.10.refs_0_), channel_id=1, source_target_pairs={{0,6},{1,25},{2,0},{3,27},{4,2},{5,29},{6,4},{7,31},{8,14},{9,1},{... | collective-permute-start | bytes 712712 | tf_op jit(solution)/shard_map/ppermute | solution.py:441
  28.1 13.9 %collective-permute-start.3 = (bf16[4,32,1920]{2,1,0:T(8,128)(2,1)S(1)}, bf16[4,32,1920]{2,1,0:T(8,128)(2,1)S(1)}, u32[]{:S(2)}, u32[]{:S(2)}) collective-permute-start(bf16[4,32,1920]{2,1,0:T(8,128)(2,1)S(1)} %get-tuple-element.55.refs_0_), channel_id=1, source_target_pairs={{0,8},{1,3},{2,10},{3,5},{4,12},{5,7},{6,14},{7,1},{8,16},{9,11},{... | collective-permute-start | bytes 1474568 | tf_op jit(solution)/shard_map/ppermute | solution.py:441
  30.1 8.5 %collective-permute-start.5 = (bf16[4,32,1792]{2,1,0:T(8,128)(2,1)S(1)}, bf16[4,32,1792]{2,1,0:T(8,128)(2,1)S(1)}, u32[]{:S(2)}, u32[]{:S(2)}) collective-permute-start(bf16[4,32,1792]{2,1,0:T(8,128)(2,1)S(1)} %get-tuple-element.56.refs_1_), channel_id=1, source_target_pairs={{0,24},{1,7},{2,26},{3,1},{4,28},{5,3},{6,30},{7,5},{8,0},{9,15},{... | collective-permute-start | bytes 1376264 | tf_op jit(solution)/shard_map/ppermute | solution.py:441
  38.6 18.6 %collective-permute-start.10 = (bf16[4,32,1920]{2,1,0:T(8,128)(2,1)S(1)}, bf16[4,32,1920]{2,1,0:T(8,128)(2,1)S(1)}, u32[]{:S(2)}, u32[]{:S(2)}) collective-permute-start(bf16[4,32,1920]{2,1,0:T(8,128)(2,1)S(1)} %get-tuple-element.55.refs_0_), channel_id=1, source_target_pairs={{0,24},{1,7},{2,26},{3,1},{4,28},{5,3},{6,30},{7,5},{8,0},{9,15},{... | collective-permute-start | bytes 1474568 | tf_op jit(solution)/shard_map/ppermute | solution.py:441
  42.0 19.5 %collective-permute-start.4 = (bf16[4,32,1920]{2,1,0:T(8,128)(2,1)S(1)}, bf16[4,32,1920]{2,1,0:T(8,128)(2,1)S(1)}, u32[]{:S(2)}, u32[]{:S(2)}) collective-permute-start(bf16[4,32,1920]{2,1,0:T(8,128)(2,1)S(1)} %collective-permute-done.3.refs_0_), channel_id=1, source_target_pairs={{0,8},{1,3},{2,10},{3,5},{4,12},{5,7},{6,14},{7,1},{8,16},{9,11},{... | collective-permute-start | bytes 1474568 | tf_op jit(solution)/shard_map/ppermute | solution.py:441
  42.0 3.5 %copy-start.4 = (bf16[512,1792]{1,0:T(8,128)(2,1)}, bf16[512,1792]{1,0:T(8,128)(2,1)S(1)}, u32[]{:S(2)}) copy-start(bf16[512,1792]{1,0:T(8,128)(2,1)S(1)} %collective-permute-done.7.refs_3_.refs_2_) | copy-start | bytes 5505028
  42.0 15.2 %collective-permute-start.11 = (bf16[4,32,1792]{2,1,0:T(8,128)(2,1)S(1)}, bf16[4,32,1792]{2,1,0:T(8,128)(2,1)S(1)}, u32[]{:S(2)}, u32[]{:S(2)}) collective-permute-start(bf16[4,32,1792]{2,1,0:T(8,128)(2,1)S(1)} %get-tuple-element.56.refs_1_), channel_id=1, source_target_pairs={{0,8},{1,3},{2,10},{3,5},{4,12},{5,7},{6,14},{7,1},{8,16},{9,11},{... | collective-permute-start | bytes 1376264 | tf_op jit(solution)/shard_map/ppermute | solution.py:441
  42.5 18.9 %collective-permute-start.6 = (bf16[4,32,1792]{2,1,0:T(8,128)(2,1)S(1)}, bf16[4,32,1792]{2,1,0:T(8,128)(2,1)S(1)}, u32[]{:S(2)}, u32[]{:S(2)}) collective-permute-start(bf16[4,32,1792]{2,1,0:T(8,128)(2,1)S(1)} %collective-permute-done.5.refs_3_), channel_id=1, source_target_pairs={{0,24},{1,7},{2,26},{3,1},{4,28},{5,3},{6,30},{7,5},{8,0},{9,15},{... | collective-permute-start | bytes 1376264 | tf_op jit(solution)/shard_map/ppermute | solution.py:441
  64.1 9.3 %collective-permute-start.12 = (bf16[128,768]{1,0:T(8,128)(2,1)}, bf16[128,768]{1,0:T(8,128)(2,1)S(1)}, u32[]{:S(2)}, u32[]{:S(2)}) collective-permute-start(bf16[128,768]{1,0:T(8,128)(2,1)} %get-tuple-element.84), channel_id=1, source_target_pairs={{0,32},{32,64},{64,96},{96,0},{1,33},{33,65},{65,97},{97,1},{2,34}... | collective-permute-start | bytes 589832 | tf_op jit(solution)/shard_map/ppermute | solution.py:445
  64.7 8.6 %collective-permute-start.13 = (bf16[128,768]{1,0:T(8,128)(2,1)}, bf16[128,768]{1,0:T(8,128)(2,1)S(1)}, u32[]{:S(2)}, u32[]{:S(2)}) collective-permute-start(bf16[128,768]{1,0:T(8,128)(2,1)} %get-tuple-element.85), channel_id=1, source_target_pairs={{0,64},{32,96},{64,0},{96,32},{1,65},{33,97},{65,1},{97,33},{2,66}... | collective-permute-start | bytes 589832 | tf_op jit(solution)/shard_map/ppermute | solution.py:445
  66.8 7.5 %collective-permute-start.14 = (bf16[128,768]{1,0:T(8,128)(2,1)}, bf16[128,768]{1,0:T(8,128)(2,1)S(1)}, u32[]{:S(2)}, u32[]{:S(2)}) collective-permute-start(bf16[128,768]{1,0:T(8,128)(2,1)} %get-tuple-element.86), channel_id=1, source_target_pairs={{0,96},{32,0},{64,32},{96,64},{1,97},{33,1},{65,33},{97,65},{2,98}... | collective-permute-start | bytes 589832 | tf_op jit(solution)/shard_map/ppermute | solution.py:445
  75.4 6.8 %collective-permute-start.18 = (bf16[128,256]{1,0:T(8,128)(2,1)S(1)}, bf16[128,256]{1,0:T(8,128)(2,1)S(1)}, u32[]{:S(2)}, u32[]{:S(2)}) collective-permute-start(bf16[128,256]{1,0:T(8,128)(2,1)S(1)} %get-tuple-element.96.refs_4_), channel_id=1, source_target_pairs={{0,32},{32,64},{64,96},{96,0},{1,33},{33,65},{65,97},{97,1},{2,34}... | collective-permute-start | bytes 196616 | tf_op jit(solution)/shard_map/ppermute | solution.py:445
  75.7 12.3 %collective-permute-start.15 = (bf16[128,512]{1,0:T(8,128)(2,1)S(1)}, bf16[128,512]{1,0:T(8,128)(2,1)S(1)}, u32[]{:S(2)}, u32[]{:S(2)}) collective-permute-start(bf16[128,512]{1,0:T(8,128)(2,1)S(1)} %get-tuple-element.88.refs_0_), channel_id=1, source_target_pairs={{0,32},{32,64},{64,96},{96,0},{1,33},{33,65},{65,97},{97,1},{2,34}... | collective-permute-start | bytes 393224 | tf_op jit(solution)/shard_map/ppermute | solution.py:445
  76.3 11.7 %collective-permute-start.16 = (bf16[128,512]{1,0:T(8,128)(2,1)S(1)}, bf16[128,512]{1,0:T(8,128)(2,1)S(1)}, u32[]{:S(2)}, u32[]{:S(2)}) collective-permute-start(bf16[128,512]{1,0:T(8,128)(2,1)S(1)} %get-tuple-element.88.refs_0_), channel_id=1, source_target_pairs={{0,64},{32,96},{64,0},{96,32},{1,65},{33,97},{65,1},{97,33},{2,66}... | collective-permute-start | bytes 393224 | tf_op jit(solution)/shard_map/ppermute | solution.py:445
  80.2 7.8 %collective-permute-start.17 = (bf16[128,512]{1,0:T(8,128)(2,1)S(1)}, bf16[128,512]{1,0:T(8,128)(2,1)S(1)}, u32[]{:S(2)}, u32[]{:S(2)}) collective-permute-start(bf16[128,512]{1,0:T(8,128)(2,1)S(1)} %get-tuple-element.88.refs_0_), channel_id=1, source_target_pairs={{0,96},{32,0},{64,32},{96,64},{1,97},{33,1},{65,33},{97,65},{2,98}... | collective-permute-start | bytes 393224 | tf_op jit(solution)/shard_map/ppermute | solution.py:445
  82.2 5.8 %collective-permute-start.19 = (bf16[128,256]{1,0:T(8,128)(2,1)S(1)}, bf16[128,256]{1,0:T(8,128)(2,1)S(1)}, u32[]{:S(2)}, u32[]{:S(2)}) collective-permute-start(bf16[128,256]{1,0:T(8,128)(2,1)S(1)} %get-tuple-element.96.refs_4_), channel_id=1, source_target_pairs={{0,64},{32,96},{64,0},{96,32},{1,65},{33,97},{65,1},{97,33},{2,66}... | collective-permute-start | bytes 196616 | tf_op jit(solution)/shard_map/ppermute | solution.py:445
  82.2 5.8 %collective-permute-start.20 = (bf16[128,256]{1,0:T(8,128)(2,1)S(1)}, bf16[128,256]{1,0:T(8,128)(2,1)S(1)}, u32[]{:S(2)}, u32[]{:S(2)}) collective-permute-start(bf16[128,256]{1,0:T(8,128)(2,1)S(1)} %get-tuple-element.96.refs_4_), channel_id=1, source_target_pairs={{0,96},{32,0},{64,32},{96,64},{1,97},{33,1},{65,33},{97,65},{2,98}... | collective-permute-start | bytes 196616 | tf_op jit(solution)/shard_map/ppermute | solution.py:445
  88.0 0.9 copy-start
  90.2 4.0 %copy-start.2 = (bf16[4,128,1792]{2,1,0:T(8,128)(2,1)S(1)}, bf16[4,128,1792]{2,1,0:T(8,128)(2,1)}, u32[]{:S(2)}) copy-start(bf16[4,128,1792]{2,1,0:T(8,128)(2,1)} %get-tuple-element.98) | copy-start | bytes 5505028
  94.2 23.2 %collective-permute-start.23 = (bf16[512,1792]{1,0:T(8,128)(2,1)}, bf16[512,1792]{1,0:T(8,128)(2,1)}, u32[]{:S(2)}, u32[]{:S(2)}) collective-permute-start(bf16[512,1792]{1,0:T(8,128)(2,1)} %convolution_convert_fusion), channel_id=1, source_target_pairs={{0,1},{1,0},{2,3},{3,2},{4,5},{5,4},{6,7},{7,6},{8,9},{9,8},{10,11... | collective-permute-start | bytes 5505032 | tf_op jit(solution)/shard_map/ppermute | solution.py:449
  96.6 25.4 %collective-permute-start.22 = (bf16[512,1792]{1,0:T(8,128)(2,1)}, bf16[512,1792]{1,0:T(8,128)(2,1)}, u32[]{:S(2)}, u32[]{:S(2)}) collective-permute-start(bf16[512,1792]{1,0:T(8,128)(2,1)} %convolution_convert_fusion.1), channel_id=1, source_target_pairs={{0,1},{1,0},{2,3},{3,2},{4,5},{5,4},{6,7},{7,6},{8,9},{9,8},{10,11... | collective-permute-start | bytes 5505032 | tf_op jit(solution)/shard_map/ppermute | solution.py:449
  99.5 3.2 %copy-start.1 = (bf16[4,128,128]{2,1,0:T(8,128)(2,1)S(1)}, bf16[4,128,128]{2,1,0:T(8,128)(2,1)}, u32[]{:S(2)}) copy-start(bf16[4,128,128]{2,1,0:T(8,128)(2,1)} %get-tuple-element.87.refs_4_.refs_8_) | copy-start | bytes 393220
  99.5 26.4 %collective-permute-start.21 = (bf16[512,1792]{1,0:T(8,128)(2,1)}, bf16[512,1792]{1,0:T(8,128)(2,1)}, u32[]{:S(2)}, u32[]{:S(2)}) collective-permute-start(bf16[512,1792]{1,0:T(8,128)(2,1)} %convolution_convert_fusion.2), channel_id=1, source_target_pairs={{0,1},{1,0},{2,3},{3,2},{4,5},{5,4},{6,7},{7,6},{8,9},{9,8},{10,11... | collective-permute-start | bytes 5505032 | tf_op jit(solution)/shard_map/ppermute | solution.py:449
  108.2 37.9 %all-to-all-start.1 = ((bf16[64,8,1920]{2,1,0:T(8,128)(2,1)}), bf16[64,8,1920]{2,1,0:T(8,128)(2,1)S(1)}, u32[]{:S(2)}, u32[]{:S(2)}) async-start(bf16[64,8,1920]{2,1,0:T(8,128)(2,1)} %bitcast.28), calls=%async_computation.1 | async-start | bytes 3932160 | tf_op jit(solution)/shard_map/all_to_all | solution.py:486
  117.5 4.6 %copy-start.3 = (bf16[4,128,1792]{2,1,0:T(8,128)(2,1)S(1)}, bf16[4,128,1792]{2,1,0:T(8,128)(2,1)}, u32[]{:S(2)}) copy-start(bf16[4,128,1792]{2,1,0:T(8,128)(2,1)} %get-tuple-element.98) | copy-start | bytes 5505028

commit v5 on v4

--- a/solution.py
+++ b/solution.py
@@ -51,10 +51,25 @@
     return ref[...].reshape(lead * rows, width)
 
 
-def pack(plane_ref, z_ref, chip_ref, core_ref, tok_ref, cot_ref, route_ref, gates_ref, out_ref):
+def pack(plane_ref, z_ref, chip_ref, core_ref, tok_ref, cot_ref, route_ref, gates_ref, *rest):
+    out_ref, meta_ref, sems = rest
     rows, full = tok_ref.shape
     width = full // SIDE
     lap = width + LANES
+    copies = []
+    for j in range(SIDE):
+        cut = slice(j * width, (j + 1) * width)
+        jobs = (
+            (tok_ref.at[:, cut], out_ref.at[j, :, :width]),
+            (cot_ref.at[:, cut], out_ref.at[j, :, lap:]),
+            (meta_ref, out_ref.at[j, :, width:lap]),
+        )
+        copies.append(
+            [pltpu.make_async_copy(src, dst, sems.at[j, n]) for n, (src, dst) in enumerate(jobs)]
+        )
+    for group in copies:
+        group[0].start()
+        group[1].start()
     eye = lax.broadcasted_iota(jnp.int32, (rows, rows), 0) == lax.broadcasted_iota(
         jnp.int32, (rows, rows), 1
     )
@@ -65,11 +80,12 @@
         for k in range(2):
             column = jnp.sum(jnp.where(eye, vals[k:k + 1, :], 0.0), axis=1, keepdims=True)
             meta = jnp.where(lane == 2 * n + k, column, meta)
-    meta = meta.astype(BF)
-    for j in range(SIDE):
-        out_ref[j, :, :width] = tok_ref[:, j * width:(j + 1) * width]
-        out_ref[j, :, width:lap] = meta
-        out_ref[j, :, lap:] = cot_ref[:, j * width:(j + 1) * width]
+    meta_ref[...] = meta.astype(BF)
+    for group in copies:
+        group[2].start()
+    for group in copies:
+        for copy in group:
+            copy.wait()
 
 
 def pack_call(spot, tokens, cotangent, routing, gates, width):
@@ -81,8 +97,10 @@
         grid_spec=pltpu.PrefetchScalarGridSpec(
             num_scalar_prefetch=4,
             grid=(1,),
-            in_specs=[pl.BlockSpec(a.shape, lambda i, *s: (0, 0)) for a in args],
-            out_specs=pl.BlockSpec(out.shape, lambda i, *s: (0, 0, 0)),
+            in_specs=[pl.BlockSpec(memory_space=pl.ANY)] * 2
+            + [pl.BlockSpec(a.shape, lambda i, *s: (0, 0)) for a in args[2:]],
+            out_specs=pl.BlockSpec(memory_space=pl.ANY),
+            scratch_shapes=[pltpu.VMEM((rows, LANES), BF), pltpu.SemaphoreType.DMA((SIDE, 3))],
         ),
         out_shape=out,
         compiler_params=params(8),

time: 147 us -> 155 us (1.054)
  Pallas kernels: 32.4 us -> 39.5 us
    pallas_call x1, Pallas kernels: 1.73 us -> 8.84 us  [pack_call(): pl.pallas_call(pack, grid_spec=pltpu.PrefetchScalarGridSpec(num_scalar_pr...]
  transfers between devices with their start and end apart: 25 -> 25, of which waited for: 8 -> 8; matrix products, arithmetic and copies ran while one was open for 12% -> 11% of each run, Pallas kernels for 18% -> 22%
where the time goes in v5:
time: 155 us; the launch traced here: 154 us
  starting transfers between devices  40.3 us (26%)
  waiting for transfers between devices  39.9 us (26%)
  Pallas kernels  39.5 us (25%)
  matrix products  21.1 us (14%)
  blocking collectives  11.6 us (7%)
    dot_general x6, matrix products, contract_rows(): lax.dot_general(left, right, (((0,), (0,)), ((), ())), preferred_element_...  21.1 us
    ppermute x9, starting transfers between devices, shift(): return lax.ppermute(arr, PLANE, pairs)  16.9 us
    all_to_all x1, waiting for transfers between devices, local(): lax.all_to_all(sent.reshape(-1, tok_rows, lap), TORUS, 0, 0, tiled=True)  16.2 us
    ppermute x9, waiting for transfers between devices, shift(): return lax.ppermute(arr, PLANE, pairs)  13.9 us
    ppermute x9, starting transfers between devices, turn(): return lax.ppermute(arr, 'ep', [(i, (i + by) % SIDE) for i in range(SIDE)])  13 us
    all_to_all x1, blocking collectives, local(): own = lax.all_to_all(send, 'ep', 0, 0, tiled=True)  11.6 us
    pallas_call x3, Pallas kernels, pre_call(): pl.pallas_call(pre_acts(count, first * rows, width, multiply), grid_spec=...  11.3 us
    ppermute x9, waiting for transfers between devices, turn(): return lax.ppermute(arr, 'ep', [(i, (i + by) % SIDE) for i in range(SIDE)])  9.67 us
  transfers between devices with their start and end apart: 25, of which 8 were waited for; matrix products, arithmetic and copies ran while one was open for 11% of the time, Pallas kernels for 22%

profile of v5, /device:TPU:0, one launch (start us, length us, event | category | flops | bytes accessed | tf_op | source)
XLA Modules:
  0.0 154.1 jit_solution(17656023842247689659)
XLA Ops:
  0.6 0.1 collective-permute-start.7
  0.7 0.5 collective-permute-start.8
  1.2 0.1 collective-permute-start.9
  1.3 8.8 %shard_map.110 = bf16[4,8,3712]{2,1,0:T(8,128)(2,1)} custom-call(s32[1]{0:T(128)} %bitcast.plane_ref, s32[1]{0:T(128)} %bitcast.1.z_ref, s32[1]{0:T(128)} %bitcast.2.chip_ref.x_ref, s32[1]{0:T(128)} %bitcast.3.core_ref, bf16[8,7168]{1,0:T(8,128)(2,1)} %tok_ref.1, bf16[8,7168]{1,0:T(8,128)(2,1)} %cot_ref.1, s32[2,8]{1,0:T(2,128)} %bitcast.43, ...), custom_call_target="tpu_custom_call" | custom-call | tf_op jit(solution)/shard_map/pallas_call | solution.py:95
  10.2 11.6 %all_to_all.10.refs_0_ = bf16[4,8,3712]{2,1,0:T(8,128)(2,1)S(1)} all-to-all(bf16[4,8,3712]{2,1,0:T(8,128)(2,1)} %shard_map.110), channel_id=1, replica_groups=mesh['ep'=4,'z'=4,'x'=4,'core'=2] {'ep'}, dimensions={0} | all-to-all | bytes 475136 | tf_op jit(solution)/shard_map/all_to_all | solution.py:484
  21.7 1.5 collective-permute-start
  23.2 2.7 %collective-permute-start.1 = (bf16[4,8,3712]{2,1,0:T(8,128)(2,1)S(1)}, bf16[4,8,3712]{2,1,0:T(8,128)(2,1)S(1)}, u32[]{:S(2)}, u32[]{:S(2)}) collective-permute-start(bf16[4,8,3712]{2,1,0:T(8,128)(2,1)S(1)} %all_to_all.10.refs_0_), channel_id=1, source_target_pairs={{0,4},{1,17},{2,6},{3,19},{4,0},{5,21},{6,2},{7,23},{8,12},{9,25},... | collective-permute-start | bytes 712712 | tf_op jit(solution)/shard_map/ppermute | solution.py:459
  26.0 3.1 %collective-permute-done.refs_1_ = bf16[4,8,3712]{2,1,0:T(8,128)(2,1)S(1)} collective-permute-done((bf16[4,8,3712]{2,1,0:T(8,128)(2,1)S(1)}, bf16[4,8,3712]{2,1,0:T(8,128)(2,1)S(1)}, u32[]{:S(2)}, u32[]{:S(2)}) %collective-permute-start) | collective-permute-done | bytes 237600 | tf_op jit(solution)/shard_map/ppermute | solution.py:459
  29.1 1.5 %collective-permute-start.2 = (bf16[4,8,3712]{2,1,0:T(8,128)(2,1)S(1)}, bf16[4,8,3712]{2,1,0:T(8,128)(2,1)S(1)}, u32[]{:S(2)}, u32[]{:S(2)}) collective-permute-start(bf16[4,8,3712]{2,1,0:T(8,128)(2,1)S(1)} %all_to_all.10.refs_0_), channel_id=1, source_target_pairs={{0,6},{1,25},{2,0},{3,27},{4,2},{5,29},{6,4},{7,31},{8,14},{9,1},{... | collective-permute-start | bytes 712712 | tf_op jit(solution)/shard_map/ppermute | solution.py:459
  30.6 2.0 %collective-permute-done.1.refs_2_ = bf16[4,8,3712]{2,1,0:T(8,128)(2,1)S(1)} collective-permute-done((bf16[4,8,3712]{2,1,0:T(8,128)(2,1)S(1)}, bf16[4,8,3712]{2,1,0:T(8,128)(2,1)S(1)}, u32[]{:S(2)}, u32[]{:S(2)}) %collective-permute-start.1) | collective-permute-done | bytes 237600 | tf_op jit(solution)/shard_map/ppermute | solution.py:459
  32.6 2.6 %collective-permute-done.2.refs_3_ = bf16[4,8,3712]{2,1,0:T(8,128)(2,1)S(1)} collective-permute-done((bf16[4,8,3712]{2,1,0:T(8,128)(2,1)S(1)}, bf16[4,8,3712]{2,1,0:T(8,128)(2,1)S(1)}, u32[]{:S(2)}, u32[]{:S(2)}) %collective-permute-start.2) | collective-permute-done | bytes 237600 | tf_op jit(solution)/shard_map/ppermute | solution.py:459
  35.2 0.1 shard_map.111
  35.2 2.0 %collective-permute-start.3 = (bf16[4,32,1920]{2,1,0:T(8,128)(2,1)S(1)}, bf16[4,32,1920]{2,1,0:T(8,128)(2,1)S(1)}, u32[]{:S(2)}, u32[]{:S(2)}) collective-permute-start(bf16[4,32,1920]{2,1,0:T(8,128)(2,1)S(1)} %get-tuple-element.55.refs_0_), channel_id=1, source_target_pairs={{0,8},{1,3},{2,10},{3,5},{4,12},{5,7},{6,14},{7,1},{8,16},{9,11},{... | collective-permute-start | bytes 1474568 | tf_op jit(solution)/shard_map/ppermute | solution.py:459
  37.2 2.2 %collective-permute-start.5 = (bf16[4,32,1792]{2,1,0:T(8,128)(2,1)S(1)}, bf16[4,32,1792]{2,1,0:T(8,128)(2,1)S(1)}, u32[]{:S(2)}, u32[]{:S(2)}) collective-permute-start(bf16[4,32,1792]{2,1,0:T(8,128)(2,1)S(1)} %get-tuple-element.56.refs_1_), channel_id=1, source_target_pairs={{0,24},{1,7},{2,26},{3,1},{4,28},{5,3},{6,30},{7,5},{8,0},{9,15},{... | collective-permute-start | bytes 1376264 | tf_op jit(solution)/shard_map/ppermute | solution.py:459
  39.4 6.3 %collective-permute-done.5.refs_3_ = bf16[4,32,1792]{2,1,0:T(8,128)(2,1)S(1)} collective-permute-done((bf16[4,32,1792]{2,1,0:T(8,128)(2,1)S(1)}, bf16[4,32,1792]{2,1,0:T(8,128)(2,1)S(1)}, u32[]{:S(2)}, u32[]{:S(2)}) %collective-permute-start.5) | collective-permute-done | bytes 458784 | tf_op jit(solution)/shard_map/ppermute | solution.py:459
  45.7 3.4 %collective-permute-start.10 = (bf16[4,32,1920]{2,1,0:T(8,128)(2,1)S(1)}, bf16[4,32,1920]{2,1,0:T(8,128)(2,1)S(1)}, u32[]{:S(2)}, u32[]{:S(2)}) collective-permute-start(bf16[4,32,1920]{2,1,0:T(8,128)(2,1)S(1)} %get-tuple-element.55.refs_0_), channel_id=1, source_target_pairs={{0,24},{1,7},{2,26},{3,1},{4,28},{5,3},{6,30},{7,5},{8,0},{9,15},{... | collective-permute-start | bytes 1474568 | tf_op jit(solution)/shard_map/ppermute | solution.py:459
  49.1 0.0 collective-permute-done.3.refs_0_
  49.1 0.0 copy-start.4
  49.1 0.5 collective-permute-start.11
  49.7 3.0 %collective-permute-start.6 = (bf16[4,32,1792]{2,1,0:T(8,128)(2,1)S(1)}, bf16[4,32,1792]{2,1,0:T(8,128)(2,1)S(1)}, u32[]{:S(2)}, u32[]{:S(2)}) collective-permute-start(bf16[4,32,1792]{2,1,0:T(8,128)(2,1)S(1)} %collective-permute-done.5.refs_3_), channel_id=1, source_target_pairs={{0,24},{1,7},{2,26},{3,1},{4,28},{5,3},{6,30},{7,5},{8,0},{9,15},{... | collective-permute-start | bytes 1376264 | tf_op jit(solution)/shard_map/ppermute | solution.py:459
  52.6 4.2 %shard_map.112 = (bf16[512,1792]{1,0:T(8,128)(2,1)S(1)}, bf16[512,1792]{1,0:T(8,128)(2,1)S(1)}, bf16[512,1792]{1,0:T(8,128)(2,1)S(1)}, bf16[512,1792]{1,0:T(8,12...) custom-call(bf16[512,1792]{1,0:T(8,128)(2,1)} %bitcast.36, bf16[512,1792]{1,0:T(8,128)(2,1)} %bitcast.39, ...), custom_call_target="tpu_custom_call" | custom-call | tf_op jit(solution)/shard_map/pallas_call | solution.py:121
  56.9 4.6 %shard_map.114 = (bf16[128,768]{1,0:T(8,128)(2,1)}, bf16[128,768]{1,0:T(8,128)(2,1)}, bf16[128,768]{1,0:T(8,128)(2,1)}, bf16[128,768]{1,0:T(8,128)(2,1)}, bf16[4...) custom-call(s32[1]{0:T(128)} %bitcast.plane_ref, ...), custom_call_target="tpu_custom_call" | custom-call | tf_op jit(solution)/shard_map/pallas_call | solution.py:228
  61.5 2.9 %shard_map.113 = (bf16[1792,512]{1,0:T(8,128)(2,1)S(1)}, bf16[1792,512]{1,0:T(8,128)(2,1)S(1)}, bf16[1792,512]{1,0:T(8,128)(2,1)S(1)}, bf16[1792,512]{1,0:T(8,12...) custom-call(bf16[512,1792]{1,0:T(8,128)(2,1)S(1)} %get-tuple-element.57.refs_0_.refs_2_, ...), custom_call_target="tpu_custom_call" | custom-call | tf_op jit(solution)/shard_map/pallas_call | solution.py:138
  64.3 0.0 collective-permute-done.11.refs_2_
  64.4 4.2 %shard_map.115 = (bf16[128,768]{1,0:T(8,128)(2,1)}, bf16[128,768]{1,0:T(8,128)(2,1)}, bf16[128,768]{1,0:T(8,128)(2,1)}, bf16[128,768]{1,0:T(8,128)(2,1)}, bf16[4...) custom-call(s32[1]{0:T(128)} %bitcast.plane_ref, ...), custom_call_target="tpu_custom_call", output_to_operand_aliasing={{0}: (11, {}), {1}: (12, {}), {2}: (13, {}), {3}: (14, {}),... | custom-call | tf_op jit(solution)/shard_map/pallas_call | solution.py:228
  68.6 0.0 collective-permute-done.6.refs_1_
  68.6 2.6 %shard_map.116 = (bf16[128,768]{1,0:T(8,128)(2,1)}, bf16[128,768]{1,0:T(8,128)(2,1)}, bf16[128,768]{1,0:T(8,128)(2,1)}, bf16[128,768]{1,0:T(8,128)(2,1)}, bf16[4...) custom-call(s32[1]{0:T(128)} %bitcast.plane_ref, ...), custom_call_target="tpu_custom_call", output_to_operand_aliasing={{0}: (9, {}), {1}: (10, {}), {2}: (11, {}), {3}: (12, {}), ... | custom-call | tf_op jit(solution)/shard_map/pallas_call | solution.py:228
  71.2 0.6 collective-permute-start.12
  71.8 2.1 %collective-permute-start.13 = (bf16[128,768]{1,0:T(8,128)(2,1)}, bf16[128,768]{1,0:T(8,128)(2,1)S(1)}, u32[]{:S(2)}, u32[]{:S(2)}) collective-permute-start(bf16[128,768]{1,0:T(8,128)(2,1)} %get-tuple-element.85), channel_id=1, source_target_pairs={{0,64},{32,96},{64,0},{96,32},{1,65},{33,97},{65,1},{97,33},{2,66}... | collective-permute-start | bytes 589832 | tf_op jit(solution)/shard_map/ppermute | solution.py:463
  73.9 0.9 collective-permute-start.14
  74.8 5.7 %collective-permute-done.12.refs_1_ = bf16[128,768]{1,0:T(8,128)(2,1)S(1)} collective-permute-done((bf16[128,768]{1,0:T(8,128)(2,1)}, bf16[128,768]{1,0:T(8,128)(2,1)S(1)}, u32[]{:S(2)}, u32[]{:S(2)}) %collective-permute-start.12) | collective-permute-done | bytes 196640 | tf_op jit(solution)/shard_map/ppermute | solution.py:463
  80.5 0.0 collective-permute-done.13.refs_2_
  80.5 0.9 collective-permute-done.14.refs_3_
  81.4 1.2 shard_map.117
  82.5 0.3 collective-permute-start.18
  82.8 0.6 collective-permute-start.15
  83.4 3.9 %collective-permute-start.16 = (bf16[128,512]{1,0:T(8,128)(2,1)S(1)}, bf16[128,512]{1,0:T(8,128)(2,1)S(1)}, u32[]{:S(2)}, u32[]{:S(2)}) collective-permute-start(bf16[128,512]{1,0:T(8,128)(2,1)S(1)} %get-tuple-element.88.refs_0_), channel_id=1, source_target_pairs={{0,64},{32,96},{64,0},{96,32},{1,65},{33,97},{65,1},{97,33},{2,66}... | collective-permute-start | bytes 393224 | tf_op jit(solution)/shard_map/ppermute | solution.py:463
  87.3 2.0 %collective-permute-start.17 = (bf16[128,512]{1,0:T(8,128)(2,1)S(1)}, bf16[128,512]{1,0:T(8,128)(2,1)S(1)}, u32[]{:S(2)}, u32[]{:S(2)}) collective-permute-start(bf16[128,512]{1,0:T(8,128)(2,1)S(1)} %get-tuple-element.88.refs_0_), channel_id=1, source_target_pairs={{0,96},{32,0},{64,32},{96,64},{1,97},{33,1},{65,33},{97,65},{2,98}... | collective-permute-start | bytes 393224 | tf_op jit(solution)/shard_map/ppermute | solution.py:463
  89.3 0.0 collective-permute-start.19
  89.3 2.7 %collective-permute-start.20 = (bf16[128,256]{1,0:T(8,128)(2,1)S(1)}, bf16[128,256]{1,0:T(8,128)(2,1)S(1)}, u32[]{:S(2)}, u32[]{:S(2)}) collective-permute-start(bf16[128,256]{1,0:T(8,128)(2,1)S(1)} %get-tuple-element.96.refs_4_), channel_id=1, source_target_pairs={{0,96},{32,0},{64,32},{96,64},{1,97},{33,1},{65,33},{97,65},{2,98}... | collective-permute-start | bytes 196616 | tf_op jit(solution)/shard_map/ppermute | solution.py:463
  92.0 3.1 %collective-permute-done.19.refs_6_ = bf16[128,256]{1,0:T(8,128)(2,1)S(1)} collective-permute-done((bf16[128,256]{1,0:T(8,128)(2,1)S(1)}, bf16[128,256]{1,0:T(8,128)(2,1)S(1)}, u32[]{:S(2)}, u32[]{:S(2)}) %collective-permute-start.19) | collective-permute-done | bytes 65568 | tf_op jit(solution)/shard_map/ppermute | solution.py:463
  95.1 0.0 collective-permute-done.20.refs_7_
  95.1 0.0 collective-permute-done.15.refs_1_
  95.1 0.0 collective-permute-done.16.refs_2_
  95.1 0.9 copy-done
  96.0 1.3 shard_map.121
  97.3 0.0 copy-start.2
  97.4 4.0 %convolution_convert_fusion = bf16[512,1792]{1,0:T(8,128)(2,1)} fusion(bf16[512,512]{1,0:T(8,128)(2,1)S(1)} %get-tuple-element.104, bf16[512,1792]{1,0:T(8,128)(2,1)} %bitcast.33), kind=kOutput, calls=%fused_computation.3 | convolution fusion | flops 940441600 | bytes 4194304 | tf_op jit(solution)/shard_map/dot_general | solution.py:471
  101.4 2.4 %convolution_convert_fusion.1 = bf16[512,1792]{1,0:T(8,128)(2,1)} fusion(bf16[512,512]{1,0:T(8,128)(2,1)S(1)} %get-tuple-element.101, bf16[512,1792]{1,0:T(8,128)(2,1)S(1)} %bitcast.29), kind=kOutput, calls=%fused_computation.4 | convolution fusion | flops 940441600 | bytes 4194304 | tf_op jit(solution)/shard_map/dot_general | solution.py:471
  103.8 0.5 collective-permute-start.22
  104.3 2.4 %convolution_convert_fusion.2 = bf16[512,1792]{1,0:T(8,128)(2,1)} fusion(bf16[512,512]{1,0:T(8,128)(2,1)S(1)} %get-tuple-element.99, bf16[512,1792]{1,0:T(8,128)(2,1)S(1)} %bitcast.30), kind=kOutput, calls=%fused_computation.5 | convolution fusion | flops 940441600 | bytes 4194304 | tf_op jit(solution)/shard_map/dot_general | solution.py:471
  106.7 0.0 collective-permute-start.21
  106.7 3.2 %shard_map.118 = (bf16[512,1792]{1,0:T(8,128)(2,1)S(1)}, bf16[512,1792]{1,0:T(8,128)(2,1)S(1)}, bf16[512,1792]{1,0:T(8,128)(2,1)S(1)}, bf16[512,1792]{1,0:T(8,128)(2,1)S(1)}) custom-call(bf16[512,1792]{1,0:T(8,128)(2,1)} %bitcast.37, bf16[512,1792]{1,0:T(8,128)(2,1)} %bitcast.40, bf16[512,1792]{1,0:T(8,128)(2,1)} %copy-done.4, ...), custom_call_target="tpu_custom_call" | custom-call | tf_op jit(solution)/shard_map/pallas_call | solution.py:121
  109.9 5.5 %shard_map.119 = bf16[4,128,1920]{2,1,0:T(8,128)(2,1)} custom-call(s32[1]{0:T(128)} %bitcast.plane_ref, s32[1]{0:T(128)} %bitcast.1.z_ref, s32[1]{0:T(128)} %bitcast.2.chip_ref.x_ref, s32[1]{0:T(128)} %bitcast.3.core_ref, bf16[128,512]{1,0:T(8,128)(2,1)S(1)} %get-tuple-element.88.refs_0_, bf16[128,512]{1,0:T(8,128)(2,1)S(1)} %collective-permute-done.15.refs_1_, ...), custom_call_target="tpu_custom_call" | custom-call | tf_op jit(solution)/shard_map/pallas_call | solution.py:396
  115.4 9.2 %all-to-all-start.1 = ((bf16[64,8,1920]{2,1,0:T(8,128)(2,1)}), bf16[64,8,1920]{2,1,0:T(8,128)(2,1)S(1)}, u32[]{:S(2)}, u32[]{:S(2)}) async-start(bf16[64,8,1920]{2,1,0:T(8,128)(2,1)} %bitcast.28), calls=%async_computation.1 | async-start | bytes 3932160 | tf_op jit(solution)/shard_map/all_to_all | solution.py:504
  124.6 0.0 collective-permute-done.23
  124.6 0.0 copy-start.3
  124.6 4.6 %add_convert_fusion = bf16[512,1792]{1,0:T(8,128)(2,1)} fusion(bf16[512,1792]{1,0:T(8,128)(2,1)} %collective-permute-done.23, bf16[512,512]{1,0:T(8,128)(2,1)S(1)} %get-tuple-element.102, bf16[512,1792]{1,0:T(8,128)(2,1)} %bitcast.34), kind=kOutput, calls=%fused_computation | convolution fusion | flops 942276608 | bytes 6029312 | tf_op jit(solution)/shard_map/dot_general | solution.py:471
  129.2 0.0 collective-permute-done.22
  129.2 3.9 %add_convert_fusion.1 = bf16[512,1792]{1,0:T(8,128)(2,1)} fusion(bf16[512,1792]{1,0:T(8,128)(2,1)} %collective-permute-done.22, bf16[512,512]{1,0:T(8,128)(2,1)S(1)} %get-tuple-element.100, bf16[512,1792]{1,0:T(8,128)(2,1)S(1)} %bitcast.31), kind=kOutput, calls=%fused_computation.1 | convolution fusion | flops 942276608 | bytes 6029312 | tf_op jit(solution)/shard_map/dot_general | solution.py:471
  133.1 0.0 collective-permute-done.21
  133.1 3.9 %add_convert_fusion.2 = bf16[512,1792]{1,0:T(8,128)(2,1)} fusion(bf16[512,1792]{1,0:T(8,128)(2,1)} %collective-permute-done.21, bf16[512,512]{1,0:T(8,128)(2,1)S(1)} %get-tuple-element.97, bf16[512,1792]{1,0:T(8,128)(2,1)S(1)} %bitcast.32), kind=kOutput, calls=%fused_computation.2 | convolution fusion | flops 942276608 | bytes 6029312 | tf_op jit(solution)/shard_map/dot_general | solution.py:471
  137.0 16.2 %all-to-all-done.1.parts_ref = bf16[64,8,1920]{2,1,0:T(8,128)(2,1)S(1)} async-done(((bf16[64,8,1920]{2,1,0:T(8,128)(2,1)}), bf16[64,8,1920]{2,1,0:T(8,128)(2,1)S(1)}, u32[]{:S(2)}, u32[]{:S(2)}) %all-to-all-start.1) | async-done | bytes 1966112 | tf_op jit(solution)/shard_map/all_to_all | solution.py:504
  153.2 0.9 shard_map.120
  (15 shorter events, 0.0 us)
Async XLA Ops:
  0.6 48.5 %collective-permute-start.7 = (bf16[512,1792]{1,0:T(8,128)(2,1)}, bf16[512,1792]{1,0:T(8,128)(2,1)S(1)}, u32[]{:S(2)}, u32[]{:S(2)}) collective-permute-start(bf16[512,1792]{1,0:T(8,128)(2,1)} %bitcast.35), channel_id=1, source_target_pairs={{0,1},{1,0},{2,3},{3,2},{4,5},{5,4},{6,7},{7,6},{8,9},{9,8},{10,11... | collective-permute-start | bytes 5505032 | tf_op jit(solution)/shard_map/ppermute | solution.py:467
  0.7 48.9 %collective-permute-start.8 = (bf16[512,1792]{1,0:T(8,128)(2,1)}, bf16[512,1792]{1,0:T(8,128)(2,1)}, u32[]{:S(2)}, u32[]{:S(2)}) collective-permute-start(bf16[512,1792]{1,0:T(8,128)(2,1)} %bitcast.38), channel_id=1, source_target_pairs={{0,1},{1,0},{2,3},{3,2},{4,5},{5,4},{6,7},{7,6},{8,9},{9,8},{10,11... | collective-permute-start | bytes 5505032 | tf_op jit(solution)/shard_map/ppermute | solution.py:467
  1.2 51.4 %collective-permute-start.9 = (bf16[512,1792]{1,0:T(8,128)(2,1)}, bf16[512,1792]{1,0:T(8,128)(2,1)}, u32[]{:S(2)}, u32[]{:S(2)}) collective-permute-start(bf16[512,1792]{1,0:T(8,128)(2,1)} %bitcast.41), channel_id=1, source_target_pairs={{0,1},{1,0},{2,3},{3,2},{4,5},{5,4},{6,7},{7,6},{8,9},{9,8},{10,11... | collective-permute-start | bytes 5505032 | tf_op jit(solution)/shard_map/ppermute | solution.py:467
  21.7 7.3 %collective-permute-start = (bf16[4,8,3712]{2,1,0:T(8,128)(2,1)S(1)}, bf16[4,8,3712]{2,1,0:T(8,128)(2,1)S(1)}, u32[]{:S(2)}, u32[]{:S(2)}) collective-permute-start(bf16[4,8,3712]{2,1,0:T(8,128)(2,1)S(1)} %all_to_all.10.refs_0_), channel_id=1, source_target_pairs={{0,2},{1,9},{2,4},{3,11},{4,6},{5,13},{6,0},{7,15},{8,10},{9,17},{... | collective-permute-start | bytes 712712 | tf_op jit(solution)/shard_map/ppermute | solution.py:459
  23.2 9.4 %collective-permute-start.1 = (bf16[4,8,3712]{2,1,0:T(8,128)(2,1)S(1)}, bf16[4,8,3712]{2,1,0:T(8,128)(2,1)S(1)}, u32[]{:S(2)}, u32[]{:S(2)}) collective-permute-start(bf16[4,8,3712]{2,1,0:T(8,128)(2,1)S(1)} %all_to_all.10.refs_0_), channel_id=1, source_target_pairs={{0,4},{1,17},{2,6},{3,19},{4,0},{5,21},{6,2},{7,23},{8,12},{9,25},... | collective-permute-start | bytes 712712 | tf_op jit(solution)/shard_map/ppermute | solution.py:459
  29.1 6.1 %collective-permute-start.2 = (bf16[4,8,3712]{2,1,0:T(8,128)(2,1)S(1)}, bf16[4,8,3712]{2,1,0:T(8,128)(2,1)S(1)}, u32[]{:S(2)}, u32[]{:S(2)}) collective-permute-start(bf16[4,8,3712]{2,1,0:T(8,128)(2,1)S(1)} %all_to_all.10.refs_0_), channel_id=1, source_target_pairs={{0,6},{1,25},{2,0},{3,27},{4,2},{5,29},{6,4},{7,31},{8,14},{9,1},{... | collective-permute-start | bytes 712712 | tf_op jit(solution)/shard_map/ppermute | solution.py:459
  35.2 13.9 %collective-permute-start.3 = (bf16[4,32,1920]{2,1,0:T(8,128)(2,1)S(1)}, bf16[4,32,1920]{2,1,0:T(8,128)(2,1)S(1)}, u32[]{:S(2)}, u32[]{:S(2)}) collective-permute-start(bf16[4,32,1920]{2,1,0:T(8,128)(2,1)S(1)} %get-tuple-element.55.refs_0_), channel_id=1, source_target_pairs={{0,8},{1,3},{2,10},{3,5},{4,12},{5,7},{6,14},{7,1},{8,16},{9,11},{... | collective-permute-start | bytes 1474568 | tf_op jit(solution)/shard_map/ppermute | solution.py:459
  37.2 8.5 %collective-permute-start.5 = (bf16[4,32,1792]{2,1,0:T(8,128)(2,1)S(1)}, bf16[4,32,1792]{2,1,0:T(8,128)(2,1)S(1)}, u32[]{:S(2)}, u32[]{:S(2)}) collective-permute-start(bf16[4,32,1792]{2,1,0:T(8,128)(2,1)S(1)} %get-tuple-element.56.refs_1_), channel_id=1, source_target_pairs={{0,24},{1,7},{2,26},{3,1},{4,28},{5,3},{6,30},{7,5},{8,0},{9,15},{... | collective-permute-start | bytes 1376264 | tf_op jit(solution)/shard_map/ppermute | solution.py:459
  45.7 18.7 %collective-permute-start.10 = (bf16[4,32,1920]{2,1,0:T(8,128)(2,1)S(1)}, bf16[4,32,1920]{2,1,0:T(8,128)(2,1)S(1)}, u32[]{:S(2)}, u32[]{:S(2)}) collective-permute-start(bf16[4,32,1920]{2,1,0:T(8,128)(2,1)S(1)} %get-tuple-element.55.refs_0_), channel_id=1, source_target_pairs={{0,24},{1,7},{2,26},{3,1},{4,28},{5,3},{6,30},{7,5},{8,0},{9,15},{... | collective-permute-start | bytes 1474568 | tf_op jit(solution)/shard_map/ppermute | solution.py:459
  49.1 19.5 %collective-permute-start.4 = (bf16[4,32,1920]{2,1,0:T(8,128)(2,1)S(1)}, bf16[4,32,1920]{2,1,0:T(8,128)(2,1)S(1)}, u32[]{:S(2)}, u32[]{:S(2)}) collective-permute-start(bf16[4,32,1920]{2,1,0:T(8,128)(2,1)S(1)} %collective-permute-done.3.refs_0_), channel_id=1, source_target_pairs={{0,8},{1,3},{2,10},{3,5},{4,12},{5,7},{6,14},{7,1},{8,16},{9,11},{... | collective-permute-start | bytes 1474568 | tf_op jit(solution)/shard_map/ppermute | solution.py:459
  49.1 3.5 %copy-start.4 = (bf16[512,1792]{1,0:T(8,128)(2,1)}, bf16[512,1792]{1,0:T(8,128)(2,1)S(1)}, u32[]{:S(2)}) copy-start(bf16[512,1792]{1,0:T(8,128)(2,1)S(1)} %collective-permute-done.7.refs_3_.refs_2_) | copy-start | bytes 5505028
  49.1 15.2 %collective-permute-start.11 = (bf16[4,32,1792]{2,1,0:T(8,128)(2,1)S(1)}, bf16[4,32,1792]{2,1,0:T(8,128)(2,1)S(1)}, u32[]{:S(2)}, u32[]{:S(2)}) collective-permute-start(bf16[4,32,1792]{2,1,0:T(8,128)(2,1)S(1)} %get-tuple-element.56.refs_1_), channel_id=1, source_target_pairs={{0,8},{1,3},{2,10},{3,5},{4,12},{5,7},{6,14},{7,1},{8,16},{9,11},{... | collective-permute-start | bytes 1376264 | tf_op jit(solution)/shard_map/ppermute | solution.py:459
  49.7 18.9 %collective-permute-start.6 = (bf16[4,32,1792]{2,1,0:T(8,128)(2,1)S(1)}, bf16[4,32,1792]{2,1,0:T(8,128)(2,1)S(1)}, u32[]{:S(2)}, u32[]{:S(2)}) collective-permute-start(bf16[4,32,1792]{2,1,0:T(8,128)(2,1)S(1)} %collective-permute-done.5.refs_3_), channel_id=1, source_target_pairs={{0,24},{1,7},{2,26},{3,1},{4,28},{5,3},{6,30},{7,5},{8,0},{9,15},{... | collective-permute-start | bytes 1376264 | tf_op jit(solution)/shard_map/ppermute | solution.py:459
  71.2 9.3 %collective-permute-start.12 = (bf16[128,768]{1,0:T(8,128)(2,1)}, bf16[128,768]{1,0:T(8,128)(2,1)S(1)}, u32[]{:S(2)}, u32[]{:S(2)}) collective-permute-start(bf16[128,768]{1,0:T(8,128)(2,1)} %get-tuple-element.84), channel_id=1, source_target_pairs={{0,32},{32,64},{64,96},{96,0},{1,33},{33,65},{65,97},{97,1},{2,34}... | collective-permute-start | bytes 589832 | tf_op jit(solution)/shard_map/ppermute | solution.py:463
  71.8 8.6 %collective-permute-start.13 = (bf16[128,768]{1,0:T(8,128)(2,1)}, bf16[128,768]{1,0:T(8,128)(2,1)S(1)}, u32[]{:S(2)}, u32[]{:S(2)}) collective-permute-start(bf16[128,768]{1,0:T(8,128)(2,1)} %get-tuple-element.85), channel_id=1, source_target_pairs={{0,64},{32,96},{64,0},{96,32},{1,65},{33,97},{65,1},{97,33},{2,66}... | collective-permute-start | bytes 589832 | tf_op jit(solution)/shard_map/ppermute | solution.py:463
  73.9 7.5 %collective-permute-start.14 = (bf16[128,768]{1,0:T(8,128)(2,1)}, bf16[128,768]{1,0:T(8,128)(2,1)S(1)}, u32[]{:S(2)}, u32[]{:S(2)}) collective-permute-start(bf16[128,768]{1,0:T(8,128)(2,1)} %get-tuple-element.86), channel_id=1, source_target_pairs={{0,96},{32,0},{64,32},{96,64},{1,97},{33,1},{65,33},{97,65},{2,98}... | collective-permute-start | bytes 589832 | tf_op jit(solution)/shard_map/ppermute | solution.py:463
  82.5 6.8 %collective-permute-start.18 = (bf16[128,256]{1,0:T(8,128)(2,1)S(1)}, bf16[128,256]{1,0:T(8,128)(2,1)S(1)}, u32[]{:S(2)}, u32[]{:S(2)}) collective-permute-start(bf16[128,256]{1,0:T(8,128)(2,1)S(1)} %get-tuple-element.96.refs_4_), channel_id=1, source_target_pairs={{0,32},{32,64},{64,96},{96,0},{1,33},{33,65},{65,97},{97,1},{2,34}... | collective-permute-start | bytes 196616 | tf_op jit(solution)/shard_map/ppermute | solution.py:463
  82.8 12.3 %collective-permute-start.15 = (bf16[128,512]{1,0:T(8,128)(2,1)S(1)}, bf16[128,512]{1,0:T(8,128)(2,1)S(1)}, u32[]{:S(2)}, u32[]{:S(2)}) collective-permute-start(bf16[128,512]{1,0:T(8,128)(2,1)S(1)} %get-tuple-element.88.refs_0_), channel_id=1, source_target_pairs={{0,32},{32,64},{64,96},{96,0},{1,33},{33,65},{65,97},{97,1},{2,34}... | collective-permute-start | bytes 393224 | tf_op jit(solution)/shard_map/ppermute | solution.py:463
  83.4 11.7 %collective-permute-start.16 = (bf16[128,512]{1,0:T(8,128)(2,1)S(1)}, bf16[128,512]{1,0:T(8,128)(2,1)S(1)}, u32[]{:S(2)}, u32[]{:S(2)}) collective-permute-start(bf16[128,512]{1,0:T(8,128)(2,1)S(1)} %get-tuple-element.88.refs_0_), channel_id=1, source_target_pairs={{0,64},{32,96},{64,0},{96,32},{1,65},{33,97},{65,1},{97,33},{2,66}... | collective-permute-start | bytes 393224 | tf_op jit(solution)/shard_map/ppermute | solution.py:463
  87.3 7.8 %collective-permute-start.17 = (bf16[128,512]{1,0:T(8,128)(2,1)S(1)}, bf16[128,512]{1,0:T(8,128)(2,1)S(1)}, u32[]{:S(2)}, u32[]{:S(2)}) collective-permute-start(bf16[128,512]{1,0:T(8,128)(2,1)S(1)} %get-tuple-element.88.refs_0_), channel_id=1, source_target_pairs={{0,96},{32,0},{64,32},{96,64},{1,97},{33,1},{65,33},{97,65},{2,98}... | collective-permute-start | bytes 393224 | tf_op jit(solution)/shard_map/ppermute | solution.py:463
  89.3 5.8 %collective-permute-start.19 = (bf16[128,256]{1,0:T(8,128)(2,1)S(1)}, bf16[128,256]{1,0:T(8,128)(2,1)S(1)}, u32[]{:S(2)}, u32[]{:S(2)}) collective-permute-start(bf16[128,256]{1,0:T(8,128)(2,1)S(1)} %get-tuple-element.96.refs_4_), channel_id=1, source_target_pairs={{0,64},{32,96},{64,0},{96,32},{1,65},{33,97},{65,1},{97,33},{2,66}... | collective-permute-start | bytes 196616 | tf_op jit(solution)/shard_map/ppermute | solution.py:463
  89.3 5.8 %collective-permute-start.20 = (bf16[128,256]{1,0:T(8,128)(2,1)S(1)}, bf16[128,256]{1,0:T(8,128)(2,1)S(1)}, u32[]{:S(2)}, u32[]{:S(2)}) collective-permute-start(bf16[128,256]{1,0:T(8,128)(2,1)S(1)} %get-tuple-element.96.refs_4_), channel_id=1, source_target_pairs={{0,96},{32,0},{64,32},{96,64},{1,97},{33,1},{65,33},{97,65},{2,98}... | collective-permute-start | bytes 196616 | tf_op jit(solution)/shard_map/ppermute | solution.py:463
  95.1 0.9 copy-start
  97.3 4.0 %copy-start.2 = (bf16[4,128,1792]{2,1,0:T(8,128)(2,1)S(1)}, bf16[4,128,1792]{2,1,0:T(8,128)(2,1)}, u32[]{:S(2)}) copy-start(bf16[4,128,1792]{2,1,0:T(8,128)(2,1)} %get-tuple-element.98) | copy-start | bytes 5505028
  101.4 23.2 %collective-permute-start.23 = (bf16[512,1792]{1,0:T(8,128)(2,1)}, bf16[512,1792]{1,0:T(8,128)(2,1)}, u32[]{:S(2)}, u32[]{:S(2)}) collective-permute-start(bf16[512,1792]{1,0:T(8,128)(2,1)} %convolution_convert_fusion), channel_id=1, source_target_pairs={{0,1},{1,0},{2,3},{3,2},{4,5},{5,4},{6,7},{7,6},{8,9},{9,8},{10,11... | collective-permute-start | bytes 5505032 | tf_op jit(solution)/shard_map/ppermute | solution.py:467
  103.8 25.4 %collective-permute-start.22 = (bf16[512,1792]{1,0:T(8,128)(2,1)}, bf16[512,1792]{1,0:T(8,128)(2,1)}, u32[]{:S(2)}, u32[]{:S(2)}) collective-permute-start(bf16[512,1792]{1,0:T(8,128)(2,1)} %convolution_convert_fusion.1), channel_id=1, source_target_pairs={{0,1},{1,0},{2,3},{3,2},{4,5},{5,4},{6,7},{7,6},{8,9},{9,8},{10,11... | collective-permute-start | bytes 5505032 | tf_op jit(solution)/shard_map/ppermute | solution.py:467
  106.7 3.2 %copy-start.1 = (bf16[4,128,128]{2,1,0:T(8,128)(2,1)S(1)}, bf16[4,128,128]{2,1,0:T(8,128)(2,1)}, u32[]{:S(2)}) copy-start(bf16[4,128,128]{2,1,0:T(8,128)(2,1)} %get-tuple-element.87.refs_4_.refs_8_) | copy-start | bytes 393220
  106.7 26.4 %collective-permute-start.21 = (bf16[512,1792]{1,0:T(8,128)(2,1)}, bf16[512,1792]{1,0:T(8,128)(2,1)}, u32[]{:S(2)}, u32[]{:S(2)}) collective-permute-start(bf16[512,1792]{1,0:T(8,128)(2,1)} %convolution_convert_fusion.2), channel_id=1, source_target_pairs={{0,1},{1,0},{2,3},{3,2},{4,5},{5,4},{6,7},{7,6},{8,9},{9,8},{10,11... | collective-permute-start | bytes 5505032 | tf_op jit(solution)/shard_map/ppermute | solution.py:467
  115.4 37.9 %all-to-all-start.1 = ((bf16[64,8,1920]{2,1,0:T(8,128)(2,1)}), bf16[64,8,1920]{2,1,0:T(8,128)(2,1)S(1)}, u32[]{:S(2)}, u32[]{:S(2)}) async-start(bf16[64,8,1920]{2,1,0:T(8,128)(2,1)} %bitcast.28), calls=%async_computation.1 | async-start | bytes 3932160 | tf_op jit(solution)/shard_map/all_to_all | solution.py:504
  124.6 4.6 %copy-start.3 = (bf16[4,128,1792]{2,1,0:T(8,128)(2,1)S(1)}, bf16[4,128,1792]{2,1,0:T(8,128)(2,1)}, u32[]{:S(2)}) copy-start(bf16[4,128,1792]{2,1,0:T(8,128)(2,1)} %get-tuple-element.98) | copy-start | bytes 5505028
